TPU v7x, 256 devices: a whole 4x4x8 slice. The times are simulated.
256 devices in a mesh: ep: 64 (over z, y, core), dp: 4 (over x).
Axes of the slice: x: 4, y: 4, z: 8, core: 2. Of those that a mesh axis runs over, the one named last changes fastest.
Arguments:
- master_weight: float32 [128, 3584, 128], P('ep', 'dp'), may hold values from -3 to 3
- first_moment: float32 [128, 3584, 128], P('ep', 'dp'), may hold values from -2 to 2
- second_moment: float32 [128, 3584, 128], P('ep', 'dp'), may hold values from 0.05 to 2
- grad_owned: bfloat16 [4, 128, 3584, 128], P('dp', 'ep'), may hold values from -2.5 to 2.5
- grad_replica: bfloat16 [4, 128, 3584, 128], P('dp', 'ep'), may hold values from -2.5 to 2.5
- old_experts: int32 [128], replicated, may hold values from 0 to 127, each once
- new_experts: int32 [128], replicated, may hold values from 0 to 127, each once
- rep_expert: int32 [128], replicated, may hold values from 0 to 127
- rep_count: int32 [64], replicated, may hold values from 0 to 2, as said below
Outputs:
- new_weight: float32 [128, 3584, 128], P('ep', 'dp')
- new_first: float32 [128, 3584, 128], P('ep', 'dp')
- new_second: float32 [128, 3584, 128], P('ep', 'dp')
Inputs may be any that keep to these rules, and one draw needn't show every extreme that they name: `old_experts`: each expert appears once. `new_experts`: each expert appears once. The first rep_count[i] of the 2 replica slots of ep index i are live; some index has all live and some none.
All inputs are finite; a program needn't handle non-finite values.
Results may differ from a plain program's by a relative error of at most 0.0003.
Values may be sent and summed in bfloat16 or wider, within the bound.
A program may use at most 64 MiB of HBM per device.

v0:
```python
import jax
import jax.numpy as jnp
from jax import lax
from jax.sharding import PartitionSpec as P

beta_first = 0.9
beta_second = 0.95
learn_rate = 0.01
decay_rate = 0.1
adam_eps = 1e-08
corr_first = 1.0 - 0.9**10
corr_second = 1.0 - 0.95**10


def adam_update(weight_now, first_now, second_now, gradient):
    moved_first = beta_first * first_now + (1.0 - beta_first) * gradient
    moved_second = beta_second * second_now + (1.0 - beta_second) * gradient * gradient
    step_size = moved_first / corr_first / (jnp.sqrt(moved_second / corr_second) + adam_eps)
    moved_weight = weight_now - learn_rate * (step_size + decay_rate * weight_now)
    return (moved_weight, moved_first, moved_second)


def per_device(
    master_weight,
    first_moment,
    second_moment,
    grad_owned,
    grad_replica,
    old_experts,
    new_experts,
    rep_expert,
    rep_count,
):
    ep_count = lax.axis_size("ep")
    exp_dev, shard_rows, columns = master_weight.shape
    rep_dev = grad_replica.shape[1]
    piece_rows = shard_rows // ep_count
    experts = exp_dev * ep_count
    replica_slots = rep_dev * ep_count
    owned_part, replica_part = (
        lax.psum_scatter(grad_owned[0].astype(jnp.float32), "dp", scatter_dimension=1, tiled=True),
        lax.psum_scatter(
            grad_replica[0].astype(jnp.float32), "dp", scatter_dimension=1, tiled=True
        ),
    )
    owned_t, replica_t = (
        lax.all_to_all(
            owned_part.reshape(exp_dev, ep_count, piece_rows, columns),
            "ep",
            split_axis=1,
            concat_axis=0,
            tiled=True,
        ),
        lax.all_to_all(
            replica_part.reshape(rep_dev, ep_count, piece_rows, columns),
            "ep",
            split_axis=1,
            concat_axis=0,
            tiled=True,
        ),
    )
    owned_t = owned_t.reshape(experts, piece_rows, columns)
    replica_t = replica_t.reshape(replica_slots, piece_rows * columns)
    live_mask = (
        lax.iota(jnp.int32, replica_slots) % rep_dev
        < jnp.repeat(rep_count, rep_dev, total_repeat_length=replica_slots)
    ).astype(jnp.float32)
    replica_match = jnp.where(
        rep_expert[None, :] == old_experts[:, None], live_mask[None, :], jnp.float32(0.0)
    )
    summed = owned_t + jnp.dot(
        replica_match,
        replica_t,
        precision=lax.Precision.HIGHEST,
        preferred_element_type=jnp.float32,
    ).reshape(experts, piece_rows, columns)
    source_index = jnp.sum(
        jnp.where(
            new_experts[:, None] == old_experts[None, :], lax.iota(jnp.int32, experts)[None, :], 0
        ),
        axis=1,
    )

    def to_pieces(array):
        return array.reshape(exp_dev, ep_count, piece_rows, columns)

    def to_slots(array):
        return jnp.take(array.reshape(experts, piece_rows, columns), source_index, axis=0).reshape(
            ep_count, exp_dev, 1, piece_rows, columns
        )

    def to_home(array):
        return array.reshape(exp_dev, shard_rows, columns)

    grads_home = lax.all_to_all(
        summed.reshape(ep_count, exp_dev, 1, piece_rows, columns),
        "ep",
        split_axis=0,
        concat_axis=2,
        tiled=True,
    )
    moved = adam_update(master_weight, first_moment, second_moment, to_home(grads_home))
    spread_w, spread_f, spread_s = (
        lax.all_to_all(to_pieces(moved[0]), "ep", split_axis=1, concat_axis=0, tiled=True),
        lax.all_to_all(to_pieces(moved[1]), "ep", split_axis=1, concat_axis=0, tiled=True),
        lax.all_to_all(to_pieces(moved[2]), "ep", split_axis=1, concat_axis=0, tiled=True),
    )
    back_w, back_f, back_s = (
        lax.all_to_all(to_slots(spread_w), "ep", split_axis=0, concat_axis=2, tiled=True),
        lax.all_to_all(to_slots(spread_f), "ep", split_axis=0, concat_axis=2, tiled=True),
        lax.all_to_all(to_slots(spread_s), "ep", split_axis=0, concat_axis=2, tiled=True),
    )
    return (to_home(back_w), to_home(back_f), to_home(back_s))


def solution(mesh):
    in_specs = (
        P("ep", "dp", None),
        P("ep", "dp", None),
        P("ep", "dp", None),
        P("dp", "ep", None, None),
        P("dp", "ep", None, None),
        P(),
        P(),
        P(),
        P(),
    )
    out_specs = (P("ep", "dp", None), P("ep", "dp", None), P("ep", "dp", None))
    return jax.shard_map(
        per_device, mesh=mesh, in_specs=in_specs, out_specs=out_specs, check_vma=False
    )
```

profile of v0, /device:TPU:1, one launch (start us, length us, event | category | flops | bytes accessed | tf_op | source)
XLA Modules:
  0.0 388.5 jit_solution(4223031944403974375)
XLA Ops:
  7.2 3.7 bitcast_convert_fusion.1
  11.0 2.1 bitcast_convert_fusion
  13.1 46.8 %reduce-scatter.3.cloned.1.call-done = f32[2,896,128]{2,1,0:T(8,128)} async-done(((f32[2,3584,128]{2,1,0:T(8,128)}), f32[2,896,128]{2,1,0:T(8,128)}) %reduce-scatter.3.cloned.1.call-update) | async-done | bytes 917520 | tf_op jit(solution)/shard_map/reduce_scatter | solution.py:41
  59.9 2.8 copy.109
  62.7 10.8 %all-to-all-start = ((f32[2,64,14,128]{3,0,2,1:T(2,128)}), f32[2,64,14,128]{3,0,2,1:T(2,128)S(1)}, u32[]{:S(2)}, u32[]{:S(2)}) async-start(f32[2,64,14,128]{3,0,2,1:T(2,128)} %bitcast.1), calls=%async_computation.1 | async-start | bytes 1835008 | tf_op jit(solution)/shard_map/all_to_all | solution.py:47
  73.5 33.9 %reduce-scatter.5.cloned.1.call-done = f32[2,896,128]{2,1,0:T(8,128)} async-done(((f32[2,3584,128]{2,1,0:T(8,128)}), f32[2,896,128]{2,1,0:T(8,128)}) %reduce-scatter.5.cloned.1.call-update) | async-done | bytes 917520 | tf_op jit(solution)/shard_map/reduce_scatter | solution.py:42
  107.3 2.8 copy.111
  110.1 10.8 %all-to-all-start.1 = ((f32[2,64,14,128]{3,0,2,1:T(2,128)}), f32[2,64,14,128]{3,0,2,1:T(2,128)S(1)}, u32[]{:S(2)}, u32[]{:S(2)}) async-start(f32[2,64,14,128]{3,0,2,1:T(2,128)} %bitcast.7), calls=%async_computation.3 | async-start | bytes 1835008 | tf_op jit(solution)/shard_map/all_to_all | solution.py:54
  120.9 1.2 gather_fusion
  122.2 0.5 copy.110
  122.7 23.8 %all-to-all-done.1 = f32[2,64,14,128]{3,0,2,1:T(2,128)S(1)} async-done(((f32[2,64,14,128]{3,0,2,1:T(2,128)}), f32[2,64,14,128]{3,0,2,1:T(2,128)S(1)}, u32[]{:S(2)}, u32[]{:S(2)}) %all-to-all-start.1) | async-done | bytes 917536 | tf_op jit(solution)/shard_map/all_to_all | solution.py:54
  146.6 0.3 copy.148
  146.9 0.3 copy.113
  147.3 0.9 convolution_add_fusion
  148.2 0.3 copy.114
  148.6 31.5 %all_to_all.135 = f32[64,2,1,14,128]{4,1,3,2,0:T(2,128)S(1)} all-to-all(f32[64,2,1,14,128]{4,1,3,2,0:T(2,128)S(1)} %copy.114), channel_id=1, replica_groups=mesh['ep'=64,'dp'=4] {'ep'}, dimensions={0} | all-to-all | bytes 1835008 | tf_op jit(solution)/shard_map/all_to_all | solution.py:95
  180.1 0.7 multiply_subtract_fusion
  180.8 1.6 copy.128
  182.4 6.1 %all-to-all-start.7 = ((f32[2,64,14,128]{3,0,2,1:T(2,128)}), f32[2,64,14,128]{3,0,2,1:T(2,128)S(1)}, u32[]{:S(2)}, u32[]{:S(2)}) async-start(f32[2,64,14,128]{3,0,2,1:T(2,128)} %bitcast.80), calls=%async_computation.9 | async-start | bytes 1835008 | tf_op jit(solution)/shard_map/all_to_all | solution.py:106
  188.5 1.6 copy.123
  190.1 23.9 %all-to-all-done.7 = f32[2,64,14,128]{3,0,2,1:T(2,128)S(1)} async-done(((f32[2,64,14,128]{3,0,2,1:T(2,128)}), f32[2,64,14,128]{3,0,2,1:T(2,128)S(1)}, u32[]{:S(2)}, u32[]{:S(2)}) %all-to-all-start.7) | async-done | bytes 917536 | tf_op jit(solution)/shard_map/all_to_all | solution.py:106
  214.1 6.1 %all-to-all-start.5 = ((f32[2,64,14,128]{3,0,2,1:T(2,128)}), f32[2,64,14,128]{3,0,2,1:T(2,128)S(1)}, u32[]{:S(2)}, u32[]{:S(2)}) async-start(f32[2,64,14,128]{3,0,2,1:T(2,128)} %bitcast.78), calls=%async_computation.7 | async-start | bytes 1835008 | tf_op jit(solution)/shard_map/all_to_all | solution.py:105
  220.2 1.6 copy.118
  221.8 24.0 %all-to-all-done.5 = f32[2,64,14,128]{3,0,2,1:T(2,128)S(1)} async-done(((f32[2,64,14,128]{3,0,2,1:T(2,128)}), f32[2,64,14,128]{3,0,2,1:T(2,128)S(1)}, u32[]{:S(2)}, u32[]{:S(2)}) %all-to-all-start.5) | async-done | bytes 917536 | tf_op jit(solution)/shard_map/all_to_all | solution.py:105
  245.8 6.3 %all-to-all-start.3 = ((f32[2,64,14,128]{3,0,2,1:T(2,128)}), f32[2,64,14,128]{3,0,2,1:T(2,128)}, u32[]{:S(2)}, u32[]{:S(2)}) async-start(f32[2,64,14,128]{3,0,2,1:T(2,128)} %bitcast.18), calls=%async_computation.5 | async-start | bytes 1835008 | tf_op jit(solution)/shard_map/all_to_all | solution.py:104
  252.2 0.5 copy.129
  252.7 0.5 copy.130
  253.3 0.5 copy.124
  253.7 0.5 copy.125
  254.3 0.8 gather_fusion.3
  255.0 0.8 gather_fusion.2
  255.8 21.7 %all-to-all-done.3 = f32[2,64,14,128]{3,0,2,1:T(2,128)} async-done(((f32[2,64,14,128]{3,0,2,1:T(2,128)}), f32[2,64,14,128]{3,0,2,1:T(2,128)}, u32[]{:S(2)}, u32[]{:S(2)}) %all-to-all-start.3) | async-done | bytes 917536 | tf_op jit(solution)/shard_map/all_to_all | solution.py:104
  277.5 1.6 copy.119
  279.2 1.6 copy.120
  280.7 1.9 gather_fusion.1
  282.6 1.6 broadcast_select_fusion
  284.2 1.4 copy.122
  285.6 6.1 %all-to-all-start.4 = ((f32[64,2,1,14,128]{4,1,3,2,0:T(2,128)}), f32[64,2,1,14,128]{4,1,3,2,0:T(2,128)S(1)}, u32[]{:S(2)}, u32[]{:S(2)}) async-start(f32[64,2,1,14,128]{4,1,3,2,0:T(2,128)} %copy.122), calls=%async_computation.6 | async-start | bytes 1835008 | tf_op jit(solution)/shard_map/all_to_all | solution.py:109
  291.7 1.4 copy.127
  293.1 24.2 %all-to-all-done.4 = f32[64,2,1,14,128]{4,1,3,2,0:T(2,128)S(1)} async-done(((f32[64,2,1,14,128]{4,1,3,2,0:T(2,128)}), f32[64,2,1,14,128]{4,1,3,2,0:T(2,128)S(1)}, u32[]{:S(2)}, u32[]{:S(2)}) %all-to-all-start.4) | async-done | bytes 917536 | tf_op jit(solution)/shard_map/all_to_all | solution.py:109
  317.3 6.1 %all-to-all-start.6 = ((f32[64,2,1,14,128]{4,1,3,2,0:T(2,128)}), f32[64,2,1,14,128]{4,1,3,2,0:T(2,128)S(1)}, u32[]{:S(2)}, u32[]{:S(2)}) async-start(f32[64,2,1,14,128]{4,1,3,2,0:T(2,128)} %copy.127), calls=%async_computation.8 | async-start | bytes 1835008 | tf_op jit(solution)/shard_map/all_to_all | solution.py:110
  323.4 1.4 copy.132
  324.8 24.2 %all-to-all-done.6 = f32[64,2,1,14,128]{4,1,3,2,0:T(2,128)S(1)} async-done(((f32[64,2,1,14,128]{4,1,3,2,0:T(2,128)}), f32[64,2,1,14,128]{4,1,3,2,0:T(2,128)S(1)}, u32[]{:S(2)}, u32[]{:S(2)}) %all-to-all-start.6) | async-done | bytes 917536 | tf_op jit(solution)/shard_map/all_to_all | solution.py:110
  349.0 6.1 %all-to-all-start.8 = ((f32[64,2,1,14,128]{4,1,3,2,0:T(2,128)}), f32[64,2,1,14,128]{4,1,3,2,0:T(2,128)S(1)}, u32[]{:S(2)}, u32[]{:S(2)}) async-start(f32[64,2,1,14,128]{4,1,3,2,0:T(2,128)} %copy.132), calls=%async_computation.10 | async-start | bytes 1835008 | tf_op jit(solution)/shard_map/all_to_all | solution.py:111
  355.1 1.0 copy.133
  356.1 1.0 copy.134
  357.1 23.6 %all-to-all-done.8 = f32[64,2,1,14,128]{4,1,3,2,0:T(2,128)S(1)} async-done(((f32[64,2,1,14,128]{4,1,3,2,0:T(2,128)}), f32[64,2,1,14,128]{4,1,3,2,0:T(2,128)S(1)}, u32[]{:S(2)}, u32[]{:S(2)}) %all-to-all-start.8) | async-done | bytes 917536 | tf_op jit(solution)/shard_map/all_to_all | solution.py:111
  380.7 1.0 copy.135
  (34 shorter events, 0.5 us)
Async XLA Ops:
  7.2 113.8 %copy-start = (s32[64]{0:T(128)S(1)}, s32[64]{0:T(128)}, u32[]{:S(2)}) copy-start(s32[64]{0:T(128)} %param.21) | copy-start | bytes 772
  7.2 3.8 copy-start.3
  7.2 52.7 %reduce-scatter.3.cloned.1.call-start = ((), (), s32[]{:S(2)}) async-start(), calls=%async_computation.11 | async-start | bytes 4587520 | tf_op jit(solution)/shard_map/reduce_scatter | solution.py:41
  10.9 96.4 %reduce-scatter.5.cloned.1.call-start = ((), (), s32[]{:S(2)}) async-start(), calls=%async_computation.12 | async-start | bytes 4587520 | tf_op jit(solution)/shard_map/reduce_scatter | solution.py:42
  13.1 107.8 %copy-start.7 = (s32[128]{0:T(128)S(1)}, s32[128]{0:T(128)}, u32[]{:S(2)}) copy-start(s32[128]{0:T(128)} %constant.129) | copy-start | bytes 1540
  62.7 47.4 %all-to-all-start = ((f32[2,64,14,128]{3,0,2,1:T(2,128)}), f32[2,64,14,128]{3,0,2,1:T(2,128)S(1)}, u32[]{:S(2)}, u32[]{:S(2)}) async-start(f32[2,64,14,128]{3,0,2,1:T(2,128)} %bitcast.1), calls=%async_computation.1 | async-start | bytes 1835008 | tf_op jit(solution)/shard_map/all_to_all | solution.py:47
  110.1 36.4 %all-to-all-start.1 = ((f32[2,64,14,128]{3,0,2,1:T(2,128)}), f32[2,64,14,128]{3,0,2,1:T(2,128)S(1)}, u32[]{:S(2)}, u32[]{:S(2)}) async-start(f32[2,64,14,128]{3,0,2,1:T(2,128)} %bitcast.7), calls=%async_computation.3 | async-start | bytes 1835008 | tf_op jit(solution)/shard_map/all_to_all | solution.py:54
  122.2 25.1 %copy-start.8 = (s32[128]{0:T(128)S(1)}, s32[128]{0:T(128)}, u32[]{:S(2)}) copy-start(s32[128]{0:T(128)} %param.20) | copy-start | bytes 1540
  122.2 25.1 %copy-start.9 = (s32[128]{0:T(128)S(1)}, s32[128]{0:T(128)}, u32[]{:S(2)}) copy-start(s32[128]{0:T(128)} %param.18) | copy-start | bytes 1540
  147.2 32.8 %copy-start.4 = (f32[2,896,128]{2,1,0:T(8,128)S(1)}, f32[2,896,128]{2,1,0:T(8,128)}, u32[]{:S(2)}) copy-start(f32[2,896,128]{2,1,0:T(8,128)} %param.13) | copy-start | bytes 2752516
  147.3 32.8 %copy-start.5 = (f32[2,896,128]{2,1,0:T(8,128)S(1)}, f32[2,896,128]{2,1,0:T(8,128)}, u32[]{:S(2)}) copy-start(f32[2,896,128]{2,1,0:T(8,128)} %param.14) | copy-start | bytes 2752516
  147.3 32.8 %copy-start.6 = (f32[2,896,128]{2,1,0:T(8,128)S(1)}, f32[2,896,128]{2,1,0:T(8,128)}, u32[]{:S(2)}) copy-start(f32[2,896,128]{2,1,0:T(8,128)} %param.15) | copy-start | bytes 2752516
  182.4 31.7 %all-to-all-start.7 = ((f32[2,64,14,128]{3,0,2,1:T(2,128)}), f32[2,64,14,128]{3,0,2,1:T(2,128)S(1)}, u32[]{:S(2)}, u32[]{:S(2)}) async-start(f32[2,64,14,128]{3,0,2,1:T(2,128)} %bitcast.80), calls=%async_computation.9 | async-start | bytes 1835008 | tf_op jit(solution)/shard_map/all_to_all | solution.py:106
  188.5 63.5 %copy-start.10 = (s32[128]{0:T(128)S(1)}, s32[128]{0:T(128)}, u32[]{:S(2)}) copy-start(s32[128]{0:T(128)} %param.19) | copy-start | bytes 1540
  214.1 31.7 %all-to-all-start.5 = ((f32[2,64,14,128]{3,0,2,1:T(2,128)}), f32[2,64,14,128]{3,0,2,1:T(2,128)S(1)}, u32[]{:S(2)}, u32[]{:S(2)}) async-start(f32[2,64,14,128]{3,0,2,1:T(2,128)} %bitcast.78), calls=%async_computation.7 | async-start | bytes 1835008 | tf_op jit(solution)/shard_map/all_to_all | solution.py:105
  245.8 31.8 %all-to-all-start.3 = ((f32[2,64,14,128]{3,0,2,1:T(2,128)}), f32[2,64,14,128]{3,0,2,1:T(2,128)}, u32[]{:S(2)}, u32[]{:S(2)}) async-start(f32[2,64,14,128]{3,0,2,1:T(2,128)} %bitcast.18), calls=%async_computation.5 | async-start | bytes 1835008 | tf_op jit(solution)/shard_map/all_to_all | solution.py:104
  284.2 7.5 %copy-start.2 = (f32[128,14,128]{2,1,0:T(8,128)S(1)}, f32[128,14,128]{2,1,0:T(8,128)}, u32[]{:S(2)}) copy-start(f32[128,14,128]{2,1,0:T(8,128)} %get-tuple-element.35) | copy-start | bytes 2752516
  284.2 39.2 %copy-start.1 = (f32[128,14,128]{2,1,0:T(8,128)S(1)}, f32[128,14,128]{2,1,0:T(8,128)}, u32[]{:S(2)}) copy-start(f32[128,14,128]{2,1,0:T(8,128)} %get-tuple-element.34) | copy-start | bytes 2752516
  285.6 31.7 %all-to-all-start.4 = ((f32[64,2,1,14,128]{4,1,3,2,0:T(2,128)}), f32[64,2,1,14,128]{4,1,3,2,0:T(2,128)S(1)}, u32[]{:S(2)}, u32[]{:S(2)}) async-start(f32[64,2,1,14,128]{4,1,3,2,0:T(2,128)} %copy.122), calls=%async_computation.6 | async-start | bytes 1835008 | tf_op jit(solution)/shard_map/all_to_all | solution.py:109
  317.3 31.7 %all-to-all-start.6 = ((f32[64,2,1,14,128]{4,1,3,2,0:T(2,128)}), f32[64,2,1,14,128]{4,1,3,2,0:T(2,128)S(1)}, u32[]{:S(2)}, u32[]{:S(2)}) async-start(f32[64,2,1,14,128]{4,1,3,2,0:T(2,128)} %copy.127), calls=%async_computation.8 | async-start | bytes 1835008 | tf_op jit(solution)/shard_map/all_to_all | solution.py:110
  349.0 31.7 %all-to-all-start.8 = ((f32[64,2,1,14,128]{4,1,3,2,0:T(2,128)}), f32[64,2,1,14,128]{4,1,3,2,0:T(2,128)S(1)}, u32[]{:S(2)}, u32[]{:S(2)}) async-start(f32[64,2,1,14,128]{4,1,3,2,0:T(2,128)} %copy.132), calls=%async_computation.10 | async-start | bytes 1835008 | tf_op jit(solution)/shard_map/all_to_all | solution.py:111
Sparse Core Ops, SparseCore 0:
  11.0 48.7 reduce-scatter.2
  62.4 44.8 reduce-scatter.4
where the time goes:
time: 390 us; the launch traced here: 389 us
  waiting for transfers between devices  246 us (63%)
  starting transfers between devices  58.3 us (15%)
  blocking collectives  31.5 us (8%)
  local copies, waits for them, and re-layouts  29 us (7%)
  between operations  14.4 us (4%)
  other arithmetic  8.24 us (2%)
    reduce_scatter x1, waiting for transfers between devices, per_device(): lax.psum_scatter(grad_owned[0].astype(jnp.float32), 'dp', scatter_dimensi...  46.8 us
    reduce_scatter x1, waiting for transfers between devices, per_device(): lax.psum_scatter(grad_replica[0].astype(jnp.float32), 'dp', scatter_dimen...  33.9 us
    all_to_all x1, blocking collectives, per_device(): lax.all_to_all(summed.reshape(ep_count, exp_dev, 1, piece_rows, columns),...  31.5 us
    all_to_all x1, waiting for transfers between devices, per_device(): lax.all_to_all(to_slots(spread_w), 'ep', split_axis=0, concat_axis=2, til...  24.2 us
    all_to_all x1, waiting for transfers between devices, per_device(): lax.all_to_all(to_slots(spread_f), 'ep', split_axis=0, concat_axis=2, til...  24.2 us
    all_to_all x1, waiting for transfers between devices, per_device(): lax.all_to_all(to_pieces(moved[1]), 'ep', split_axis=1, concat_axis=0, ti...  24 us
    all_to_all x1, waiting for transfers between devices, per_device(): lax.all_to_all(to_pieces(moved[2]), 'ep', split_axis=1, concat_axis=0, ti...  23.9 us
    all_to_all x1, waiting for transfers between devices, per_device(): lax.all_to_all(replica_part.reshape(rep_dev, ep_count, piece_rows, column...  23.8 us
  transfers between devices with their start and end apart: 10, of which 9 were waited for; matrix products, arithmetic and copies ran while one was open for 5% of the time, Pallas kernels for 0%

commit v1 on v0

v1 whole, which is shorter than its diff:
```python
import jax
import jax.numpy as jnp
from jax import lax
from jax.sharding import PartitionSpec as P

beta_first = 0.9
beta_second = 0.95
learn_rate = 0.01
decay_rate = 0.1
adam_eps = 1e-08
corr_first = 1.0 - 0.9**10
corr_second = 1.0 - 0.95**10


def adam_update(weight_now, first_now, second_now, gradient):
    moved_first = beta_first * first_now + (1.0 - beta_first) * gradient
    moved_second = beta_second * second_now + (1.0 - beta_second) * gradient * gradient
    step_size = moved_first / corr_first / (jnp.sqrt(moved_second / corr_second) + adam_eps)
    moved_weight = weight_now - learn_rate * (step_size + decay_rate * weight_now)
    return (moved_weight, moved_first, moved_second)


def per_device(
    master_weight,
    first_moment,
    second_moment,
    grad_owned,
    grad_replica,
    old_experts,
    new_experts,
    rep_expert,
    rep_count,
):
    ep_count = lax.axis_size("ep")
    exp_dev, shard_rows, columns = master_weight.shape
    rep_dev = grad_replica.shape[1]
    piece_rows = shard_rows // ep_count
    experts = exp_dev * ep_count
    replica_slots = rep_dev * ep_count

    state = jnp.stack([master_weight, first_moment, second_moment])
    state_p = lax.all_to_all(
        state.reshape(3, exp_dev, ep_count, piece_rows, columns),
        "ep",
        split_axis=2,
        concat_axis=1,
        tiled=True,
    ).reshape(3, experts, piece_rows, columns)

    owned_part = lax.psum_scatter(
        grad_owned[0].astype(jnp.float32), "dp", scatter_dimension=1, tiled=True
    )
    replica_part = lax.psum_scatter(
        grad_replica[0].astype(jnp.float32), "dp", scatter_dimension=1, tiled=True
    )
    grads = jnp.concatenate([owned_part, replica_part], axis=0)
    grads_p = lax.all_to_all(
        grads.reshape(exp_dev + rep_dev, ep_count, piece_rows, columns),
        "ep",
        split_axis=1,
        concat_axis=0,
        tiled=True,
    ).reshape(ep_count, exp_dev + rep_dev, piece_rows, columns)
    owned_t = grads_p[:, :exp_dev].reshape(experts, piece_rows, columns)
    replica_t = grads_p[:, exp_dev:].reshape(replica_slots, piece_rows * columns)

    live_mask = (
        lax.iota(jnp.int32, replica_slots) % rep_dev
        < jnp.repeat(rep_count, rep_dev, total_repeat_length=replica_slots)
    ).astype(jnp.float32)
    replica_match = jnp.where(
        rep_expert[None, :] == old_experts[:, None], live_mask[None, :], jnp.float32(0.0)
    )
    gradient = owned_t + jnp.dot(
        replica_match,
        replica_t,
        precision=lax.Precision.HIGHEST,
        preferred_element_type=jnp.float32,
    ).reshape(experts, piece_rows, columns)
    source_index = jnp.sum(
        jnp.where(
            new_experts[:, None] == old_experts[None, :], lax.iota(jnp.int32, experts)[None, :], 0
        ),
        axis=1,
    )
    moved = adam_update(state_p[0], state_p[1], state_p[2], gradient)
    moved = jnp.take(jnp.stack(moved), source_index, axis=1)
    back = lax.all_to_all(
        moved.reshape(3, ep_count, exp_dev, 1, piece_rows, columns),
        "ep",
        split_axis=1,
        concat_axis=3,
        tiled=True,
    ).reshape(3, exp_dev, shard_rows, columns)
    return (back[0], back[1], back[2])


def solution(mesh):
    in_specs = (
        P("ep", "dp", None),
        P("ep", "dp", None),
        P("ep", "dp", None),
        P("dp", "ep", None, None),
        P("dp", "ep", None, None),
        P(),
        P(),
        P(),
        P(),
    )
    out_specs = (P("ep", "dp", None), P("ep", "dp", None), P("ep", "dp", None))
    return jax.shard_map(
        per_device, mesh=mesh, in_specs=in_specs, out_specs=out_specs, check_vma=False
    )
```

time: 390 us -> 266 us (0.68)
  waiting for transfers between devices: 246 us -> 110 us
  blocking collectives: 31.5 us -> 71.7 us
  starting transfers between devices: 58.3 us -> 24.3 us
    all_to_all x8 -> x2, waiting for transfers between devices: 165 us -> 37.8 us  [the longest x1 37.8 us: per_device(): lax.all_to_all(grads.reshape(exp_dev + rep_dev, ep_count, piece_rows, col...]
    all_to_all x1, blocking collectives: 31.5 us -> 71.7 us  [per_device(): lax.all_to_all(moved.reshape(3, ep_count, exp_dev, 1, piece_rows, columns...]
    all_to_all x8 -> x2, starting transfers between devices: 58.2 us -> 24.2 us  [the longest x1 13.1 us: per_device(): lax.all_to_all(state.reshape(3, exp_dev, ep_count, piece_rows, columns),...]
    reduce_scatter x1, waiting for transfers between devices: 46.8 us -> 25.1 us  [per_device(): lax.psum_scatter(grad_owned[0].astype(jnp.float32), 'dp', scatter_dimensi...]
    reduce_scatter x1, waiting for transfers between devices: 33.9 us -> 47.4 us  [per_device(): lax.psum_scatter(grad_replica[0].astype(jnp.float32), 'dp', scatter_dimen...]
    reshape x7 -> x0, local copies, waits for them, and re-layouts: 7.15 us -> none  [the longest x3 4.18 us: to_slots(): jnp.take(array.reshape(experts, piece_rows, columns), source_index, axis=0)]
    slice x0 -> x5, local copies, waits for them, and re-layouts: none -> 6.01 us  [the longest x2 2.98 us: per_device(): grads_p[:, exp_dev:].reshape(replica_slots, piece_rows * columns)]
    another operation x0 -> x2, local copies, waits for them, and re-layouts: none -> 5.77 us  [the longest x1 3.23 us: per_device(): moved = jnp.take(jnp.stack(moved), source_index, axis=1)]
  transfers between devices with their start and end apart: 10 -> 4, of which waited for: 9 -> 3; matrix products, arithmetic and copies ran while one was open for 5% -> 7% of each run, Pallas kernels for 0% -> 0%
where the time goes in v1:
time: 266 us
  waiting for transfers between devices  110 us (41%)
  blocking collectives  71.7 us (27%)
  local copies, waits for them, and re-layouts  30.2 us (11%)
  starting transfers between devices  24.3 us (9%)
  between operations  14.3 us (5%)
  other arithmetic  11.4 us (4%)
  matrix products  3.31 us (1%)
    all_to_all x1, blocking collectives, per_device(): lax.all_to_all(moved.reshape(3, ep_count, exp_dev, 1, piece_rows, columns...  71.7 us
    reduce_scatter x1, waiting for transfers between devices, per_device(): lax.psum_scatter(grad_replica[0].astype(jnp.float32), 'dp', scatter_dimen...  47.4 us
    all_to_all x1, waiting for transfers between devices, per_device(): lax.all_to_all(grads.reshape(exp_dev + rep_dev, ep_count, piece_rows, col...  37.8 us
    reduce_scatter x1, waiting for transfers between devices, per_device(): lax.psum_scatter(grad_owned[0].astype(jnp.float32), 'dp', scatter_dimensi...  25.1 us
    all_to_all x1, starting transfers between devices, per_device(): lax.all_to_all(state.reshape(3, exp_dev, ep_count, piece_rows, columns),...  13.1 us
    all_to_all x1, starting transfers between devices, per_device(): lax.all_to_all(grads.reshape(exp_dev + rep_dev, ep_count, piece_rows, col...  11.1 us
    unnamed x27, local copies, waits for them, and re-layouts  8 us
  transfers between devices with their start and end apart: 4, of which 3 were waited for; matrix products, arithmetic and copies ran while one was open for 7% of the time, Pallas kernels for 0%

profile of v1, /device:TPU:1, one launch (start us, length us, event | category | flops | bytes accessed | tf_op | source)
XLA Modules:
  0.0 265.6 jit_solution(9435780429903846478)
XLA Ops:
  7.2 0.0 copy-start
  7.2 0.0 reduce-scatter.3.cloned.1.call-start
  7.2 3.5 %bitcast_convert_fusion.1 = f32[2,3584,128]{2,1,0:T(8,128)} fusion(bf16[1,2,3584,128]{3,2,1,0:T(8,128)(2,1)} %param.14), kind=kLoop, calls=%fused_computation.8 | loop fusion | flops 917504 | bytes 5505024 | tf_op jit(solution)/shard_map/convert_element_type | solution.py:51
  10.8 0.0 reduce-scatter.3.cloned.1.call-update
  10.8 0.0 reduce-scatter.5.cloned.1.call-start
  10.8 1.4 copy-done.2
  12.3 2.1 bitcast_convert_fusion
  14.4 0.0 reduce-scatter.5.cloned.1.call-update
  14.4 1.2 copy-done.3
  15.5 0.7 copy.81
  16.2 0.7 copy.82
  17.0 0.0 copy-done.5
  17.0 0.7 copy.83
  17.7 1.3 pad_maximum_fusion
  19.0 2.5 copy.84
  21.5 13.1 %all-to-all-start = ((f32[3,2,64,14,128]{4,1,3,0,2:T(2,128)}), f32[3,2,64,14,128]{4,1,3,0,2:T(2,128)S(1)}, u32[]{:S(2)}, u32[]{:S(2)}) async-start(f32[3,2,64,14,128]{4,1,3,0,2:T(2,128)} %copy.84), calls=%async_computation | async-start | bytes 5505024 | tf_op jit(solution)/shard_map/all_to_all | solution.py:42
  34.6 25.1 %reduce-scatter.3.cloned.1.call-done = f32[2,896,128]{2,1,0:T(8,128)} async-done(((f32[2,3584,128]{2,1,0:T(8,128)}), f32[2,896,128]{2,1,0:T(8,128)}) %reduce-scatter.3.cloned.1.call-update) | async-done | bytes 917520 | tf_op jit(solution)/shard_map/reduce_scatter | solution.py:50
  59.7 47.4 %reduce-scatter.5.cloned.1.call-done = f32[2,896,128]{2,1,0:T(8,128)} async-done(((f32[2,3584,128]{2,1,0:T(8,128)}), f32[2,896,128]{2,1,0:T(8,128)}) %reduce-scatter.5.cloned.1.call-update) | async-done | bytes 917520 | tf_op jit(solution)/shard_map/reduce_scatter | solution.py:53
  107.2 1.6 pad_maximum_fusion.2
  108.8 2.5 copy.88
  111.2 0.0 all-to-all-done
  111.2 11.1 %all-to-all-start.1 = ((f32[4,64,14,128]{3,0,2,1:T(4,128)}), f32[4,64,14,128]{3,0,2,1:T(4,128)}, u32[]{:S(2)}, u32[]{:S(2)}) async-start(f32[4,64,14,128]{3,0,2,1:T(4,128)} %bitcast.61), calls=%async_computation.3 | async-start | bytes 3670016 | tf_op jit(solution)/shard_map/all_to_all | solution.py:57
  122.3 0.2 select_reduce_fusion
  122.5 0.1 reduce_sum.14
  122.7 1.2 gather_fusion
  124.0 0.4 copy.102
  124.4 0.5 fusion.13
  124.8 0.7 copy.92
  125.6 1.6 copy.86
  127.2 1.6 copy.87
  128.8 37.8 %all-to-all-done.1 = f32[4,64,14,128]{3,0,2,1:T(4,128)} async-done(((f32[4,64,14,128]{3,0,2,1:T(4,128)}), f32[4,64,14,128]{3,0,2,1:T(4,128)}, u32[]{:S(2)}, u32[]{:S(2)}) %all-to-all-start.1) | async-done | bytes 1835040 | tf_op jit(solution)/shard_map/all_to_all | solution.py:57
  166.7 2.8 %fusion.14 = (f32[64,2,14,128]{3,1,2,0:T(2,128)S(1)}, f32[64,2,14,128]{3,1,2,0:T(2,128)S(1)}) fusion(f32[64,4,14,128]{3,1,2,0:T(4,128)} %bitcast.13), kind=kLoop, calls=%fused_computation.38 | loop fusion | bytes 3670016 | tf_op jit(solution)/shard_map/slice | solution.py:65
  169.5 0.1 copy.90
  169.7 0.0 copy-start.6
  169.7 0.3 copy.103
  170.0 1.2 copy.91
  171.2 0.5 copy.89
  171.7 3.3 %subtract_bitcast_fusion = (f32[1,128,14,128]{3,1,2,0:T(8,128)S(1)}, f32[1,128,14,128]{3,1,2,0:T(8,128)S(1)}, f32[1,128,14,128]{3,1,2,0:T(8,128)S(1)}) fusion(f32[128,14,128]{2,0,1:T(8,128)} %bitcast.65, f32[128,14,128]{2,0,1:T(8,128)} %bitcast.66, f32[128,14,128]{2,0,1:T(8,128)S(1)} %bitcast.64, f32[128,14,128]{2,0,1:T(8,128)S(1)} %bitcast.68, ...), kind=kOutput, calls=%fused_computation.15 | convolution fusion | flops 355565568 | bytes 7341568 | tf_op jit(solution)/shard_map/dot_general | solution.py:74
  175.0 0.3 pad_maximum_fusion.1
  175.3 3.2 %copy.93 = f32[3,128,14,128]{3,2,1,0:T(8,128)} copy(f32[3,128,14,128]{3,1,2,0:T(8,128)S(1)} %pad_maximum_fusion.1) | data formatting | bytes 5505024 | tf_op jit(solution)/shard_map/stack | solution.py:87
  178.5 2.6 gather_fusion.1
  181.1 2.0 copy_select_fusion
  183.1 71.7 %all_to_all.45 = f32[3,64,2,1,14,128]{5,2,4,0,3,1:T(2,128)S(1)} all-to-all(f32[3,64,2,1,14,128]{5,2,4,0,3,1:T(2,128)S(1)} %copy_select_fusion), channel_id=1, replica_groups=mesh['ep'=64,'dp'=4] {'ep'}, dimensions={1} | all-to-all | bytes 5505024 | tf_op jit(solution)/shard_map/all_to_all | solution.py:88
  254.9 0.9 fusion.12
  255.8 0.0 copy-start.1
  255.8 1.0 copy.95
  256.8 1.0 copy.96
  257.8 1.0 copy.97
  (19 shorter events, 0.1 us)
Async XLA Ops:
  7.2 115.5 %copy-start = (s32[64]{0:T(128)S(1)}, s32[64]{0:T(128)}, u32[]{:S(2)}) copy-start(s32[64]{0:T(128)} %param.19) | copy-start | bytes 772
  7.2 52.6 %reduce-scatter.3.cloned.1.call-start = ((), (), s32[]{:S(2)}) async-start(), calls=%async_computation.5 | async-start | bytes 4587520 | tf_op jit(solution)/shard_map/reduce_scatter | solution.py:50
  10.8 1.5 copy-start.2
  10.8 96.4 %reduce-scatter.5.cloned.1.call-start = ((), (), s32[]{:S(2)}) async-start(), calls=%async_computation.6 | async-start | bytes 4587520 | tf_op jit(solution)/shard_map/reduce_scatter | solution.py:53
  14.3 1.2 copy-start.3
  14.3 1.9 copy-start.4
  15.5 1.4 copy-start.5
  21.5 89.7 %all-to-all-start = ((f32[3,2,64,14,128]{4,1,3,0,2:T(2,128)}), f32[3,2,64,14,128]{4,1,3,0,2:T(2,128)S(1)}, u32[]{:S(2)}, u32[]{:S(2)}) async-start(f32[3,2,64,14,128]{4,1,3,0,2:T(2,128)} %copy.84), calls=%async_computation | async-start | bytes 5505024 | tf_op jit(solution)/shard_map/all_to_all | solution.py:42
  111.2 11.1 %copy-start.7 = (s32[128]{0:T(128)S(1)}, s32[128]{0:T(128)}, u32[]{:S(2)}) copy-start(s32[128]{0:T(128)} %param.16) | copy-start | bytes 1540
  111.2 11.1 %copy-start.9 = (s32[128]{0:T(128)S(1)}, s32[128]{0:T(128)}, u32[]{:S(2)}) copy-start(s32[128]{0:T(128)} %param.17) | copy-start | bytes 1540
  111.2 11.4 %copy-start.8 = (s32[128]{0:T(128)S(1)}, s32[128]{0:T(128)}, u32[]{:S(2)}) copy-start(s32[128]{0:T(128)} %constant.134) | copy-start | bytes 1540
  111.2 55.4 %all-to-all-start.1 = ((f32[4,64,14,128]{3,0,2,1:T(4,128)}), f32[4,64,14,128]{3,0,2,1:T(4,128)}, u32[]{:S(2)}, u32[]{:S(2)}) async-start(f32[4,64,14,128]{3,0,2,1:T(4,128)} %bitcast.61), calls=%async_computation.3 | async-start | bytes 3670016 | tf_op jit(solution)/shard_map/all_to_all | solution.py:57
  169.7 2.0 copy-start.6
  255.8 3.0 %copy-start.1 = (s32[64]{0:T(128)S(1)}, s32[64]{0:T(128)}, u32[]{:S(2)}) copy-start(s32[64]{0:T(128)} %param.19) | copy-start | bytes 772
Sparse Core Ops, SparseCore 0:
  10.9 48.7 reduce-scatter.2
  62.3 44.8 reduce-scatter.4

commit v2 on v1

--- a/solution.py
+++ b/solution.py
@@ -20,7 +20,7 @@
     return (moved_weight, moved_first, moved_second)
 
 
-def per_device(
+def per_device_body(
     master_weight,
     first_moment,
     second_moment,
@@ -47,13 +47,18 @@
         tiled=True,
     ).reshape(3, experts, piece_rows, columns)
 
-    owned_part = lax.psum_scatter(
-        grad_owned[0].astype(jnp.float32), "dp", scatter_dimension=1, tiled=True
+    dp_count = lax.axis_size("dp")
+    dp_index = lax.axis_index("dp")
+    raw = jnp.concatenate([grad_owned[0], grad_replica[0]], axis=0).reshape(
+        exp_dev + rep_dev, dp_count, shard_rows, columns
     )
-    replica_part = lax.psum_scatter(
-        grad_replica[0].astype(jnp.float32), "dp", scatter_dimension=1, tiled=True
-    )
-    grads = jnp.concatenate([owned_part, replica_part], axis=0)
+    grads = lax.dynamic_index_in_dim(raw, dp_index, axis=1, keepdims=False).astype(jnp.float32)
+    for shift in range(1, dp_count):
+        block = lax.dynamic_index_in_dim(raw, (dp_index + shift) % dp_count, axis=1, keepdims=False)
+        got = lax.ppermute(
+            block, "dp", [(i, (i + shift) % dp_count) for i in range(dp_count)]
+        )
+        grads = grads + got.astype(jnp.float32)
     grads_p = lax.all_to_all(
         grads.reshape(exp_dev + rep_dev, ep_count, piece_rows, columns),
         "ep",
@@ -109,5 +114,5 @@
     )
     out_specs = (P("ep", "dp", None), P("ep", "dp", None), P("ep", "dp", None))
     return jax.shard_map(
-        per_device, mesh=mesh, in_specs=in_specs, out_specs=out_specs, check_vma=False
+        per_device_body, mesh=mesh, in_specs=in_specs, out_specs=out_specs, check_vma=False
     )

time: 266 us -> 280 us (1.053)
  waiting for transfers between devices: 110 us -> 128 us
  between operations: 14.3 us -> 0.99 us
  local copies, waits for them, and re-layouts: 30.2 us -> 37.5 us
    reduce_scatter x2 -> x0, waiting for transfers between devices: 72.5 us -> none  [the longest x1 47.4 us: per_device(): lax.psum_scatter(grad_replica[0].astype(jnp.float32), 'dp', scatter_dimen...]
    all_to_all x2, waiting for transfers between devices: 37.8 us -> 89.3 us  [the longest x1 52 us: per_device_body(): lax.all_to_all(state.reshape(3, exp_dev, ep_count, piece_rows, columns),...]
    ppermute x0 -> x3, waiting for transfers between devices: none -> 38.6 us  [per_device_body(): lax.ppermute(block, 'dp', [(i, (i + shift) % dp_count) for i in range(dp_...]
    ppermute x0 -> x3, starting transfers between devices: none -> 5.63 us  [per_device_body(): lax.ppermute(block, 'dp', [(i, (i + shift) % dp_count) for i in range(dp_...]
    convert_element_type x3 -> x1, other arithmetic: 5.62 us -> 0.01 us  [per_device_body(): live_mask = (lax.iota(jnp.int32, replica_slots) % rep_dev < jnp.repeat(re...]
    squeeze x0 -> x1, other arithmetic: none -> 5.14 us  [per_device_body(): lax.dynamic_index_in_dim(raw, (dp_index + shift) % dp_count, axis=1, keep...]
    add x0 -> x1, other arithmetic: none -> 4.49 us  [per_device_body(): grads = grads + got.astype(jnp.float32)]
    all_to_all x2, starting transfers between devices: 24.2 us -> 20 us  [the longest x1 13.3 us: per_device_body(): lax.all_to_all(grads.reshape(exp_dev + rep_dev, ep_count, piece_rows, col...]
  transfers between devices with their start and end apart: 4 -> 5, of which waited for: 3 -> 4; matrix products, arithmetic and copies ran while one was open for 7% -> 7% of each run, Pallas kernels for 0% -> 0%
where the time goes in v2:
time: 280 us; the launch traced here: 279 us
  waiting for transfers between devices  128 us (46%)
  blocking collectives  72 us (26%)
  local copies, waits for them, and re-layouts  37.5 us (13%)
  starting transfers between devices  25.6 us (9%)
  other arithmetic  13.7 us (5%)
    all_to_all x1, blocking collectives, per_device_body(): lax.all_to_all(moved.reshape(3, ep_count, exp_dev, 1, piece_rows, columns...  72 us
    all_to_all x1, waiting for transfers between devices, per_device_body(): lax.all_to_all(state.reshape(3, exp_dev, ep_count, piece_rows, columns),...  52 us
    ppermute x3, waiting for transfers between devices, per_device_body(): lax.ppermute(block, 'dp', [(i, (i + shift) % dp_count) for i in range(dp_...  38.6 us
    all_to_all x1, waiting for transfers between devices, per_device_body(): lax.all_to_all(grads.reshape(exp_dev + rep_dev, ep_count, piece_rows, col...  37.3 us
    all_to_all x1, starting transfers between devices, per_device_body(): lax.all_to_all(grads.reshape(exp_dev + rep_dev, ep_count, piece_rows, col...  13.3 us
    unnamed x29, local copies, waits for them, and re-layouts  8.78 us
    concatenate x2, local copies, waits for them, and re-layouts, per_device_body(): jnp.concatenate([grad_owned[0], grad_replica[0]], axis=0)  6.66 us
    all_to_all x1, starting transfers between devices, per_device_body(): lax.all_to_all(state.reshape(3, exp_dev, ep_count, piece_rows, columns),...  6.64 us
  transfers between devices with their start and end apart: 5, of which 4 were waited for; matrix products, arithmetic and copies ran while one was open for 7% of the time, Pallas kernels for 0%

profile of v2, /device:TPU:1, one launch (start us, length us, event | category | flops | bytes accessed | tf_op | source)
XLA Modules:
  0.0 279.2 jit_solution(12235778595401532669)
XLA Ops:
  0.6 0.0 copy-start
  0.7 3.5 %copy.91 = bf16[2,4,896,128]{3,0,2,1:T(2,128)(2,1)S(1)} copy(bf16[2,4,896,128]{3,2,1,0:T(8,128)(2,1)} %bitcast.81) | data formatting | bytes 3670016 | tf_op jit(solution)/shard_map/concatenate | solution.py:52
  4.2 3.1 %copy.92 = bf16[2,4,896,128]{3,0,2,1:T(2,128)(2,1)} copy(bf16[2,4,896,128]{3,2,1,0:T(8,128)(2,1)S(1)} %bitcast.82) | data formatting | bytes 3670016 | tf_op jit(solution)/shard_map/concatenate | solution.py:52
  7.4 5.1 %fusion.8 = (bf16[4,896,128]{2,0,1:T(4,128)(2,1)}, bf16[4,896,128]{2,0,1:T(4,128)(2,1)}, bf16[4,896,128]{2,0,1:T(4,128)(2,1)}) fusion(s32[]{:T(128)S(6)} %select_n.89, bf16[2,4,896,128]{3,0,2,1:T(2,128)(2,1)} %copy.92, bf16[2,4,896,128]{3,0,2,1:T(2,128)(2,1)S(1)} %copy.91, s32[]{:T(128)S(6)} %select_n.91, s32[]{:T(128)S(6)} %select_n.93), kind=kLoop, calls=%fused_computation.30 | loop fusion | flops 5505024 | bytes 6422540 | tf_op jit(solution)/shard_map/jit(dynamic_index_in_dim)/squeeze | solution.py:57
  12.5 2.0 collective-permute-start
  14.5 2.5 collective-permute-start.1
  17.0 1.2 collective-permute-start.2
  18.1 15.7 %collective-permute-done = bf16[4,896,128]{2,0,1:T(4,128)(2,1)S(1)} collective-permute-done((bf16[4,896,128]{2,0,1:T(4,128)(2,1)}, bf16[4,896,128]{2,0,1:T(4,128)(2,1)S(1)}, u32[]{:S(2)}, u32[]{:S(2)}) %collective-permute-start) | collective-permute-done | bytes 917536 | tf_op jit(solution)/shard_map/ppermute | solution.py:58
  33.9 22.9 %collective-permute-done.1 = bf16[4,896,128]{2,0,1:T(4,128)(2,1)} collective-permute-done((bf16[4,896,128]{2,0,1:T(4,128)(2,1)}, bf16[4,896,128]{2,0,1:T(4,128)(2,1)}, u32[]{:S(2)}, u32[]{:S(2)}) %collective-permute-start.1) | collective-permute-done | bytes 917536 | tf_op jit(solution)/shard_map/ppermute | solution.py:58
  56.7 0.0 collective-permute-done.2
  56.7 4.5 %fusion.1 = f32[4,896,128]{2,0,1:T(4,128)} fusion(bf16[4,896,128]{2,0,1:T(4,128)(2,1)} %collective-permute-done.2, bf16[4,896,128]{2,0,1:T(4,128)(2,1)} %collective-permute-done.1, bf16[4,896,128]{2,0,1:T(4,128)(2,1)S(1)} %collective-permute-done, s32[]{:T(128)S(6)} %select_n.87, bf16[2,4,896,128]{3,0,2,1:T(2,128)(2,1)} %copy.92, ...), kind=kLoop, calls=%fused_computation.16 | loop fusion | flops 5046272 | bytes 8257540 | tf_op jit(solution)/shard_map/add | solution.py:61
  61.2 13.3 %all-to-all-start.1 = ((f32[4,64,14,128]{3,0,2,1:T(4,128)}), f32[4,64,14,128]{3,0,2,1:T(4,128)S(1)}, u32[]{:S(2)}, u32[]{:S(2)}) async-start(f32[4,64,14,128]{3,0,2,1:T(4,128)} %bitcast.67), calls=%async_computation.1 | async-start | bytes 3670016 | tf_op jit(solution)/shard_map/all_to_all | solution.py:62
  74.6 0.0 copy-start.6
  74.6 0.7 copy.84
  75.3 1.9 copy.85
  77.2 0.7 copy.86
  77.9 1.3 pad_maximum_fusion
  79.2 2.5 copy.87
  81.7 37.3 %all-to-all-done.1 = f32[4,64,14,128]{3,0,2,1:T(4,128)S(1)} async-done(((f32[4,64,14,128]{3,0,2,1:T(4,128)}), f32[4,64,14,128]{3,0,2,1:T(4,128)S(1)}, u32[]{:S(2)}, u32[]{:S(2)}) %all-to-all-start.1) | async-done | bytes 1835040 | tf_op jit(solution)/shard_map/all_to_all | solution.py:62
  119.0 1.2 copy-done.1
  120.2 6.6 %all-to-all-start = ((f32[3,2,64,14,128]{4,1,3,0,2:T(2,128)}), f32[3,2,64,14,128]{4,1,3,0,2:T(2,128)S(1)}, u32[]{:S(2)}, u32[]{:S(2)}) async-start(f32[3,2,64,14,128]{4,1,3,0,2:T(2,128)} %copy.87), calls=%async_computation | async-start | bytes 5505024 | tf_op jit(solution)/shard_map/all_to_all | solution.py:42
  126.9 0.2 select_reduce_fusion
  127.0 0.1 reduce_sum.14
  127.2 1.2 gather_fusion
  128.5 3.8 %fusion.23 = (f32[64,2,14,128]{3,1,2,0:T(2,128)S(1)}, f32[64,2,14,128]{3,1,2,0:T(2,128)}) fusion(f32[64,4,14,128]{3,1,2,0:T(4,128)} %bitcast.66), kind=kLoop, calls=%fused_computation.53 | loop fusion | bytes 3670016 | tf_op jit(solution)/shard_map/slice | solution.py:70
  132.3 0.1 copy.94
  132.4 1.2 copy.107
  133.7 2.4 copy.95
  136.1 2.6 copy.93
  138.6 52.0 %all-to-all-done = f32[3,2,64,14,128]{4,1,3,0,2:T(2,128)S(1)} async-done(((f32[3,2,64,14,128]{4,1,3,0,2:T(2,128)}), f32[3,2,64,14,128]{4,1,3,0,2:T(2,128)S(1)}, u32[]{:S(2)}, u32[]{:S(2)}) %all-to-all-start) | async-done | bytes 2752544 | tf_op jit(solution)/shard_map/all_to_all | solution.py:42
  190.6 0.4 copy.106
  191.0 0.3 fusion.22
  191.3 0.0 copy-start.2
  191.3 0.0 copy-start.3
  191.3 0.0 copy-start.7
  191.3 0.7 copy.96
  192.0 0.7 copy.89
  192.8 0.7 copy.90
  193.5 1.6 subtract_bitcast_fusion
  195.1 0.3 pad_maximum_fusion.1
  195.4 3.2 %copy.97 = f32[3,128,14,128]{3,2,1,0:T(8,128)} copy(f32[3,128,14,128]{3,1,2,0:T(8,128)S(1)} %pad_maximum_fusion.1) | data formatting | bytes 5505024 | tf_op jit(solution)/shard_map/stack | solution.py:92
  198.6 2.6 gather_fusion.1
  201.3 2.0 copy_select_fusion
  203.3 72.0 %all_to_all.45 = f32[3,64,2,1,14,128]{5,2,4,0,3,1:T(2,128)S(1)} all-to-all(f32[3,64,2,1,14,128]{5,2,4,0,3,1:T(2,128)S(1)} %copy_select_fusion), channel_id=1, replica_groups=mesh['ep'=64,'dp'=4] {'ep'}, dimensions={1} | all-to-all | bytes 5505024 | tf_op jit(solution)/shard_map/all_to_all | solution.py:93
  275.3 0.9 fusion.21
  276.3 1.0 copy.100
  277.3 1.0 copy.101
  278.2 1.0 copy.99
  (21 shorter events, 0.1 us)
Async XLA Ops:
  0.6 126.6 %copy-start = (s32[64]{0:T(128)S(1)}, s32[64]{0:T(128)}, u32[]{:S(2)}) copy-start(s32[64]{0:T(128)} %param.19) | copy-start | bytes 772
  0.7 3.5 %copy-start.4 = (bf16[1,2,3584,128]{3,2,1,0:T(8,128)(2,1)S(1)}, bf16[1,2,3584,128]{3,2,1,0:T(8,128)(2,1)}, u32[]{:S(2)}) copy-start(bf16[1,2,3584,128]{3,2,1,0:T(8,128)(2,1)} %param.15) | copy-start | bytes 5505028
  12.5 21.4 %collective-permute-start = (bf16[4,896,128]{2,0,1:T(4,128)(2,1)}, bf16[4,896,128]{2,0,1:T(4,128)(2,1)S(1)}, u32[]{:S(2)}, u32[]{:S(2)}) collective-permute-start(bf16[4,896,128]{2,0,1:T(4,128)(2,1)} %get-tuple-element.30), channel_id=1, source_target_pairs={{0,1},{1,2},{2,3},{3,0},{4,5},{5,6},{6,7},{7,4},{8,9},{9,10},{10,1... | collective-permute-start | bytes 2752520 | tf_op jit(solution)/shard_map/ppermute | solution.py:58
  14.5 42.2 %collective-permute-start.1 = (bf16[4,896,128]{2,0,1:T(4,128)(2,1)}, bf16[4,896,128]{2,0,1:T(4,128)(2,1)}, u32[]{:S(2)}, u32[]{:S(2)}) collective-permute-start(bf16[4,896,128]{2,0,1:T(4,128)(2,1)} %get-tuple-element.31), channel_id=1, source_target_pairs={{0,2},{1,3},{2,0},{3,1},{4,6},{5,7},{6,4},{7,5},{8,10},{9,11},{10,... | collective-permute-start | bytes 2752520 | tf_op jit(solution)/shard_map/ppermute | solution.py:58
  17.0 39.7 %collective-permute-start.2 = (bf16[4,896,128]{2,0,1:T(4,128)(2,1)}, bf16[4,896,128]{2,0,1:T(4,128)(2,1)}, u32[]{:S(2)}, u32[]{:S(2)}) collective-permute-start(bf16[4,896,128]{2,0,1:T(4,128)(2,1)} %get-tuple-element.32), channel_id=1, source_target_pairs={{0,3},{1,0},{2,1},{3,2},{4,7},{5,4},{6,5},{7,6},{8,11},{9,8},{10,9... | collective-permute-start | bytes 2752520 | tf_op jit(solution)/shard_map/ppermute | solution.py:58
  61.2 13.3 %copy-start.5 = (f32[2,896,128]{2,1,0:T(8,128)S(1)}, f32[2,896,128]{2,1,0:T(8,128)}, u32[]{:S(2)}) copy-start(f32[2,896,128]{2,1,0:T(8,128)} %param.11) | copy-start | bytes 2752516
  61.2 57.7 %all-to-all-start.1 = ((f32[4,64,14,128]{3,0,2,1:T(4,128)}), f32[4,64,14,128]{3,0,2,1:T(4,128)S(1)}, u32[]{:S(2)}, u32[]{:S(2)}) async-start(f32[4,64,14,128]{3,0,2,1:T(4,128)} %bitcast.67), calls=%async_computation.1 | async-start | bytes 3670016 | tf_op jit(solution)/shard_map/all_to_all | solution.py:62
  74.6 2.6 copy-start.6
  81.7 45.2 %copy-start.8 = (s32[128]{0:T(128)S(1)}, s32[128]{0:T(128)}, u32[]{:S(2)}) copy-start(s32[128]{0:T(128)} %param.16) | copy-start | bytes 1540
  81.7 45.2 %copy-start.10 = (s32[128]{0:T(128)S(1)}, s32[128]{0:T(128)}, u32[]{:S(2)}) copy-start(s32[128]{0:T(128)} %param.17) | copy-start | bytes 1540
  81.7 45.5 %copy-start.9 = (s32[128]{0:T(128)S(1)}, s32[128]{0:T(128)}, u32[]{:S(2)}) copy-start(s32[128]{0:T(128)} %constant.170) | copy-start | bytes 1540
  119.0 1.2 copy-start.1
  120.2 70.4 %all-to-all-start = ((f32[3,2,64,14,128]{4,1,3,0,2:T(2,128)}), f32[3,2,64,14,128]{4,1,3,0,2:T(2,128)S(1)}, u32[]{:S(2)}, u32[]{:S(2)}) async-start(f32[3,2,64,14,128]{4,1,3,0,2:T(2,128)} %copy.87), calls=%async_computation | async-start | bytes 5505024 | tf_op jit(solution)/shard_map/all_to_all | solution.py:42
  191.3 2.2 copy-start.2
  191.3 2.2 copy-start.3
  191.3 2.2 copy-start.7

commit v3 on v2

--- a/solution.py
+++ b/solution.py
@@ -59,37 +59,40 @@
             block, "dp", [(i, (i + shift) % dp_count) for i in range(dp_count)]
         )
         grads = grads + got.astype(jnp.float32)
+    source_index = jnp.sum(
+        jnp.where(
+            new_experts[:, None] == old_experts[None, :], lax.iota(jnp.int32, experts)[None, :], 0
+        ),
+        axis=1,
+    )
+    state_new = jnp.take(state_p, source_index, axis=1)
+
     grads_p = lax.all_to_all(
         grads.reshape(exp_dev + rep_dev, ep_count, piece_rows, columns),
         "ep",
         split_axis=1,
         concat_axis=0,
         tiled=True,
-    ).reshape(ep_count, exp_dev + rep_dev, piece_rows, columns)
-    owned_t = grads_p[:, :exp_dev].reshape(experts, piece_rows, columns)
-    replica_t = grads_p[:, exp_dev:].reshape(replica_slots, piece_rows * columns)
+    ).reshape(ep_count * (exp_dev + rep_dev), piece_rows * columns)
 
-    live_mask = (
-        lax.iota(jnp.int32, replica_slots) % rep_dev
-        < jnp.repeat(rep_count, rep_dev, total_repeat_length=replica_slots)
-    ).astype(jnp.float32)
-    replica_match = jnp.where(
-        rep_expert[None, :] == old_experts[:, None], live_mask[None, :], jnp.float32(0.0)
+    column = lax.iota(jnp.int32, ep_count * (exp_dev + rep_dev))
+    device_of, within = column // (exp_dev + rep_dev), column % (exp_dev + rep_dev)
+    is_owned = within < exp_dev
+    old_slot = jnp.clip(device_of * exp_dev + within, 0, experts - 1)
+    rep_slot = jnp.clip(device_of * rep_dev + within - exp_dev, 0, replica_slots - 1)
+    live = (rep_slot % rep_dev < rep_count[rep_slot // rep_dev]).astype(jnp.float32)
+    column_expert = jnp.where(is_owned, old_experts[old_slot], rep_expert[rep_slot])
+    column_weight = jnp.where(is_owned, jnp.float32(1.0), live)
+    combine = jnp.where(
+        new_experts[:, None] == column_expert[None, :], column_weight[None, :], jnp.float32(0.0)
     )
-    gradient = owned_t + jnp.dot(
-        replica_match,
-        replica_t,
+    gradient = jnp.dot(
+        combine,
+        grads_p,
         precision=lax.Precision.HIGHEST,
         preferred_element_type=jnp.float32,
     ).reshape(experts, piece_rows, columns)
-    source_index = jnp.sum(
-        jnp.where(
-            new_experts[:, None] == old_experts[None, :], lax.iota(jnp.int32, experts)[None, :], 0
-        ),
-        axis=1,
-    )
-    moved = adam_update(state_p[0], state_p[1], state_p[2], gradient)
-    moved = jnp.take(jnp.stack(moved), source_index, axis=1)
+    moved = jnp.stack(adam_update(state_new[0], state_new[1], state_new[2], gradient))
     back = lax.all_to_all(
         moved.reshape(3, ep_count, exp_dev, 1, piece_rows, columns),
         "ep",

time: 280 us -> 282 us (level)
    slice x4 -> x0, local copies, waits for them, and re-layouts: 7.18 us -> none  [the longest x2 3.9 us: per_device_body(): grads_p[:, exp_dev:].reshape(replica_slots, piece_rows * columns)]
    gather x2 -> x4, local copies, waits for them, and re-layouts: 3.86 us -> 8.24 us  [the longest x1 2.64 us: per_device_body(): state_new = jnp.take(state_p, source_index, axis=1)]
    reshape x0 -> x1, local copies, waits for them, and re-layouts: none -> 3.24 us  [per_device_body(): state_p = lax.all_to_all(state.reshape(3, exp_dev, ep_count, piece_rows,...]
    unnamed x29 -> x25, local copies, waits for them, and re-layouts: 8.78 us -> 10.1 us
where the time goes in v3:
time: 282 us; the launch traced here: 281 us
  waiting for transfers between devices  127 us (45%)
  blocking collectives  72 us (26%)
  local copies, waits for them, and re-layouts  38.7 us (14%)
  starting transfers between devices  25.6 us (9%)
  other arithmetic  14.6 us (5%)
    all_to_all x1, blocking collectives, per_device_body(): lax.all_to_all(moved.reshape(3, ep_count, exp_dev, 1, piece_rows, columns...  72 us
    all_to_all x1, waiting for transfers between devices, per_device_body(): lax.all_to_all(state.reshape(3, exp_dev, ep_count, piece_rows, columns),...  51.1 us
    ppermute x3, waiting for transfers between devices, per_device_body(): lax.ppermute(block, 'dp', [(i, (i + shift) % dp_count) for i in range(dp_...  38.6 us
    all_to_all x1, waiting for transfers between devices, per_device_body(): lax.all_to_all(grads.reshape(exp_dev + rep_dev, ep_count, piece_rows, col...  37.3 us
    all_to_all x1, starting transfers between devices, per_device_body(): lax.all_to_all(grads.reshape(exp_dev + rep_dev, ep_count, piece_rows, col...  13.3 us
    unnamed x25, local copies, waits for them, and re-layouts  10.1 us
    concatenate x2, local copies, waits for them, and re-layouts, per_device_body(): jnp.concatenate([grad_owned[0], grad_replica[0]], axis=0)  6.67 us
    all_to_all x1, starting transfers between devices, per_device_body(): lax.all_to_all(state.reshape(3, exp_dev, ep_count, piece_rows, columns),...  6.64 us
  transfers between devices with their start and end apart: 5, of which 4 were waited for; matrix products, arithmetic and copies ran while one was open for 7% of the time, Pallas kernels for 0%

profile of v3, /device:TPU:1, one launch (start us, length us, event | category | flops | bytes accessed | tf_op | source)
XLA Modules:
  0.0 281.5 jit_solution(7166358018590053425)
XLA Ops:
  0.6 0.0 copy-start
  0.7 0.0 copy-start.4
  0.7 3.5 %copy.56 = bf16[2,4,896,128]{3,0,2,1:T(2,128)(2,1)S(1)} copy(bf16[2,4,896,128]{3,2,1,0:T(8,128)(2,1)} %bitcast.83) | data formatting | bytes 3670016 | tf_op jit(solution)/shard_map/concatenate | solution.py:52
  4.2 0.0 copy-done.4
  4.2 3.2 %copy.57 = bf16[2,4,896,128]{3,0,2,1:T(2,128)(2,1)} copy(bf16[2,4,896,128]{3,2,1,0:T(8,128)(2,1)S(1)} %bitcast.84) | data formatting | bytes 3670016 | tf_op jit(solution)/shard_map/concatenate | solution.py:52
  7.4 5.1 %fusion.12 = (bf16[4,896,128]{2,0,1:T(4,128)(2,1)}, bf16[4,896,128]{2,0,1:T(4,128)(2,1)}, bf16[4,896,128]{2,0,1:T(4,128)(2,1)}) fusion(s32[]{:T(128)S(6)} %select_n.205, bf16[2,4,896,128]{3,0,2,1:T(2,128)(2,1)} %copy.57, bf16[2,4,896,128]{3,0,2,1:T(2,128)(2,1)S(1)} %copy.56, s32[]{:T(128)S(6)} %select_n.207, s32[]{:T(128)S(6)} %select_n.209), kind=kLoop, calls=%fused_computation.34 | loop fusion | flops 5505024 | bytes 6422540 | tf_op jit(solution)/shard_map/jit(dynamic_index_in_dim)/squeeze | solution.py:57
  12.5 2.0 collective-permute-start
  14.5 2.5 collective-permute-start.1
  17.0 1.2 collective-permute-start.2
  18.2 15.7 %collective-permute-done = bf16[4,896,128]{2,0,1:T(4,128)(2,1)S(1)} collective-permute-done((bf16[4,896,128]{2,0,1:T(4,128)(2,1)}, bf16[4,896,128]{2,0,1:T(4,128)(2,1)S(1)}, u32[]{:S(2)}, u32[]{:S(2)}) %collective-permute-start) | collective-permute-done | bytes 917536 | tf_op jit(solution)/shard_map/ppermute | solution.py:58
  33.9 22.9 %collective-permute-done.1 = bf16[4,896,128]{2,0,1:T(4,128)(2,1)} collective-permute-done((bf16[4,896,128]{2,0,1:T(4,128)(2,1)}, bf16[4,896,128]{2,0,1:T(4,128)(2,1)}, u32[]{:S(2)}, u32[]{:S(2)}) %collective-permute-start.1) | collective-permute-done | bytes 917536 | tf_op jit(solution)/shard_map/ppermute | solution.py:58
  56.7 0.0 collective-permute-done.2
  56.7 4.5 %fusion.2 = f32[4,896,128]{2,0,1:T(4,128)} fusion(bf16[4,896,128]{2,0,1:T(4,128)(2,1)} %collective-permute-done.2, bf16[4,896,128]{2,0,1:T(4,128)(2,1)} %collective-permute-done.1, bf16[4,896,128]{2,0,1:T(4,128)(2,1)S(1)} %collective-permute-done, s32[]{:T(128)S(6)} %select_n.203, bf16[2,4,896,128]{3,0,2,1:T(2,128)(2,1)} %copy.57, ...), kind=kLoop, calls=%fused_computation.19 | loop fusion | flops 5046272 | bytes 8257540 | tf_op jit(solution)/shard_map/add | solution.py:61
  61.3 13.3 %all-to-all-start.1 = ((f32[4,64,14,128]{3,0,2,1:T(4,128)}), f32[4,64,14,128]{3,0,2,1:T(4,128)S(1)}, u32[]{:S(2)}, u32[]{:S(2)}) async-start(f32[4,64,14,128]{3,0,2,1:T(4,128)} %bitcast.76), calls=%async_computation.1 | async-start | bytes 3670016 | tf_op jit(solution)/shard_map/all_to_all | solution.py:70
  74.6 0.0 copy-done.6
  74.6 0.0 copy-start.7
  74.6 0.7 copy.49
  75.3 1.9 copy.50
  77.2 0.7 copy.51
  77.9 1.3 pad_maximum_fusion
  79.2 2.5 copy.52
  81.7 37.3 %all-to-all-done.1 = f32[4,64,14,128]{3,0,2,1:T(4,128)S(1)} async-done(((f32[4,64,14,128]{3,0,2,1:T(4,128)}), f32[4,64,14,128]{3,0,2,1:T(4,128)S(1)}, u32[]{:S(2)}, u32[]{:S(2)}) %all-to-all-start.1) | async-done | bytes 1835040 | tf_op jit(solution)/shard_map/all_to_all | solution.py:70
  119.0 1.3 copy-done.3
  120.2 6.6 %all-to-all-start = ((f32[3,2,64,14,128]{4,1,3,0,2:T(2,128)}), f32[3,2,64,14,128]{4,1,3,0,2:T(2,128)S(1)}, u32[]{:S(2)}, u32[]{:S(2)}) async-start(f32[3,2,64,14,128]{4,1,3,0,2:T(2,128)} %copy.52), calls=%async_computation | async-start | bytes 5505024 | tf_op jit(solution)/shard_map/all_to_all | solution.py:42
  126.9 0.0 copy-start.8
  126.9 0.0 copy-done.2
  127.0 1.9 gather_fusion.1
  128.9 1.9 gather_fusion.2
  130.8 1.9 gather_fusion.3
  132.7 0.2 select_reduce_fusion
  132.9 1.8 copy.58
  134.7 2.0 copy.72
  136.7 2.8 copy.59
  139.5 51.1 %all-to-all-done = f32[3,2,64,14,128]{4,1,3,0,2:T(2,128)S(1)} async-done(((f32[3,2,64,14,128]{4,1,3,0,2:T(2,128)}), f32[3,2,64,14,128]{4,1,3,0,2:T(2,128)S(1)}, u32[]{:S(2)}, u32[]{:S(2)}) %all-to-all-start) | async-done | bytes 2752544 | tf_op jit(solution)/shard_map/all_to_all | solution.py:42
  190.6 1.5 copy.53
  192.2 3.2 %copy.54 = f32[3,128,14,128]{3,2,1,0:T(8,128)} copy(f32[3,128,14,128]{3,1,2,0:T(8,128)S(1)} %bitcast.72) | data formatting | bytes 5505024 | tf_op jit(solution)/shard_map/reshape | solution.py:48
  195.4 2.6 gather_fusion
  198.1 0.0 copy-start.5
  198.1 1.0 fusion
  199.1 0.5 copy-done.5
  199.6 2.5 multiply_subtract_fusion
  202.1 2.4 pad_maximum_fusion.1
  204.6 0.9 copy.66
  205.5 72.0 %all_to_all.45 = f32[3,64,2,1,14,128]{5,2,4,0,3,1:T(2,128)S(1)} all-to-all(f32[3,64,2,1,14,128]{5,2,4,0,3,1:T(2,128)S(1)} %copy.66), channel_id=1, replica_groups=mesh['ep'=64,'dp'=4] {'ep'}, dimensions={1} | all-to-all | bytes 5505024 | tf_op jit(solution)/shard_map/all_to_all | solution.py:96
  277.6 0.9 fusion.34
  278.5 1.0 copy.63
  279.5 1.0 copy.64
  280.5 1.0 copy.65
  (18 shorter events, 0.1 us)
Async XLA Ops:
  0.6 128.2 %copy-start = (s32[128]{0:T(128)S(1)}, s32[128]{0:T(128)}, u32[]{:S(2)}) copy-start(s32[128]{0:T(128)} %param.16) | copy-start | bytes 1540
  0.7 3.5 %copy-start.4 = (bf16[1,2,3584,128]{3,2,1,0:T(8,128)(2,1)S(1)}, bf16[1,2,3584,128]{3,2,1,0:T(8,128)(2,1)}, u32[]{:S(2)}) copy-start(bf16[1,2,3584,128]{3,2,1,0:T(8,128)(2,1)} %param.13) | copy-start | bytes 5505028
  12.5 21.4 %collective-permute-start = (bf16[4,896,128]{2,0,1:T(4,128)(2,1)}, bf16[4,896,128]{2,0,1:T(4,128)(2,1)S(1)}, u32[]{:S(2)}, u32[]{:S(2)}) collective-permute-start(bf16[4,896,128]{2,0,1:T(4,128)(2,1)} %get-tuple-element.15), channel_id=1, source_target_pairs={{0,1},{1,2},{2,3},{3,0},{4,5},{5,6},{6,7},{7,4},{8,9},{9,10},{10,1... | collective-permute-start | bytes 2752520 | tf_op jit(solution)/shard_map/ppermute | solution.py:58
  14.5 42.2 %collective-permute-start.1 = (bf16[4,896,128]{2,0,1:T(4,128)(2,1)}, bf16[4,896,128]{2,0,1:T(4,128)(2,1)}, u32[]{:S(2)}, u32[]{:S(2)}) collective-permute-start(bf16[4,896,128]{2,0,1:T(4,128)(2,1)} %get-tuple-element.16), channel_id=1, source_target_pairs={{0,2},{1,3},{2,0},{3,1},{4,6},{5,7},{6,4},{7,5},{8,10},{9,11},{10,... | collective-permute-start | bytes 2752520 | tf_op jit(solution)/shard_map/ppermute | solution.py:58
  17.0 39.7 %collective-permute-start.2 = (bf16[4,896,128]{2,0,1:T(4,128)(2,1)}, bf16[4,896,128]{2,0,1:T(4,128)(2,1)}, u32[]{:S(2)}, u32[]{:S(2)}) collective-permute-start(bf16[4,896,128]{2,0,1:T(4,128)(2,1)} %get-tuple-element.17), channel_id=1, source_target_pairs={{0,3},{1,0},{2,1},{3,2},{4,7},{5,4},{6,5},{7,6},{8,11},{9,8},{10,9... | collective-permute-start | bytes 2752520 | tf_op jit(solution)/shard_map/ppermute | solution.py:58
  61.3 13.3 %copy-start.6 = (f32[2,896,128]{2,1,0:T(8,128)S(1)}, f32[2,896,128]{2,1,0:T(8,128)}, u32[]{:S(2)}) copy-start(f32[2,896,128]{2,1,0:T(8,128)} %param.9) | copy-start | bytes 2752516
  61.3 57.7 %all-to-all-start.1 = ((f32[4,64,14,128]{3,0,2,1:T(4,128)}), f32[4,64,14,128]{3,0,2,1:T(4,128)S(1)}, u32[]{:S(2)}, u32[]{:S(2)}) async-start(f32[4,64,14,128]{3,0,2,1:T(4,128)} %bitcast.76), calls=%async_computation.1 | async-start | bytes 3670016 | tf_op jit(solution)/shard_map/all_to_all | solution.py:70
  74.6 2.6 copy-start.7
  81.7 45.2 %copy-start.2 = (s32[128]{0:T(128)S(1)}, s32[128]{0:T(128)}, u32[]{:S(2)}) copy-start(s32[128]{0:T(128)} %param.14) | copy-start | bytes 1540
  81.7 49.1 %copy-start.1 = (s32[64]{0:T(128)S(1)}, s32[64]{0:T(128)}, u32[]{:S(2)}) copy-start(s32[64]{0:T(128)} %param.17) | copy-start | bytes 772
  119.0 1.3 copy-start.3
  120.2 70.4 %all-to-all-start = ((f32[3,2,64,14,128]{4,1,3,0,2:T(2,128)}), f32[3,2,64,14,128]{4,1,3,0,2:T(2,128)S(1)}, u32[]{:S(2)}, u32[]{:S(2)}) async-start(f32[3,2,64,14,128]{4,1,3,0,2:T(2,128)} %copy.52), calls=%async_computation | async-start | bytes 5505024 | tf_op jit(solution)/shard_map/all_to_all | solution.py:42
  126.9 5.8 %copy-start.8 = (s32[128]{0:T(128)S(1)}, s32[128]{0:T(128)}, u32[]{:S(2)}) copy-start(s32[128]{0:T(128)} %param.15) | copy-start | bytes 1540
  198.1 1.5 copy-start.5

commit v4 on v3

--- a/solution.py
+++ b/solution.py
@@ -52,12 +52,16 @@
     raw = jnp.concatenate([grad_owned[0], grad_replica[0]], axis=0).reshape(
         exp_dev + rep_dev, dp_count, shard_rows, columns
     )
-    grads = lax.dynamic_index_in_dim(raw, dp_index, axis=1, keepdims=False).astype(jnp.float32)
+    own_block = lax.dynamic_index_in_dim(raw, dp_index, axis=1, keepdims=False)
+    received = []
     for shift in range(1, dp_count):
         block = lax.dynamic_index_in_dim(raw, (dp_index + shift) % dp_count, axis=1, keepdims=False)
         got = lax.ppermute(
             block, "dp", [(i, (i + shift) % dp_count) for i in range(dp_count)]
         )
+        received.append(got)
+    grads = own_block.astype(jnp.float32)
+    for got in received:
         grads = grads + got.astype(jnp.float32)
     source_index = jnp.sum(
         jnp.where(
@@ -73,7 +77,8 @@
         split_axis=1,
         concat_axis=0,
         tiled=True,
-    ).reshape(ep_count * (exp_dev + rep_dev), piece_rows * columns)
+    )
+    grads_p = grads_p.reshape(ep_count * (exp_dev + rep_dev), piece_rows * columns)
 
     column = lax.iota(jnp.int32, ep_count * (exp_dev + rep_dev))
     device_of, within = column // (exp_dev + rep_dev), column % (exp_dev + rep_dev)

time: 282 us -> 282 us (level)
  no operation moved by 1% of the time
where the time goes in v4:
time: 282 us; the launch traced here: 281 us
  waiting for transfers between devices  127 us (45%)
  blocking collectives  72 us (26%)
  local copies, waits for them, and re-layouts  38.7 us (14%)
  starting transfers between devices  25.6 us (9%)
  other arithmetic  14.6 us (5%)
    all_to_all x1, blocking collectives, per_device_body(): lax.all_to_all(moved.reshape(3, ep_count, exp_dev, 1, piece_rows, columns...  72 us
    all_to_all x1, waiting for transfers between devices, per_device_body(): lax.all_to_all(state.reshape(3, exp_dev, ep_count, piece_rows, columns),...  51.1 us
    ppermute x3, waiting for transfers between devices, per_device_body(): lax.ppermute(block, 'dp', [(i, (i + shift) % dp_count) for i in range(dp_...  38.6 us
    all_to_all x1, waiting for transfers between devices, per_device_body(): lax.all_to_all(grads.reshape(exp_dev + rep_dev, ep_count, piece_rows, col...  37.3 us
    all_to_all x1, starting transfers between devices, per_device_body(): lax.all_to_all(grads.reshape(exp_dev + rep_dev, ep_count, piece_rows, col...  13.3 us
    unnamed x25, local copies, waits for them, and re-layouts  10.1 us
    concatenate x2, local copies, waits for them, and re-layouts, per_device_body(): jnp.concatenate([grad_owned[0], grad_replica[0]], axis=0)  6.67 us
    all_to_all x1, starting transfers between devices, per_device_body(): lax.all_to_all(state.reshape(3, exp_dev, ep_count, piece_rows, columns),...  6.64 us
  transfers between devices with their start and end apart: 5, of which 4 were waited for; matrix products, arithmetic and copies ran while one was open for 7% of the time, Pallas kernels for 0%

profile of v4, /device:TPU:1, one launch (start us, length us, event | category | flops | bytes accessed | tf_op | source)
XLA Modules:
  0.0 281.5 jit_solution(7166358018590053425)
XLA Ops:
  0.6 0.0 copy-start
  0.7 0.0 copy-start.4
  0.7 3.5 %copy.56 = bf16[2,4,896,128]{3,0,2,1:T(2,128)(2,1)S(1)} copy(bf16[2,4,896,128]{3,2,1,0:T(8,128)(2,1)} %bitcast.83) | data formatting | bytes 3670016 | tf_op jit(solution)/shard_map/concatenate | solution.py:52
  4.2 0.0 copy-done.4
  4.2 3.2 %copy.57 = bf16[2,4,896,128]{3,0,2,1:T(2,128)(2,1)} copy(bf16[2,4,896,128]{3,2,1,0:T(8,128)(2,1)S(1)} %bitcast.84) | data formatting | bytes 3670016 | tf_op jit(solution)/shard_map/concatenate | solution.py:52
  7.4 5.1 %fusion.12 = (bf16[4,896,128]{2,0,1:T(4,128)(2,1)}, bf16[4,896,128]{2,0,1:T(4,128)(2,1)}, bf16[4,896,128]{2,0,1:T(4,128)(2,1)}) fusion(s32[]{:T(128)S(6)} %select_n.205, bf16[2,4,896,128]{3,0,2,1:T(2,128)(2,1)} %copy.57, bf16[2,4,896,128]{3,0,2,1:T(2,128)(2,1)S(1)} %copy.56, s32[]{:T(128)S(6)} %select_n.207, s32[]{:T(128)S(6)} %select_n.209), kind=kLoop, calls=%fused_computation.34 | loop fusion | flops 5505024 | bytes 6422540 | tf_op jit(solution)/shard_map/jit(dynamic_index_in_dim)/squeeze | solution.py:58
  12.5 2.0 collective-permute-start
  14.5 2.5 collective-permute-start.1
  17.0 1.2 collective-permute-start.2
  18.2 15.7 %collective-permute-done = bf16[4,896,128]{2,0,1:T(4,128)(2,1)S(1)} collective-permute-done((bf16[4,896,128]{2,0,1:T(4,128)(2,1)}, bf16[4,896,128]{2,0,1:T(4,128)(2,1)S(1)}, u32[]{:S(2)}, u32[]{:S(2)}) %collective-permute-start) | collective-permute-done | bytes 917536 | tf_op jit(solution)/shard_map/ppermute | solution.py:59
  33.9 22.9 %collective-permute-done.1 = bf16[4,896,128]{2,0,1:T(4,128)(2,1)} collective-permute-done((bf16[4,896,128]{2,0,1:T(4,128)(2,1)}, bf16[4,896,128]{2,0,1:T(4,128)(2,1)}, u32[]{:S(2)}, u32[]{:S(2)}) %collective-permute-start.1) | collective-permute-done | bytes 917536 | tf_op jit(solution)/shard_map/ppermute | solution.py:59
  56.7 0.0 collective-permute-done.2
  56.7 4.5 %fusion.2 = f32[4,896,128]{2,0,1:T(4,128)} fusion(bf16[4,896,128]{2,0,1:T(4,128)(2,1)} %collective-permute-done.2, bf16[4,896,128]{2,0,1:T(4,128)(2,1)} %collective-permute-done.1, bf16[4,896,128]{2,0,1:T(4,128)(2,1)S(1)} %collective-permute-done, s32[]{:T(128)S(6)} %select_n.203, bf16[2,4,896,128]{3,0,2,1:T(2,128)(2,1)} %copy.57, ...), kind=kLoop, calls=%fused_computation.19 | loop fusion | flops 5046272 | bytes 8257540 | tf_op jit(solution)/shard_map/add | solution.py:65
  61.3 13.3 %all-to-all-start.1 = ((f32[4,64,14,128]{3,0,2,1:T(4,128)}), f32[4,64,14,128]{3,0,2,1:T(4,128)S(1)}, u32[]{:S(2)}, u32[]{:S(2)}) async-start(f32[4,64,14,128]{3,0,2,1:T(4,128)} %bitcast.76), calls=%async_computation.1 | async-start | bytes 3670016 | tf_op jit(solution)/shard_map/all_to_all | solution.py:74
  74.6 0.0 copy-done.6
  74.6 0.0 copy-start.7
  74.6 0.7 copy.49
  75.3 1.9 copy.50
  77.2 0.7 copy.51
  77.9 1.3 pad_maximum_fusion
  79.2 2.5 copy.52
  81.7 37.3 %all-to-all-done.1 = f32[4,64,14,128]{3,0,2,1:T(4,128)S(1)} async-done(((f32[4,64,14,128]{3,0,2,1:T(4,128)}), f32[4,64,14,128]{3,0,2,1:T(4,128)S(1)}, u32[]{:S(2)}, u32[]{:S(2)}) %all-to-all-start.1) | async-done | bytes 1835040 | tf_op jit(solution)/shard_map/all_to_all | solution.py:74
  119.0 1.3 copy-done.3
  120.2 6.6 %all-to-all-start = ((f32[3,2,64,14,128]{4,1,3,0,2:T(2,128)}), f32[3,2,64,14,128]{4,1,3,0,2:T(2,128)S(1)}, u32[]{:S(2)}, u32[]{:S(2)}) async-start(f32[3,2,64,14,128]{4,1,3,0,2:T(2,128)} %copy.52), calls=%async_computation | async-start | bytes 5505024 | tf_op jit(solution)/shard_map/all_to_all | solution.py:42
  126.9 0.0 copy-start.8
  126.9 0.0 copy-done.2
  127.0 1.9 gather_fusion.1
  128.9 1.9 gather_fusion.2
  130.8 1.9 gather_fusion.3
  132.7 0.2 select_reduce_fusion
  132.9 1.8 copy.58
  134.7 2.0 copy.72
  136.7 2.8 copy.59
  139.5 51.1 %all-to-all-done = f32[3,2,64,14,128]{4,1,3,0,2:T(2,128)S(1)} async-done(((f32[3,2,64,14,128]{4,1,3,0,2:T(2,128)}), f32[3,2,64,14,128]{4,1,3,0,2:T(2,128)S(1)}, u32[]{:S(2)}, u32[]{:S(2)}) %all-to-all-start) | async-done | bytes 2752544 | tf_op jit(solution)/shard_map/all_to_all | solution.py:42
  190.6 1.5 copy.53
  192.2 3.2 %copy.54 = f32[3,128,14,128]{3,2,1,0:T(8,128)} copy(f32[3,128,14,128]{3,1,2,0:T(8,128)S(1)} %bitcast.72) | data formatting | bytes 5505024 | tf_op jit(solution)/shard_map/reshape | solution.py:48
  195.4 2.6 gather_fusion
  198.1 0.0 copy-start.5
  198.1 1.0 fusion
  199.1 0.5 copy-done.5
  199.6 2.5 multiply_subtract_fusion
  202.1 2.4 pad_maximum_fusion.1
  204.6 0.9 copy.66
  205.5 72.0 %all_to_all.45 = f32[3,64,2,1,14,128]{5,2,4,0,3,1:T(2,128)S(1)} all-to-all(f32[3,64,2,1,14,128]{5,2,4,0,3,1:T(2,128)S(1)} %copy.66), channel_id=1, replica_groups=mesh['ep'=64,'dp'=4] {'ep'}, dimensions={1} | all-to-all | bytes 5505024 | tf_op jit(solution)/shard_map/all_to_all | solution.py:101
  277.6 0.9 fusion.34
  278.5 1.0 copy.63
  279.5 1.0 copy.64
  280.5 1.0 copy.65
  (18 shorter events, 0.1 us)
Async XLA Ops:
  0.6 128.2 %copy-start = (s32[128]{0:T(128)S(1)}, s32[128]{0:T(128)}, u32[]{:S(2)}) copy-start(s32[128]{0:T(128)} %param.16) | copy-start | bytes 1540
  0.7 3.5 %copy-start.4 = (bf16[1,2,3584,128]{3,2,1,0:T(8,128)(2,1)S(1)}, bf16[1,2,3584,128]{3,2,1,0:T(8,128)(2,1)}, u32[]{:S(2)}) copy-start(bf16[1,2,3584,128]{3,2,1,0:T(8,128)(2,1)} %param.13) | copy-start | bytes 5505028
  12.5 21.4 %collective-permute-start = (bf16[4,896,128]{2,0,1:T(4,128)(2,1)}, bf16[4,896,128]{2,0,1:T(4,128)(2,1)S(1)}, u32[]{:S(2)}, u32[]{:S(2)}) collective-permute-start(bf16[4,896,128]{2,0,1:T(4,128)(2,1)} %get-tuple-element.15), channel_id=1, source_target_pairs={{0,1},{1,2},{2,3},{3,0},{4,5},{5,6},{6,7},{7,4},{8,9},{9,10},{10,1... | collective-permute-start | bytes 2752520 | tf_op jit(solution)/shard_map/ppermute | solution.py:59
  14.5 42.2 %collective-permute-start.1 = (bf16[4,896,128]{2,0,1:T(4,128)(2,1)}, bf16[4,896,128]{2,0,1:T(4,128)(2,1)}, u32[]{:S(2)}, u32[]{:S(2)}) collective-permute-start(bf16[4,896,128]{2,0,1:T(4,128)(2,1)} %get-tuple-element.16), channel_id=1, source_target_pairs={{0,2},{1,3},{2,0},{3,1},{4,6},{5,7},{6,4},{7,5},{8,10},{9,11},{10,... | collective-permute-start | bytes 2752520 | tf_op jit(solution)/shard_map/ppermute | solution.py:59
  17.0 39.7 %collective-permute-start.2 = (bf16[4,896,128]{2,0,1:T(4,128)(2,1)}, bf16[4,896,128]{2,0,1:T(4,128)(2,1)}, u32[]{:S(2)}, u32[]{:S(2)}) collective-permute-start(bf16[4,896,128]{2,0,1:T(4,128)(2,1)} %get-tuple-element.17), channel_id=1, source_target_pairs={{0,3},{1,0},{2,1},{3,2},{4,7},{5,4},{6,5},{7,6},{8,11},{9,8},{10,9... | collective-permute-start | bytes 2752520 | tf_op jit(solution)/shard_map/ppermute | solution.py:59
  61.3 13.3 %copy-start.6 = (f32[2,896,128]{2,1,0:T(8,128)S(1)}, f32[2,896,128]{2,1,0:T(8,128)}, u32[]{:S(2)}) copy-start(f32[2,896,128]{2,1,0:T(8,128)} %param.9) | copy-start | bytes 2752516
  61.3 57.7 %all-to-all-start.1 = ((f32[4,64,14,128]{3,0,2,1:T(4,128)}), f32[4,64,14,128]{3,0,2,1:T(4,128)S(1)}, u32[]{:S(2)}, u32[]{:S(2)}) async-start(f32[4,64,14,128]{3,0,2,1:T(4,128)} %bitcast.76), calls=%async_computation.1 | async-start | bytes 3670016 | tf_op jit(solution)/shard_map/all_to_all | solution.py:74
  74.6 2.6 copy-start.7
  81.7 45.2 %copy-start.2 = (s32[128]{0:T(128)S(1)}, s32[128]{0:T(128)}, u32[]{:S(2)}) copy-start(s32[128]{0:T(128)} %param.14) | copy-start | bytes 1540
  81.7 49.1 %copy-start.1 = (s32[64]{0:T(128)S(1)}, s32[64]{0:T(128)}, u32[]{:S(2)}) copy-start(s32[64]{0:T(128)} %param.17) | copy-start | bytes 772
  119.0 1.3 copy-start.3
  120.2 70.4 %all-to-all-start = ((f32[3,2,64,14,128]{4,1,3,0,2:T(2,128)}), f32[3,2,64,14,128]{4,1,3,0,2:T(2,128)S(1)}, u32[]{:S(2)}, u32[]{:S(2)}) async-start(f32[3,2,64,14,128]{4,1,3,0,2:T(2,128)} %copy.52), calls=%async_computation | async-start | bytes 5505024 | tf_op jit(solution)/shard_map/all_to_all | solution.py:42
  126.9 5.8 %copy-start.8 = (s32[128]{0:T(128)S(1)}, s32[128]{0:T(128)}, u32[]{:S(2)}) copy-start(s32[128]{0:T(128)} %param.15) | copy-start | bytes 1540
  198.1 1.5 copy-start.5

commit v5 on v4

--- a/solution.py
+++ b/solution.py
@@ -38,14 +38,13 @@
     experts = exp_dev * ep_count
     replica_slots = rep_dev * ep_count
 
-    state = jnp.stack([master_weight, first_moment, second_moment])
+    state = jnp.stack([master_weight, first_moment, second_moment]).reshape(
+        3, exp_dev, ep_count, piece_rows, columns
+    )
     state_p = lax.all_to_all(
-        state.reshape(3, exp_dev, ep_count, piece_rows, columns),
-        "ep",
-        split_axis=2,
-        concat_axis=1,
-        tiled=True,
-    ).reshape(3, experts, piece_rows, columns)
+        state.transpose(2, 0, 1, 3, 4), "ep", split_axis=0, concat_axis=0, tiled=True
+    )
+    state_p = state_p.transpose(1, 0, 2, 3, 4).reshape(3, experts, piece_rows, columns)
 
     dp_count = lax.axis_size("dp")
     dp_index = lax.axis_index("dp")
@@ -72,9 +71,9 @@
     state_new = jnp.take(state_p, source_index, axis=1)
 
     grads_p = lax.all_to_all(
-        grads.reshape(exp_dev + rep_dev, ep_count, piece_rows, columns),
+        grads.reshape(exp_dev + rep_dev, ep_count, piece_rows, columns).transpose(1, 0, 2, 3),
         "ep",
-        split_axis=1,
+        split_axis=0,
         concat_axis=0,
         tiled=True,
     )
@@ -99,12 +98,13 @@
     ).reshape(experts, piece_rows, columns)
     moved = jnp.stack(adam_update(state_new[0], state_new[1], state_new[2], gradient))
     back = lax.all_to_all(
-        moved.reshape(3, ep_count, exp_dev, 1, piece_rows, columns),
+        moved.reshape(3, ep_count, exp_dev, piece_rows, columns).transpose(1, 0, 2, 3, 4),
         "ep",
-        split_axis=1,
-        concat_axis=3,
+        split_axis=0,
+        concat_axis=0,
         tiled=True,
-    ).reshape(3, exp_dev, shard_rows, columns)
+    )
+    back = back.transpose(1, 2, 0, 3, 4).reshape(3, exp_dev, shard_rows, columns)
     return (back[0], back[1], back[2])
 
 

time: 282 us -> 280 us (level)
    transpose x0 -> x2, local copies, waits for them, and re-layouts: none -> 4.02 us  [the longest x1 2.49 us: per_device_body(): state.transpose(2, 0, 1, 3, 4)]
    another operation x2 -> x0, other arithmetic: 3.71 us -> none  [the longest x1 2.45 us: per_device_body(): jnp.stack(adam_update(state_new[0], state_new[1], state_new[2], gradient))]
    another operation x2 -> x0, local copies, waits for them, and re-layouts: 3.43 us -> none  [the longest x1 2.49 us: per_device_body(): state = jnp.stack([master_weight, first_moment, second_moment])]
where the time goes in v5:
time: 280 us; the launch traced here: 279 us
  waiting for transfers between devices  127 us (45%)
  blocking collectives  72 us (26%)
  local copies, waits for them, and re-layouts  37.7 us (13%)
  starting transfers between devices  25.6 us (9%)
  other arithmetic  13.5 us (5%)
    all_to_all x1, blocking collectives, per_device_body(): lax.all_to_all(moved.reshape(3, ep_count, exp_dev, piece_rows, columns).t...  72 us
    all_to_all x1, waiting for transfers between devices, per_device_body(): lax.all_to_all(state.transpose(2, 0, 1, 3, 4), 'ep', split_axis=0, concat...  51.1 us
    ppermute x3, waiting for transfers between devices, per_device_body(): lax.ppermute(block, 'dp', [(i, (i + shift) % dp_count) for i in range(dp_...  38.6 us
    all_to_all x1, waiting for transfers between devices, per_device_body(): lax.all_to_all(grads.reshape(exp_dev + rep_dev, ep_count, piece_rows, col...  37.3 us
    all_to_all x1, starting transfers between devices, per_device_body(): lax.all_to_all(grads.reshape(exp_dev + rep_dev, ep_count, piece_rows, col...  13.3 us
    unnamed x25, local copies, waits for them, and re-layouts  10.1 us
    concatenate x2, local copies, waits for them, and re-layouts, per_device_body(): jnp.concatenate([grad_owned[0], grad_replica[0]], axis=0)  6.67 us
    all_to_all x1, starting transfers between devices, per_device_body(): lax.all_to_all(state.transpose(2, 0, 1, 3, 4), 'ep', split_axis=0, concat...  6.64 us
  transfers between devices with their start and end apart: 5, of which 4 were waited for; matrix products, arithmetic and copies ran while one was open for 7% of the time, Pallas kernels for 0%

profile of v5, /device:TPU:1, one launch (start us, length us, event | category | flops | bytes accessed | tf_op | source)
XLA Modules:
  0.0 279.3 jit_solution(6664827326541697474)
XLA Ops:
  0.6 0.0 copy-start
  0.7 0.0 copy-start.4
  0.7 3.5 %copy.56 = bf16[2,4,896,128]{3,0,2,1:T(2,128)(2,1)S(1)} copy(bf16[2,4,896,128]{3,2,1,0:T(8,128)(2,1)} %bitcast.80) | data formatting | bytes 3670016 | tf_op jit(solution)/shard_map/concatenate | solution.py:51
  4.2 0.0 copy-done.4
  4.2 3.2 %copy.57 = bf16[2,4,896,128]{3,0,2,1:T(2,128)(2,1)} copy(bf16[2,4,896,128]{3,2,1,0:T(8,128)(2,1)S(1)} %bitcast.81) | data formatting | bytes 3670016 | tf_op jit(solution)/shard_map/concatenate | solution.py:51
  7.4 5.1 %fusion.12 = (bf16[4,896,128]{2,0,1:T(4,128)(2,1)}, bf16[4,896,128]{2,0,1:T(4,128)(2,1)}, bf16[4,896,128]{2,0,1:T(4,128)(2,1)}) fusion(s32[]{:T(128)S(6)} %select_n.205, bf16[2,4,896,128]{3,0,2,1:T(2,128)(2,1)} %copy.57, bf16[2,4,896,128]{3,0,2,1:T(2,128)(2,1)S(1)} %copy.56, s32[]{:T(128)S(6)} %select_n.207, s32[]{:T(128)S(6)} %select_n.209), kind=kLoop, calls=%fused_computation.35 | loop fusion | flops 5505024 | bytes 6422540 | tf_op jit(solution)/shard_map/jit(dynamic_index_in_dim)/squeeze | solution.py:57
  12.5 2.0 collective-permute-start
  14.5 2.5 collective-permute-start.1
  17.0 1.2 collective-permute-start.2
  18.2 15.7 %collective-permute-done = bf16[4,896,128]{2,0,1:T(4,128)(2,1)S(1)} collective-permute-done((bf16[4,896,128]{2,0,1:T(4,128)(2,1)}, bf16[4,896,128]{2,0,1:T(4,128)(2,1)S(1)}, u32[]{:S(2)}, u32[]{:S(2)}) %collective-permute-start) | collective-permute-done | bytes 917536 | tf_op jit(solution)/shard_map/ppermute | solution.py:58
  33.9 22.9 %collective-permute-done.1 = bf16[4,896,128]{2,0,1:T(4,128)(2,1)} collective-permute-done((bf16[4,896,128]{2,0,1:T(4,128)(2,1)}, bf16[4,896,128]{2,0,1:T(4,128)(2,1)}, u32[]{:S(2)}, u32[]{:S(2)}) %collective-permute-start.1) | collective-permute-done | bytes 917536 | tf_op jit(solution)/shard_map/ppermute | solution.py:58
  56.7 0.0 collective-permute-done.2
  56.7 4.5 %fusion.2 = f32[4,896,128]{2,0,1:T(4,128)} fusion(bf16[4,896,128]{2,0,1:T(4,128)(2,1)} %collective-permute-done.2, bf16[4,896,128]{2,0,1:T(4,128)(2,1)} %collective-permute-done.1, bf16[4,896,128]{2,0,1:T(4,128)(2,1)S(1)} %collective-permute-done, s32[]{:T(128)S(6)} %select_n.203, bf16[2,4,896,128]{3,0,2,1:T(2,128)(2,1)} %copy.57, ...), kind=kLoop, calls=%fused_computation.20 | loop fusion | flops 5046272 | bytes 8257540 | tf_op jit(solution)/shard_map/add | solution.py:64
  61.3 13.3 %all-to-all-start.1 = ((f32[64,4,14,128]{3,1,2,0:T(4,128)}), f32[64,4,14,128]{3,1,2,0:T(4,128)S(1)}, u32[]{:S(2)}, u32[]{:S(2)}) async-start(f32[64,4,14,128]{3,1,2,0:T(4,128)} %bitcast.73), calls=%async_computation.1 | async-start | bytes 3670016 | tf_op jit(solution)/shard_map/all_to_all | solution.py:73
  74.6 0.0 copy-done.6
  74.6 0.0 copy-start.7
  74.6 0.7 copy.49
  75.3 1.9 copy.50
  77.2 0.0 copy-done.7
  77.2 0.7 copy.51
  77.9 1.3 maximum_bitcast_fusion
  79.2 2.5 copy.52
  81.7 37.3 %all-to-all-done.1 = f32[64,4,14,128]{3,1,2,0:T(4,128)S(1)} async-done(((f32[64,4,14,128]{3,1,2,0:T(4,128)}), f32[64,4,14,128]{3,1,2,0:T(4,128)S(1)}, u32[]{:S(2)}, u32[]{:S(2)}) %all-to-all-start.1) | async-done | bytes 1835040 | tf_op jit(solution)/shard_map/all_to_all | solution.py:73
  119.0 1.3 copy-done.3
  120.2 6.6 %all-to-all-start = ((f32[64,3,2,14,128]{4,2,3,1,0:T(2,128)}), f32[64,3,2,14,128]{4,2,3,1,0:T(2,128)S(1)}, u32[]{:S(2)}, u32[]{:S(2)}) async-start(f32[64,3,2,14,128]{4,2,3,1,0:T(2,128)} %copy.52), calls=%async_computation | async-start | bytes 5505024 | tf_op jit(solution)/shard_map/all_to_all | solution.py:44
  126.9 0.0 copy-start.8
  126.9 0.0 copy-done.2
  127.0 1.9 gather_fusion.1
  128.9 1.9 gather_fusion.2
  130.8 1.9 gather_fusion.3
  132.7 0.2 select_reduce_fusion
  132.9 1.8 copy.58
  134.7 2.0 copy.73
  136.7 2.8 copy.59
  139.5 51.1 %all-to-all-done = f32[64,3,2,14,128]{4,2,3,1,0:T(2,128)S(1)} async-done(((f32[64,3,2,14,128]{4,2,3,1,0:T(2,128)}), f32[64,3,2,14,128]{4,2,3,1,0:T(2,128)S(1)}, u32[]{:S(2)}, u32[]{:S(2)}) %all-to-all-start) | async-done | bytes 2752544 | tf_op jit(solution)/shard_map/all_to_all | solution.py:44
  190.6 1.5 copy.53
  192.2 3.2 %copy.54 = f32[3,128,14,128]{3,2,1,0:T(8,128)} copy(f32[3,128,14,128]{3,1,2,0:T(8,128)S(1)} %bitcast.70) | data formatting | bytes 5505024 | tf_op jit(solution)/shard_map/reshape | solution.py:47
  195.4 2.6 gather_fusion
  198.1 0.0 copy-start.5
  198.1 1.0 fusion
  199.1 0.5 copy-done.5
  199.6 2.5 multiply_subtract_fusion
  202.1 1.3 copy_bitcast_fusion
  203.4 72.0 %all_to_all.15 = f32[64,3,2,14,128]{4,2,3,1,0:T(2,128)S(1)} all-to-all(f32[64,3,2,14,128]{4,2,3,1,0:T(2,128)S(1)} %copy_bitcast_fusion), channel_id=1, replica_groups=mesh['ep'=64,'dp'=4] {'ep'}, dimensions={0} | all-to-all | bytes 5505024 | tf_op jit(solution)/shard_map/all_to_all | solution.py:100
  275.5 0.9 fusion.34
  276.4 1.0 copy.63
  277.4 1.0 copy.64
  278.4 1.0 copy.65
  (17 shorter events, 0.1 us)
Async XLA Ops:
  0.6 128.2 %copy-start = (s32[128]{0:T(128)S(1)}, s32[128]{0:T(128)}, u32[]{:S(2)}) copy-start(s32[128]{0:T(128)} %param.16) | copy-start | bytes 1540
  0.7 3.5 %copy-start.4 = (bf16[1,2,3584,128]{3,2,1,0:T(8,128)(2,1)S(1)}, bf16[1,2,3584,128]{3,2,1,0:T(8,128)(2,1)}, u32[]{:S(2)}) copy-start(bf16[1,2,3584,128]{3,2,1,0:T(8,128)(2,1)} %param.13) | copy-start | bytes 5505028
  12.5 21.4 %collective-permute-start = (bf16[4,896,128]{2,0,1:T(4,128)(2,1)}, bf16[4,896,128]{2,0,1:T(4,128)(2,1)S(1)}, u32[]{:S(2)}, u32[]{:S(2)}) collective-permute-start(bf16[4,896,128]{2,0,1:T(4,128)(2,1)} %get-tuple-element.15), channel_id=1, source_target_pairs={{0,1},{1,2},{2,3},{3,0},{4,5},{5,6},{6,7},{7,4},{8,9},{9,10},{10,1... | collective-permute-start | bytes 2752520 | tf_op jit(solution)/shard_map/ppermute | solution.py:58
  14.5 42.2 %collective-permute-start.1 = (bf16[4,896,128]{2,0,1:T(4,128)(2,1)}, bf16[4,896,128]{2,0,1:T(4,128)(2,1)}, u32[]{:S(2)}, u32[]{:S(2)}) collective-permute-start(bf16[4,896,128]{2,0,1:T(4,128)(2,1)} %get-tuple-element.16), channel_id=1, source_target_pairs={{0,2},{1,3},{2,0},{3,1},{4,6},{5,7},{6,4},{7,5},{8,10},{9,11},{10,... | collective-permute-start | bytes 2752520 | tf_op jit(solution)/shard_map/ppermute | solution.py:58
  17.0 39.7 %collective-permute-start.2 = (bf16[4,896,128]{2,0,1:T(4,128)(2,1)}, bf16[4,896,128]{2,0,1:T(4,128)(2,1)}, u32[]{:S(2)}, u32[]{:S(2)}) collective-permute-start(bf16[4,896,128]{2,0,1:T(4,128)(2,1)} %get-tuple-element.17), channel_id=1, source_target_pairs={{0,3},{1,0},{2,1},{3,2},{4,7},{5,4},{6,5},{7,6},{8,11},{9,8},{10,9... | collective-permute-start | bytes 2752520 | tf_op jit(solution)/shard_map/ppermute | solution.py:58
  61.3 13.3 %copy-start.6 = (f32[2,896,128]{2,1,0:T(8,128)S(1)}, f32[2,896,128]{2,1,0:T(8,128)}, u32[]{:S(2)}) copy-start(f32[2,896,128]{2,1,0:T(8,128)} %param.9) | copy-start | bytes 2752516
  61.3 57.7 %all-to-all-start.1 = ((f32[64,4,14,128]{3,1,2,0:T(4,128)}), f32[64,4,14,128]{3,1,2,0:T(4,128)S(1)}, u32[]{:S(2)}, u32[]{:S(2)}) async-start(f32[64,4,14,128]{3,1,2,0:T(4,128)} %bitcast.73), calls=%async_computation.1 | async-start | bytes 3670016 | tf_op jit(solution)/shard_map/all_to_all | solution.py:73
  74.6 2.6 copy-start.7
  81.7 45.2 %copy-start.2 = (s32[128]{0:T(128)S(1)}, s32[128]{0:T(128)}, u32[]{:S(2)}) copy-start(s32[128]{0:T(128)} %param.14) | copy-start | bytes 1540
  81.7 49.1 %copy-start.1 = (s32[64]{0:T(128)S(1)}, s32[64]{0:T(128)}, u32[]{:S(2)}) copy-start(s32[64]{0:T(128)} %param.17) | copy-start | bytes 772
  119.0 1.3 copy-start.3
  120.2 70.4 %all-to-all-start = ((f32[64,3,2,14,128]{4,2,3,1,0:T(2,128)}), f32[64,3,2,14,128]{4,2,3,1,0:T(2,128)S(1)}, u32[]{:S(2)}, u32[]{:S(2)}) async-start(f32[64,3,2,14,128]{4,2,3,1,0:T(2,128)} %copy.52), calls=%async_computation | async-start | bytes 5505024 | tf_op jit(solution)/shard_map/all_to_all | solution.py:44
  126.9 5.8 %copy-start.8 = (s32[128]{0:T(128)S(1)}, s32[128]{0:T(128)}, u32[]{:S(2)}) copy-start(s32[128]{0:T(128)} %param.15) | copy-start | bytes 1540
  198.1 1.5 copy-start.5

commit v6 on v5

--- a/solution.py
+++ b/solution.py
@@ -48,20 +48,27 @@
 
     dp_count = lax.axis_size("dp")
     dp_index = lax.axis_index("dp")
-    raw = jnp.concatenate([grad_owned[0], grad_replica[0]], axis=0).reshape(
-        exp_dev + rep_dev, dp_count, shard_rows, columns
-    )
-    own_block = lax.dynamic_index_in_dim(raw, dp_index, axis=1, keepdims=False)
+    def block_of(array, index):
+        return lax.dynamic_slice_in_dim(array, index * shard_rows, shard_rows, axis=1)
+
+    own_block = [block_of(grad_owned[0], dp_index), block_of(grad_replica[0], dp_index)]
     received = []
     for shift in range(1, dp_count):
-        block = lax.dynamic_index_in_dim(raw, (dp_index + shift) % dp_count, axis=1, keepdims=False)
-        got = lax.ppermute(
-            block, "dp", [(i, (i + shift) % dp_count) for i in range(dp_count)]
+        target = (dp_index + shift) % dp_count
+        received.append(
+            [
+                lax.ppermute(
+                    block_of(array, target),
+                    "dp",
+                    [(i, (i + shift) % dp_count) for i in range(dp_count)],
+                )
+                for array in (grad_owned[0], grad_replica[0])
+            ]
         )
-        received.append(got)
-    grads = own_block.astype(jnp.float32)
+    sums = [part.astype(jnp.float32) for part in own_block]
     for got in received:
-        grads = grads + got.astype(jnp.float32)
+        sums = [total + part.astype(jnp.float32) for total, part in zip(sums, got)]
+    grads = jnp.concatenate(sums, axis=0)
     source_index = jnp.sum(
         jnp.where(
             new_experts[:, None] == old_experts[None, :], lax.iota(jnp.int32, experts)[None, :], 0

time: 280 us -> 270 us (0.964)
  waiting for transfers between devices: 127 us -> 118 us
  other arithmetic: 13.5 us -> 7.07 us
  starting transfers between devices: 25.6 us -> 31.8 us
    ppermute x3 -> x6, waiting for transfers between devices: 38.6 us -> 29.8 us  [per_device_body(): lax.ppermute(block_of(array, target), 'dp', [(i, (i + shift) % dp_count)...]
    ppermute x3 -> x6, starting transfers between devices: 5.63 us -> 11.7 us  [per_device_body(): lax.ppermute(block_of(array, target), 'dp', [(i, (i + shift) % dp_count)...]
    squeeze x1 -> x0, other arithmetic: 5.14 us -> none  [per_device_body(): lax.dynamic_index_in_dim(raw, (dp_index + shift) % dp_count, axis=1, keep...]
    concatenate x2 -> x1, local copies, waits for them, and re-layouts: 6.67 us -> 2.43 us  [per_device_body(): grads = jnp.concatenate(sums, axis=0)]
    dynamic_slice x0 -> x2, local copies, waits for them, and re-layouts: none -> 3.31 us  [block_of(): lax.dynamic_slice_in_dim(array, index * shard_rows, shard_rows, axis=1)]
  transfers between devices with their start and end apart: 5 -> 8, of which waited for: 4 -> 7; matrix products, arithmetic and copies ran while one was open for 7% -> 8% of each run, Pallas kernels for 0% -> 0%
where the time goes in v6:
time: 270 us; the launch traced here: 269 us
  waiting for transfers between devices  118 us (44%)
  blocking collectives  72 us (27%)
  local copies, waits for them, and re-layouts  36.7 us (14%)
  starting transfers between devices  31.8 us (12%)
  other arithmetic  7.07 us (3%)
    all_to_all x1, blocking collectives, per_device_body(): lax.all_to_all(moved.reshape(3, ep_count, exp_dev, piece_rows, columns).t...  72 us
    all_to_all x1, waiting for transfers between devices, per_device_body(): lax.all_to_all(state.transpose(2, 0, 1, 3, 4), 'ep', split_axis=0, concat...  51.2 us
    all_to_all x1, waiting for transfers between devices, per_device_body(): lax.all_to_all(grads.reshape(exp_dev + rep_dev, ep_count, piece_rows, col...  37.3 us
    ppermute x6, waiting for transfers between devices, per_device_body(): lax.ppermute(block_of(array, target), 'dp', [(i, (i + shift) % dp_count)...  29.8 us
    all_to_all x1, starting transfers between devices, per_device_body(): lax.all_to_all(grads.reshape(exp_dev + rep_dev, ep_count, piece_rows, col...  13.3 us
    ppermute x6, starting transfers between devices, per_device_body(): lax.ppermute(block_of(array, target), 'dp', [(i, (i + shift) % dp_count)...  11.7 us
    unnamed x25, local copies, waits for them, and re-layouts  10 us
    all_to_all x1, starting transfers between devices, per_device_body(): lax.all_to_all(state.transpose(2, 0, 1, 3, 4), 'ep', split_axis=0, concat...  6.82 us
  transfers between devices with their start and end apart: 8, of which 7 were waited for; matrix products, arithmetic and copies ran while one was open for 8% of the time, Pallas kernels for 0%

profile of v6, /device:TPU:1, one launch (start us, length us, event | category | flops | bytes accessed | tf_op | source)
XLA Modules:
  0.0 269.4 jit_solution(12539695419791701694)
XLA Ops:
  0.6 0.0 copy-start
  0.7 2.3 dynamic-slice_bitcast_fusion.5
  3.0 2.0 collective-permute-start
  5.0 1.3 collective-permute-start.2
  6.3 1.7 collective-permute-start.1
  8.0 1.0 dynamic-slice_bitcast_fusion.2
  9.0 0.3 collective-permute-start.3
  9.4 2.4 collective-permute-start.5
  11.7 2.6 collective-permute-done
  14.3 4.0 %collective-permute-start.4 = (bf16[2,896,128]{2,1,0:T(8,128)(2,1)S(1)}, bf16[2,896,128]{2,1,0:T(8,128)(2,1)}, u32[]{:S(2)}, u32[]{:S(2)}) collective-permute-start(bf16[2,896,128]{2,1,0:T(8,128)(2,1)S(1)} %get-tuple-element.23), channel_id=1, source_target_pairs={{0,2},{1,3},{2,0},{3,1},{4,6},{5,7},{6,4},{7,5},{8,10},{9,11},{10,... | collective-permute-start | bytes 1376264 | tf_op jit(solution)/shard_map/ppermute | solution.py:60
  18.3 9.1 %collective-permute-done.1 = bf16[2,896,128]{2,1,0:T(8,128)(2,1)} collective-permute-done((bf16[2,896,128]{2,1,0:T(8,128)(2,1)S(1)}, bf16[2,896,128]{2,1,0:T(8,128)(2,1)}, u32[]{:S(2)}, u32[]{:S(2)}) %collective-permute-start.1) | collective-permute-done | bytes 458784 | tf_op jit(solution)/shard_map/ppermute | solution.py:60
  27.4 1.6 fusion.8
  29.0 5.1 %collective-permute-done.3 = bf16[2,896,128]{2,1,0:T(8,128)(2,1)} collective-permute-done((bf16[2,896,128]{2,1,0:T(8,128)(2,1)}, bf16[2,896,128]{2,1,0:T(8,128)(2,1)}, u32[]{:S(2)}, u32[]{:S(2)}) %collective-permute-start.3) | collective-permute-done | bytes 458784 | tf_op jit(solution)/shard_map/ppermute | solution.py:60
  34.1 1.9 collective-permute-done.5
  35.9 11.1 %collective-permute-done.4 = bf16[2,896,128]{2,1,0:T(8,128)(2,1)} collective-permute-done((bf16[2,896,128]{2,1,0:T(8,128)(2,1)S(1)}, bf16[2,896,128]{2,1,0:T(8,128)(2,1)}, u32[]{:S(2)}, u32[]{:S(2)}) %collective-permute-start.4) | collective-permute-done | bytes 458784 | tf_op jit(solution)/shard_map/ppermute | solution.py:60
  47.1 1.6 fusion.6
  48.6 0.1 pad_maximum_fusion.1
  48.7 2.4 copy.54
  51.2 13.3 %all-to-all-start.1 = ((f32[64,4,14,128]{3,1,2,0:T(4,128)}), f32[64,4,14,128]{3,1,2,0:T(4,128)S(1)}, u32[]{:S(2)}, u32[]{:S(2)}) async-start(f32[64,4,14,128]{3,1,2,0:T(4,128)} %bitcast.24), calls=%async_computation.1 | async-start | bytes 3670016 | tf_op jit(solution)/shard_map/all_to_all | solution.py:80
  64.5 0.7 copy.47
  65.2 1.9 copy.48
  67.1 0.7 copy.49
  67.9 1.3 maximum_bitcast_fusion
  69.1 2.5 copy.50
  71.6 37.3 %all-to-all-done.1 = f32[64,4,14,128]{3,1,2,0:T(4,128)S(1)} async-done(((f32[64,4,14,128]{3,1,2,0:T(4,128)}), f32[64,4,14,128]{3,1,2,0:T(4,128)S(1)}, u32[]{:S(2)}, u32[]{:S(2)}) %all-to-all-start.1) | async-done | bytes 1835040 | tf_op jit(solution)/shard_map/all_to_all | solution.py:80
  108.9 1.2 copy-done.3
  110.2 6.8 %all-to-all-start = ((f32[64,3,2,14,128]{4,2,3,1,0:T(2,128)}), f32[64,3,2,14,128]{4,2,3,1,0:T(2,128)S(1)}, u32[]{:S(2)}, u32[]{:S(2)}) async-start(f32[64,3,2,14,128]{4,2,3,1,0:T(2,128)} %copy.50), calls=%async_computation | async-start | bytes 5505024 | tf_op jit(solution)/shard_map/all_to_all | solution.py:44
  117.0 0.0 copy-start.8
  117.0 1.9 gather_fusion.1
  118.9 1.9 gather_fusion.3
  120.9 1.9 gather_fusion.2
  122.7 0.2 select_reduce_fusion
  123.0 1.8 copy.55
  124.8 2.0 copy.70
  126.8 2.7 %copy.56 = f32[1792,256]{1,0:T(8,128)} copy(f32[1792,256]{0,1:T(8,128)} %bitcast.79) | data formatting | bytes 3670016 | tf_op jit(solution)/shard_map/dot_general | solution.py:100
  129.5 51.2 %all-to-all-done = f32[64,3,2,14,128]{4,2,3,1,0:T(2,128)S(1)} async-done(((f32[64,3,2,14,128]{4,2,3,1,0:T(2,128)}), f32[64,3,2,14,128]{4,2,3,1,0:T(2,128)S(1)}, u32[]{:S(2)}, u32[]{:S(2)}) %all-to-all-start) | async-done | bytes 2752544 | tf_op jit(solution)/shard_map/all_to_all | solution.py:44
  180.7 1.5 copy.51
  182.3 3.2 %copy.52 = f32[3,128,14,128]{3,2,1,0:T(8,128)} copy(f32[3,128,14,128]{3,1,2,0:T(8,128)S(1)} %bitcast.77) | data formatting | bytes 5505024 | tf_op jit(solution)/shard_map/reshape | solution.py:47
  185.5 2.6 gather_fusion
  188.2 1.0 fusion
  189.2 0.5 copy-done.4
  189.7 2.5 multiply_subtract_fusion
  192.2 1.3 copy_bitcast_fusion
  193.5 72.0 %all_to_all.15 = f32[64,3,2,14,128]{4,2,3,1,0:T(2,128)S(1)} all-to-all(f32[64,3,2,14,128]{4,2,3,1,0:T(2,128)S(1)} %copy_bitcast_fusion), channel_id=1, replica_groups=mesh['ep'=64,'dp'=4] {'ep'}, dimensions={0} | all-to-all | bytes 5505024 | tf_op jit(solution)/shard_map/all_to_all | solution.py:107
  265.5 0.9 fusion.29
  266.5 1.0 copy.62
  267.5 1.0 copy.61
  268.5 1.0 copy.60
  (25 shorter events, 0.1 us)
Async XLA Ops:
  0.6 118.3 %copy-start = (s32[64]{0:T(128)S(1)}, s32[64]{0:T(128)}, u32[]{:S(2)}) copy-start(s32[64]{0:T(128)} %param.17) | copy-start | bytes 772
  0.6 7.4 %copy-start.5 = (bf16[1,2,3584,128]{3,2,1,0:T(8,128)(2,1)S(1)}, bf16[1,2,3584,128]{3,2,1,0:T(8,128)(2,1)}, u32[]{:S(2)}) copy-start(bf16[1,2,3584,128]{3,2,1,0:T(8,128)(2,1)} %param.13) | copy-start | bytes 5505028
  3.0 11.3 %collective-permute-start = (bf16[2,896,128]{2,1,0:T(8,128)(2,1)S(1)}, bf16[2,896,128]{2,1,0:T(8,128)(2,1)S(1)}, u32[]{:S(2)}, u32[]{:S(2)}) collective-permute-start(bf16[2,896,128]{2,1,0:T(8,128)(2,1)S(1)} %get-tuple-element.18), channel_id=1, source_target_pairs={{0,1},{1,2},{2,3},{3,0},{4,5},{5,6},{6,7},{7,4},{8,9},{9,10},{10,1... | collective-permute-start | bytes 1376264 | tf_op jit(solution)/shard_map/ppermute | solution.py:60
  5.0 13.3 %collective-permute-start.2 = (bf16[2,896,128]{2,1,0:T(8,128)(2,1)}, bf16[2,896,128]{2,1,0:T(8,128)(2,1)}, u32[]{:S(2)}, u32[]{:S(2)}) collective-permute-start(bf16[2,896,128]{2,1,0:T(8,128)(2,1)} %get-tuple-element.19), channel_id=1, source_target_pairs={{0,3},{1,0},{2,1},{3,2},{4,7},{5,4},{6,5},{7,6},{8,11},{9,8},{10,9... | collective-permute-start | bytes 1376264 | tf_op jit(solution)/shard_map/ppermute | solution.py:60
  6.3 21.1 %collective-permute-start.1 = (bf16[2,896,128]{2,1,0:T(8,128)(2,1)S(1)}, bf16[2,896,128]{2,1,0:T(8,128)(2,1)}, u32[]{:S(2)}, u32[]{:S(2)}) collective-permute-start(bf16[2,896,128]{2,1,0:T(8,128)(2,1)S(1)} %get-tuple-element.20), channel_id=1, source_target_pairs={{0,2},{1,3},{2,0},{3,1},{4,6},{5,7},{6,4},{7,5},{8,10},{9,11},{10,... | collective-permute-start | bytes 1376264 | tf_op jit(solution)/shard_map/ppermute | solution.py:60
  9.0 25.0 %collective-permute-start.3 = (bf16[2,896,128]{2,1,0:T(8,128)(2,1)}, bf16[2,896,128]{2,1,0:T(8,128)(2,1)}, u32[]{:S(2)}, u32[]{:S(2)}) collective-permute-start(bf16[2,896,128]{2,1,0:T(8,128)(2,1)} %get-tuple-element.21), channel_id=1, source_target_pairs={{0,1},{1,2},{2,3},{3,0},{4,5},{5,6},{6,7},{7,4},{8,9},{9,10},{10,1... | collective-permute-start | bytes 1376264 | tf_op jit(solution)/shard_map/ppermute | solution.py:60
  9.4 26.6 %collective-permute-start.5 = (bf16[2,896,128]{2,1,0:T(8,128)(2,1)}, bf16[2,896,128]{2,1,0:T(8,128)(2,1)}, u32[]{:S(2)}, u32[]{:S(2)}) collective-permute-start(bf16[2,896,128]{2,1,0:T(8,128)(2,1)} %get-tuple-element.22), channel_id=1, source_target_pairs={{0,3},{1,0},{2,1},{3,2},{4,7},{5,4},{6,5},{7,6},{8,11},{9,8},{10,9... | collective-permute-start | bytes 1376264 | tf_op jit(solution)/shard_map/ppermute | solution.py:60
  14.3 32.7 %collective-permute-start.4 = (bf16[2,896,128]{2,1,0:T(8,128)(2,1)S(1)}, bf16[2,896,128]{2,1,0:T(8,128)(2,1)}, u32[]{:S(2)}, u32[]{:S(2)}) collective-permute-start(bf16[2,896,128]{2,1,0:T(8,128)(2,1)S(1)} %get-tuple-element.23), channel_id=1, source_target_pairs={{0,2},{1,3},{2,0},{3,1},{4,6},{5,7},{6,4},{7,5},{8,10},{9,11},{10,... | collective-permute-start | bytes 1376264 | tf_op jit(solution)/shard_map/ppermute | solution.py:60
  51.2 13.3 %copy-start.6 = (f32[2,896,128]{2,1,0:T(8,128)S(1)}, f32[2,896,128]{2,1,0:T(8,128)}, u32[]{:S(2)}) copy-start(f32[2,896,128]{2,1,0:T(8,128)} %param.9) | copy-start | bytes 2752516
  51.2 57.7 %all-to-all-start.1 = ((f32[64,4,14,128]{3,1,2,0:T(4,128)}), f32[64,4,14,128]{3,1,2,0:T(4,128)S(1)}, u32[]{:S(2)}, u32[]{:S(2)}) async-start(f32[64,4,14,128]{3,1,2,0:T(4,128)} %bitcast.24), calls=%async_computation.1 | async-start | bytes 3670016 | tf_op jit(solution)/shard_map/all_to_all | solution.py:80
  64.5 2.6 copy-start.7
  71.6 45.4 %copy-start.2 = (s32[128]{0:T(128)S(1)}, s32[128]{0:T(128)}, u32[]{:S(2)}) copy-start(s32[128]{0:T(128)} %param.14) | copy-start | bytes 1540
  71.6 49.2 %copy-start.1 = (s32[128]{0:T(128)S(1)}, s32[128]{0:T(128)}, u32[]{:S(2)}) copy-start(s32[128]{0:T(128)} %param.16) | copy-start | bytes 1540
  108.9 1.2 copy-start.3
  110.2 70.6 %all-to-all-start = ((f32[64,3,2,14,128]{4,2,3,1,0:T(2,128)}), f32[64,3,2,14,128]{4,2,3,1,0:T(2,128)S(1)}, u32[]{:S(2)}, u32[]{:S(2)}) async-start(f32[64,3,2,14,128]{4,2,3,1,0:T(2,128)} %copy.50), calls=%async_computation | async-start | bytes 5505024 | tf_op jit(solution)/shard_map/all_to_all | solution.py:44
  117.0 5.8 %copy-start.8 = (s32[128]{0:T(128)S(1)}, s32[128]{0:T(128)}, u32[]{:S(2)}) copy-start(s32[128]{0:T(128)} %param.15) | copy-start | bytes 1540
  188.2 1.5 copy-start.4

commit v7 on v6

--- a/solution.py
+++ b/solution.py
@@ -1,6 +1,8 @@
 import jax
 import jax.numpy as jnp
 from jax import lax
+from jax.experimental import pallas as pl
+from jax.experimental.pallas import tpu as pltpu
 from jax.sharding import PartitionSpec as P
 
 beta_first = 0.9
@@ -18,6 +20,64 @@
     step_size = moved_first / corr_first / (jnp.sqrt(moved_second / corr_second) + adam_eps)
     moved_weight = weight_now - learn_rate * (step_size + decay_rate * weight_now)
     return (moved_weight, moved_first, moved_second)
+
+
+def exchange_kernel(src_ref, dst_ref, sems):
+    count = src_ref.shape[0]
+    me = lax.axis_index("ep")
+    row = lax.axis_index("dp")
+    mesh_id = pl.DeviceIdType.MESH
+
+    barrier = pltpu.get_barrier_semaphore()
+
+    def greet(k, carry):
+        peer = lax.rem(me + k, count)
+        pl.semaphore_signal(barrier, inc=1, device_id=(peer, row), device_id_type=mesh_id)
+        return carry
+
+    lax.fori_loop(1, count, greet, 0)
+    pl.semaphore_wait(barrier, count - 1)
+
+    local = pltpu.make_async_copy(src_ref.at[me], dst_ref.at[me], sems.at[2])
+    local.start()
+
+    def send(k, carry):
+        peer = lax.rem(me + k, count)
+        pltpu.make_async_remote_copy(
+            src_ref=src_ref.at[peer],
+            dst_ref=dst_ref.at[me],
+            send_sem=sems.at[0],
+            recv_sem=sems.at[1],
+            device_id=(peer, row),
+            device_id_type=mesh_id,
+        ).start()
+        return carry
+
+    lax.fori_loop(1, count, send, 0)
+    every = pltpu.make_async_remote_copy(
+        src_ref=src_ref.at[pl.ds(0, count - 1)],
+        dst_ref=dst_ref.at[pl.ds(0, count - 1)],
+        send_sem=sems.at[0],
+        recv_sem=sems.at[1],
+        device_id=(lax.rem(me + 1, count), row),
+        device_id_type=mesh_id,
+    )
+    every.wait_send()
+    every.wait_recv()
+    local.wait()
+
+
+def exchange(array):
+    size = array.size * array.dtype.itemsize
+    return pl.pallas_call(
+        exchange_kernel,
+        out_shape=jax.ShapeDtypeStruct(array.shape, array.dtype),
+        in_specs=[pl.BlockSpec(memory_space=pl.ANY)],
+        out_specs=pl.BlockSpec(memory_space=pl.ANY),
+        scratch_shapes=[pltpu.SemaphoreType.DMA((3,))],
+        compiler_params=pltpu.CompilerParams(collective_id=0, has_side_effects=True),
+        cost_estimate=pl.CostEstimate(flops=0, transcendentals=0, bytes_accessed=2 * size),
+    )(array)
 
 
 def per_device_body(
@@ -48,6 +108,7 @@
 
     dp_count = lax.axis_size("dp")
     dp_index = lax.axis_index("dp")
+
     def block_of(array, index):
         return lax.dynamic_slice_in_dim(array, index * shard_rows, shard_rows, axis=1)
 
@@ -104,12 +165,8 @@
         preferred_element_type=jnp.float32,
     ).reshape(experts, piece_rows, columns)
     moved = jnp.stack(adam_update(state_new[0], state_new[1], state_new[2], gradient))
-    back = lax.all_to_all(
-        moved.reshape(3, ep_count, exp_dev, piece_rows, columns).transpose(1, 0, 2, 3, 4),
-        "ep",
-        split_axis=0,
-        concat_axis=0,
-        tiled=True,
+    back = exchange(
+        moved.reshape(3, ep_count, exp_dev, piece_rows, columns).transpose(1, 0, 2, 3, 4)
     )
     back = back.transpose(1, 2, 0, 3, 4).reshape(3, exp_dev, shard_rows, columns)
     return (back[0], back[1], back[2])

time: 270 us -> 273 us (1.011)
  blocking collectives: 72 us -> 0 us
  Pallas kernels: 0 us -> 68.5 us
  local copies, waits for them, and re-layouts: 36.7 us -> 41 us
    all_to_all x1 -> x0, blocking collectives: 72 us -> none  [per_device_body(): lax.all_to_all(moved.reshape(3, ep_count, exp_dev, piece_rows, columns).t...]
    pallas_call x0 -> x1, Pallas kernels: none -> 68.5 us  [exchange(): pl.pallas_call(exchange_kernel, out_shape=jax.ShapeDtypeStruct(array.shap...]
    unnamed x25 -> x27, local copies, waits for them, and re-layouts: 10 us -> 10 us
where the time goes in v7:
time: 273 us; the launch traced here: 271 us
  waiting for transfers between devices  118 us (43%)
  Pallas kernels  68.5 us (25%)
  local copies, waits for them, and re-layouts  41 us (15%)
  starting transfers between devices  31.8 us (12%)
  other arithmetic  7.78 us (3%)
    pallas_call x1, Pallas kernels, exchange(): pl.pallas_call(exchange_kernel, out_shape=jax.ShapeDtypeStruct(array.shap...  68.5 us
    all_to_all x1, waiting for transfers between devices, per_device_body(): lax.all_to_all(state.transpose(2, 0, 1, 3, 4), 'ep', split_axis=0, concat...  51.2 us
    all_to_all x1, waiting for transfers between devices, per_device_body(): lax.all_to_all(grads.reshape(exp_dev + rep_dev, ep_count, piece_rows, col...  37.3 us
    ppermute x6, waiting for transfers between devices, per_device_body(): lax.ppermute(block_of(array, target), 'dp', [(i, (i + shift) % dp_count)...  29.8 us
    all_to_all x1, starting transfers between devices, per_device_body(): lax.all_to_all(grads.reshape(exp_dev + rep_dev, ep_count, piece_rows, col...  13.3 us
    ppermute x6, starting transfers between devices, per_device_body(): lax.ppermute(block_of(array, target), 'dp', [(i, (i + shift) % dp_count)...  11.7 us
    unnamed x27, local copies, waits for them, and re-layouts  10 us
    all_to_all x1, starting transfers between devices, per_device_body(): lax.all_to_all(state.transpose(2, 0, 1, 3, 4), 'ep', split_axis=0, concat...  6.82 us
  transfers between devices with their start and end apart: 8, of which 7 were waited for; matrix products, arithmetic and copies ran while one was open for 8% of the time, Pallas kernels for 0%

profile of v7, /device:TPU:1, one launch (start us, length us, event | category | flops | bytes accessed | tf_op | source)
XLA Modules:
  0.0 271.0 jit_solution(3097003325864312296)
XLA Ops:
  0.7 2.3 dynamic-slice_bitcast_fusion.5
  3.0 2.0 collective-permute-start
  5.0 1.3 collective-permute-start.2
  6.3 1.7 collective-permute-start.1
  8.0 1.0 dynamic-slice_bitcast_fusion.2
  9.4 2.4 collective-permute-start.5
  11.7 2.6 collective-permute-done
  14.3 4.0 %collective-permute-start.4 = (bf16[2,896,128]{2,1,0:T(8,128)(2,1)S(1)}, bf16[2,896,128]{2,1,0:T(8,128)(2,1)}, u32[]{:S(2)}, u32[]{:S(2)}) collective-permute-start(bf16[2,896,128]{2,1,0:T(8,128)(2,1)S(1)} %get-tuple-element.23), channel_id=1, source_target_pairs={{0,2},{1,3},{2,0},{3,1},{4,6},{5,7},{6,4},{7,5},{8,10},{9,11},{10,... | collective-permute-start | bytes 1376264 | tf_op jit(solution)/shard_map/ppermute | solution.py:121
  18.3 9.1 %collective-permute-done.1 = bf16[2,896,128]{2,1,0:T(8,128)(2,1)} collective-permute-done((bf16[2,896,128]{2,1,0:T(8,128)(2,1)S(1)}, bf16[2,896,128]{2,1,0:T(8,128)(2,1)}, u32[]{:S(2)}, u32[]{:S(2)}) %collective-permute-start.1) | collective-permute-done | bytes 458784 | tf_op jit(solution)/shard_map/ppermute | solution.py:121
  27.4 1.6 fusion.8
  29.0 5.1 %collective-permute-done.3 = bf16[2,896,128]{2,1,0:T(8,128)(2,1)} collective-permute-done((bf16[2,896,128]{2,1,0:T(8,128)(2,1)}, bf16[2,896,128]{2,1,0:T(8,128)(2,1)}, u32[]{:S(2)}, u32[]{:S(2)}) %collective-permute-start.3) | collective-permute-done | bytes 458784 | tf_op jit(solution)/shard_map/ppermute | solution.py:121
  34.1 1.9 collective-permute-done.5
  35.9 11.1 %collective-permute-done.4 = bf16[2,896,128]{2,1,0:T(8,128)(2,1)} collective-permute-done((bf16[2,896,128]{2,1,0:T(8,128)(2,1)S(1)}, bf16[2,896,128]{2,1,0:T(8,128)(2,1)}, u32[]{:S(2)}, u32[]{:S(2)}) %collective-permute-start.4) | collective-permute-done | bytes 458784 | tf_op jit(solution)/shard_map/ppermute | solution.py:121
  47.1 1.6 fusion.6
  48.7 2.4 copy.60
  51.2 13.3 %all-to-all-start.1 = ((f32[64,4,14,128]{3,1,2,0:T(4,128)}), f32[64,4,14,128]{3,1,2,0:T(4,128)S(1)}, u32[]{:S(2)}, u32[]{:S(2)}) async-start(f32[64,4,14,128]{3,1,2,0:T(4,128)} %bitcast.24), calls=%async_computation.1 | async-start | bytes 3670016 | tf_op jit(solution)/shard_map/all_to_all | solution.py:141
  64.5 0.7 copy.53
  65.2 1.9 copy.54
  67.1 0.7 copy.55
  67.9 1.3 maximum_bitcast_fusion.1
  69.1 2.5 copy.56
  71.6 37.3 %all-to-all-done.1 = f32[64,4,14,128]{3,1,2,0:T(4,128)S(1)} async-done(((f32[64,4,14,128]{3,1,2,0:T(4,128)}), f32[64,4,14,128]{3,1,2,0:T(4,128)S(1)}, u32[]{:S(2)}, u32[]{:S(2)}) %all-to-all-start.1) | async-done | bytes 1835040 | tf_op jit(solution)/shard_map/all_to_all | solution.py:141
  108.9 1.2 copy-done.4
  110.2 6.8 %all-to-all-start = ((f32[64,3,2,14,128]{4,2,3,1,0:T(2,128)}), f32[64,3,2,14,128]{4,2,3,1,0:T(2,128)S(1)}, u32[]{:S(2)}, u32[]{:S(2)}) async-start(f32[64,3,2,14,128]{4,2,3,1,0:T(2,128)} %copy.56), calls=%async_computation | async-start | bytes 5505024 | tf_op jit(solution)/shard_map/all_to_all | solution.py:104
  117.0 1.9 gather_fusion.1
  118.9 1.9 gather_fusion.3
  120.9 1.9 gather_fusion.2
  123.0 1.8 copy.61
  124.8 2.0 copy.77
  126.8 2.7 %copy.62 = f32[1792,256]{1,0:T(8,128)} copy(f32[1792,256]{0,1:T(8,128)} %bitcast.79) | data formatting | bytes 3670016 | tf_op jit(solution)/shard_map/dot_general | solution.py:161
  129.5 51.2 %all-to-all-done = f32[64,3,2,14,128]{4,2,3,1,0:T(2,128)S(1)} async-done(((f32[64,3,2,14,128]{4,2,3,1,0:T(2,128)}), f32[64,3,2,14,128]{4,2,3,1,0:T(2,128)S(1)}, u32[]{:S(2)}, u32[]{:S(2)}) %all-to-all-start) | async-done | bytes 2752544 | tf_op jit(solution)/shard_map/all_to_all | solution.py:104
  180.7 1.5 copy.57
  182.3 3.2 %copy.58 = f32[3,128,14,128]{3,2,1,0:T(8,128)} copy(f32[3,128,14,128]{3,1,2,0:T(8,128)S(1)} %bitcast.77) | data formatting | bytes 5505024 | tf_op jit(solution)/shard_map/reshape | solution.py:107
  185.5 2.6 gather_fusion
  188.2 1.0 fusion
  189.6 2.5 multiply_subtract_fusion
  192.2 0.5 copy.63
  192.7 0.5 copy.64
  193.3 0.5 copy.65
  193.8 2.0 maximum_bitcast_fusion.src_ref
  195.8 68.5 %shard_map.112 = f32[64,3,2,14,128]{4,3,2,1,0:T(8,128)} custom-call(f32[64,3,2,14,128]{4,3,2,1,0:T(8,128)} %maximum_bitcast_fusion.src_ref), custom_call_target="tpu_custom_call" | custom-call | bytes 5505024 | tf_op jit(solution)/shard_map/pallas_call | solution.py:72
  264.4 2.2 fusion.29
  266.6 0.5 copy.68
  267.0 1.0 copy.71
  268.0 0.5 copy.67
  268.5 1.0 copy.70
  269.5 0.5 copy.66
  270.0 1.0 copy.69
  (33 shorter events, 1.2 us)
Async XLA Ops:
  0.6 118.3 %copy-start = (s32[64]{0:T(128)S(1)}, s32[64]{0:T(128)}, u32[]{:S(2)}) copy-start(s32[64]{0:T(128)} %param.17) | copy-start | bytes 772
  0.6 7.4 %copy-start.6 = (bf16[1,2,3584,128]{3,2,1,0:T(8,128)(2,1)S(1)}, bf16[1,2,3584,128]{3,2,1,0:T(8,128)(2,1)}, u32[]{:S(2)}) copy-start(bf16[1,2,3584,128]{3,2,1,0:T(8,128)(2,1)} %param.13) | copy-start | bytes 5505028
  3.0 11.3 %collective-permute-start = (bf16[2,896,128]{2,1,0:T(8,128)(2,1)S(1)}, bf16[2,896,128]{2,1,0:T(8,128)(2,1)S(1)}, u32[]{:S(2)}, u32[]{:S(2)}) collective-permute-start(bf16[2,896,128]{2,1,0:T(8,128)(2,1)S(1)} %get-tuple-element.18), channel_id=1, source_target_pairs={{0,1},{1,2},{2,3},{3,0},{4,5},{5,6},{6,7},{7,4},{8,9},{9,10},{10,1... | collective-permute-start | bytes 1376264 | tf_op jit(solution)/shard_map/ppermute | solution.py:121
  5.0 13.3 %collective-permute-start.2 = (bf16[2,896,128]{2,1,0:T(8,128)(2,1)}, bf16[2,896,128]{2,1,0:T(8,128)(2,1)}, u32[]{:S(2)}, u32[]{:S(2)}) collective-permute-start(bf16[2,896,128]{2,1,0:T(8,128)(2,1)} %get-tuple-element.19), channel_id=1, source_target_pairs={{0,3},{1,0},{2,1},{3,2},{4,7},{5,4},{6,5},{7,6},{8,11},{9,8},{10,9... | collective-permute-start | bytes 1376264 | tf_op jit(solution)/shard_map/ppermute | solution.py:121
  6.3 21.1 %collective-permute-start.1 = (bf16[2,896,128]{2,1,0:T(8,128)(2,1)S(1)}, bf16[2,896,128]{2,1,0:T(8,128)(2,1)}, u32[]{:S(2)}, u32[]{:S(2)}) collective-permute-start(bf16[2,896,128]{2,1,0:T(8,128)(2,1)S(1)} %get-tuple-element.20), channel_id=1, source_target_pairs={{0,2},{1,3},{2,0},{3,1},{4,6},{5,7},{6,4},{7,5},{8,10},{9,11},{10,... | collective-permute-start | bytes 1376264 | tf_op jit(solution)/shard_map/ppermute | solution.py:121
  9.0 25.0 %collective-permute-start.3 = (bf16[2,896,128]{2,1,0:T(8,128)(2,1)}, bf16[2,896,128]{2,1,0:T(8,128)(2,1)}, u32[]{:S(2)}, u32[]{:S(2)}) collective-permute-start(bf16[2,896,128]{2,1,0:T(8,128)(2,1)} %get-tuple-element.21), channel_id=1, source_target_pairs={{0,1},{1,2},{2,3},{3,0},{4,5},{5,6},{6,7},{7,4},{8,9},{9,10},{10,1... | collective-permute-start | bytes 1376264 | tf_op jit(solution)/shard_map/ppermute | solution.py:121
  9.4 26.6 %collective-permute-start.5 = (bf16[2,896,128]{2,1,0:T(8,128)(2,1)}, bf16[2,896,128]{2,1,0:T(8,128)(2,1)}, u32[]{:S(2)}, u32[]{:S(2)}) collective-permute-start(bf16[2,896,128]{2,1,0:T(8,128)(2,1)} %get-tuple-element.22), channel_id=1, source_target_pairs={{0,3},{1,0},{2,1},{3,2},{4,7},{5,4},{6,5},{7,6},{8,11},{9,8},{10,9... | collective-permute-start | bytes 1376264 | tf_op jit(solution)/shard_map/ppermute | solution.py:121
  14.3 32.7 %collective-permute-start.4 = (bf16[2,896,128]{2,1,0:T(8,128)(2,1)S(1)}, bf16[2,896,128]{2,1,0:T(8,128)(2,1)}, u32[]{:S(2)}, u32[]{:S(2)}) collective-permute-start(bf16[2,896,128]{2,1,0:T(8,128)(2,1)S(1)} %get-tuple-element.23), channel_id=1, source_target_pairs={{0,2},{1,3},{2,0},{3,1},{4,6},{5,7},{6,4},{7,5},{8,10},{9,11},{10,... | collective-permute-start | bytes 1376264 | tf_op jit(solution)/shard_map/ppermute | solution.py:121
  51.2 13.3 %copy-start.7 = (f32[2,896,128]{2,1,0:T(8,128)S(1)}, f32[2,896,128]{2,1,0:T(8,128)}, u32[]{:S(2)}) copy-start(f32[2,896,128]{2,1,0:T(8,128)} %param.9) | copy-start | bytes 2752516
  51.2 57.7 %all-to-all-start.1 = ((f32[64,4,14,128]{3,1,2,0:T(4,128)}), f32[64,4,14,128]{3,1,2,0:T(4,128)S(1)}, u32[]{:S(2)}, u32[]{:S(2)}) async-start(f32[64,4,14,128]{3,1,2,0:T(4,128)} %bitcast.24), calls=%async_computation.1 | async-start | bytes 3670016 | tf_op jit(solution)/shard_map/all_to_all | solution.py:141
  64.5 2.6 copy-start.8
  71.6 45.4 %copy-start.3 = (s32[128]{0:T(128)S(1)}, s32[128]{0:T(128)}, u32[]{:S(2)}) copy-start(s32[128]{0:T(128)} %param.14) | copy-start | bytes 1540
  71.6 49.2 %copy-start.2 = (s32[128]{0:T(128)S(1)}, s32[128]{0:T(128)}, u32[]{:S(2)}) copy-start(s32[128]{0:T(128)} %param.16) | copy-start | bytes 1540
  108.9 1.2 copy-start.4
  110.2 70.6 %all-to-all-start = ((f32[64,3,2,14,128]{4,2,3,1,0:T(2,128)}), f32[64,3,2,14,128]{4,2,3,1,0:T(2,128)S(1)}, u32[]{:S(2)}, u32[]{:S(2)}) async-start(f32[64,3,2,14,128]{4,2,3,1,0:T(2,128)} %copy.56), calls=%async_computation | async-start | bytes 5505024 | tf_op jit(solution)/shard_map/all_to_all | solution.py:104
  117.0 5.8 %copy-start.9 = (s32[128]{0:T(128)S(1)}, s32[128]{0:T(128)}, u32[]{:S(2)}) copy-start(s32[128]{0:T(128)} %param.15) | copy-start | bytes 1540
  188.1 1.5 copy-start.5
  268.5 2.5 copy-start.1

commit v8 on v6

--- a/solution.py
+++ b/solution.py
@@ -1,6 +1,8 @@
 import jax
 import jax.numpy as jnp
 from jax import lax
+from jax.experimental import pallas as pl
+from jax.experimental.pallas import tpu as pltpu
 from jax.sharding import PartitionSpec as P
 
 beta_first = 0.9
@@ -18,6 +20,71 @@
     step_size = moved_first / corr_first / (jnp.sqrt(moved_second / corr_second) + adam_eps)
     moved_weight = weight_now - learn_rate * (step_size + decay_rate * weight_now)
     return (moved_weight, moved_first, moved_second)
+
+
+def exchange_kernel(*refs):
+    arrays = (len(refs) - 1) // 2
+    srcs, dsts, sems = refs[:arrays], refs[arrays : 2 * arrays], refs[2 * arrays]
+    count = srcs[0].shape[0]
+    me = lax.axis_index("ep")
+    row = lax.axis_index("dp")
+    mesh_id = pl.DeviceIdType.MESH
+
+    barrier = pltpu.get_barrier_semaphore()
+
+    def greet(k, carry):
+        peer = lax.rem(me + k, count)
+        pl.semaphore_signal(barrier, inc=1, device_id=(peer, row), device_id_type=mesh_id)
+        return carry
+
+    lax.fori_loop(1, count, greet, 0)
+    pl.semaphore_wait(barrier, count - 1)
+
+    locals_ = []
+    for a in range(arrays):
+        local = pltpu.make_async_copy(srcs[a].at[me], dsts[a].at[me], sems.at[a, 2])
+        local.start()
+        locals_.append(local)
+
+    def send(k, carry):
+        peer = lax.rem(me + k, count)
+        for a in range(arrays):
+            pltpu.make_async_remote_copy(
+                src_ref=srcs[a].at[peer],
+                dst_ref=dsts[a].at[me],
+                send_sem=sems.at[a, 0],
+                recv_sem=sems.at[a, 1],
+                device_id=(peer, row),
+                device_id_type=mesh_id,
+            ).start()
+        return carry
+
+    lax.fori_loop(1, count, send, 0)
+    for a in range(arrays):
+        every = pltpu.make_async_remote_copy(
+            src_ref=srcs[a].at[pl.ds(0, count - 1)],
+            dst_ref=dsts[a].at[pl.ds(0, count - 1)],
+            send_sem=sems.at[a, 0],
+            recv_sem=sems.at[a, 1],
+            device_id=(lax.rem(me + 1, count), row),
+            device_id_type=mesh_id,
+        )
+        every.wait_send()
+        every.wait_recv()
+        locals_[a].wait()
+
+
+def exchange(*arrays):
+    size = sum(array.size * array.dtype.itemsize for array in arrays)
+    return pl.pallas_call(
+        exchange_kernel,
+        out_shape=tuple(jax.ShapeDtypeStruct(array.shape, array.dtype) for array in arrays),
+        in_specs=[pl.BlockSpec(memory_space=pl.ANY)] * len(arrays),
+        out_specs=tuple(pl.BlockSpec(memory_space=pl.ANY) for _ in arrays),
+        scratch_shapes=[pltpu.SemaphoreType.DMA((len(arrays), 3))],
+        compiler_params=pltpu.CompilerParams(collective_id=0, has_side_effects=True),
+        cost_estimate=pl.CostEstimate(flops=0, transcendentals=0, bytes_accessed=2 * size),
+    )(*arrays)
 
 
 def per_device_body(
@@ -48,6 +115,7 @@
 
     dp_count = lax.axis_size("dp")
     dp_index = lax.axis_index("dp")
+
     def block_of(array, index):
         return lax.dynamic_slice_in_dim(array, index * shard_rows, shard_rows, axis=1)
 
@@ -103,16 +171,11 @@
         precision=lax.Precision.HIGHEST,
         preferred_element_type=jnp.float32,
     ).reshape(experts, piece_rows, columns)
-    moved = jnp.stack(adam_update(state_new[0], state_new[1], state_new[2], gradient))
-    back = lax.all_to_all(
-        moved.reshape(3, ep_count, exp_dev, piece_rows, columns).transpose(1, 0, 2, 3, 4),
-        "ep",
-        split_axis=0,
-        concat_axis=0,
-        tiled=True,
+    moved = adam_update(state_new[0], state_new[1], state_new[2], gradient)
+    back = exchange(*(array.reshape(ep_count, exp_dev, piece_rows, columns) for array in moved))
+    return tuple(
+        array.transpose(1, 0, 2, 3).reshape(exp_dev, shard_rows, columns) for array in back
     )
-    back = back.transpose(1, 2, 0, 3, 4).reshape(3, exp_dev, shard_rows, columns)
-    return (back[0], back[1], back[2])
 
 
 def solution(mesh):

time: 270 us -> 273 us (1.011); the launches traced: 269 us -> 269 us
  blocking collectives: 72 us -> 0 us
  Pallas kernels: 0 us -> 66.2 us
  local copies, waits for them, and re-layouts: 36.7 us -> 43.1 us
    all_to_all x1 -> x0, blocking collectives: 72 us -> none  [per_device_body(): lax.all_to_all(moved.reshape(3, ep_count, exp_dev, piece_rows, columns).t...]
    pallas_call x0 -> x1, Pallas kernels: none -> 66.2 us  [exchange(): pl.pallas_call(exchange_kernel, out_shape=tuple((jax.ShapeDtypeStruct(arr...]
    add x0 -> x2, local copies, waits for them, and re-layouts: none -> 3.03 us  [the longest x1 1.52 us: adam_update(): beta_second * second_now + (1.0 - beta_second) * gradient * gradient]
    transpose x0 -> x3, local copies, waits for them, and re-layouts: none -> 2.73 us  [per_device_body(): array.transpose(1, 0, 2, 3).reshape(exp_dev, shard_rows, columns)]
    unnamed x25 -> x29, local copies, waits for them, and re-layouts: 10 us -> 10.1 us
where the time goes in v8:
time: 273 us; the launch traced here: 269 us
  waiting for transfers between devices  118 us (43%)
  Pallas kernels  66.2 us (24%)
  local copies, waits for them, and re-layouts  43.1 us (16%)
  starting transfers between devices  31.8 us (12%)
  other arithmetic  5.79 us (2%)
    pallas_call x1, Pallas kernels, exchange(): pl.pallas_call(exchange_kernel, out_shape=tuple((jax.ShapeDtypeStruct(arr...  66.2 us
    all_to_all x1, waiting for transfers between devices, per_device_body(): lax.all_to_all(state.transpose(2, 0, 1, 3, 4), 'ep', split_axis=0, concat...  51.2 us
    all_to_all x1, waiting for transfers between devices, per_device_body(): lax.all_to_all(grads.reshape(exp_dev + rep_dev, ep_count, piece_rows, col...  37.3 us
    ppermute x6, waiting for transfers between devices, per_device_body(): lax.ppermute(block_of(array, target), 'dp', [(i, (i + shift) % dp_count)...  29.8 us
    all_to_all x1, starting transfers between devices, per_device_body(): lax.all_to_all(grads.reshape(exp_dev + rep_dev, ep_count, piece_rows, col...  13.3 us
    ppermute x6, starting transfers between devices, per_device_body(): lax.ppermute(block_of(array, target), 'dp', [(i, (i + shift) % dp_count)...  11.7 us
    unnamed x29, local copies, waits for them, and re-layouts  10.1 us
    all_to_all x1, starting transfers between devices, per_device_body(): lax.all_to_all(state.transpose(2, 0, 1, 3, 4), 'ep', split_axis=0, concat...  6.82 us
  transfers between devices with their start and end apart: 8, of which 7 were waited for; matrix products, arithmetic and copies ran while one was open for 8% of the time, Pallas kernels for 0%

profile of v8, /device:TPU:1, one launch (start us, length us, event | category | flops | bytes accessed | tf_op | source)
XLA Modules:
  0.0 268.7 jit_solution(17195784772062758614)
XLA Ops:
  0.7 2.3 dynamic-slice_bitcast_fusion.5
  3.0 2.0 collective-permute-start
  5.0 1.3 collective-permute-start.2
  6.3 1.7 collective-permute-start.1
  8.0 1.0 dynamic-slice_bitcast_fusion.2
  9.0 0.3 collective-permute-start.3
  9.4 2.4 collective-permute-start.5
  11.7 2.6 collective-permute-done
  14.3 4.0 %collective-permute-start.4 = (bf16[2,896,128]{2,1,0:T(8,128)(2,1)S(1)}, bf16[2,896,128]{2,1,0:T(8,128)(2,1)}, u32[]{:S(2)}, u32[]{:S(2)}) collective-permute-start(bf16[2,896,128]{2,1,0:T(8,128)(2,1)S(1)} %get-tuple-element.26), channel_id=1, source_target_pairs={{0,2},{1,3},{2,0},{3,1},{4,6},{5,7},{6,4},{7,5},{8,10},{9,11},{10,... | collective-permute-start | bytes 1376264 | tf_op jit(solution)/shard_map/ppermute | solution.py:128
  18.3 9.1 %collective-permute-done.1 = bf16[2,896,128]{2,1,0:T(8,128)(2,1)} collective-permute-done((bf16[2,896,128]{2,1,0:T(8,128)(2,1)S(1)}, bf16[2,896,128]{2,1,0:T(8,128)(2,1)}, u32[]{:S(2)}, u32[]{:S(2)}) %collective-permute-start.1) | collective-permute-done | bytes 458784 | tf_op jit(solution)/shard_map/ppermute | solution.py:128
  27.4 1.6 fusion.8
  29.0 5.1 %collective-permute-done.3 = bf16[2,896,128]{2,1,0:T(8,128)(2,1)} collective-permute-done((bf16[2,896,128]{2,1,0:T(8,128)(2,1)}, bf16[2,896,128]{2,1,0:T(8,128)(2,1)}, u32[]{:S(2)}, u32[]{:S(2)}) %collective-permute-start.3) | collective-permute-done | bytes 458784 | tf_op jit(solution)/shard_map/ppermute | solution.py:128
  34.1 1.9 collective-permute-done.5
  35.9 11.1 %collective-permute-done.4 = bf16[2,896,128]{2,1,0:T(8,128)(2,1)} collective-permute-done((bf16[2,896,128]{2,1,0:T(8,128)(2,1)S(1)}, bf16[2,896,128]{2,1,0:T(8,128)(2,1)}, u32[]{:S(2)}, u32[]{:S(2)}) %collective-permute-start.4) | collective-permute-done | bytes 458784 | tf_op jit(solution)/shard_map/ppermute | solution.py:128
  47.1 1.6 fusion.6
  48.7 2.4 copy.60
  51.2 13.3 %all-to-all-start.1 = ((f32[64,4,14,128]{3,1,2,0:T(4,128)}), f32[64,4,14,128]{3,1,2,0:T(4,128)S(1)}, u32[]{:S(2)}, u32[]{:S(2)}) async-start(f32[64,4,14,128]{3,1,2,0:T(4,128)} %bitcast.24), calls=%async_computation.1 | async-start | bytes 3670016 | tf_op jit(solution)/shard_map/all_to_all | solution.py:148
  64.5 0.7 copy.53
  65.2 1.9 copy.54
  67.1 0.7 copy.55
  67.9 1.3 maximum_bitcast_fusion
  69.1 2.5 copy.56
  71.6 37.3 %all-to-all-done.1 = f32[64,4,14,128]{3,1,2,0:T(4,128)S(1)} async-done(((f32[64,4,14,128]{3,1,2,0:T(4,128)}), f32[64,4,14,128]{3,1,2,0:T(4,128)S(1)}, u32[]{:S(2)}, u32[]{:S(2)}) %all-to-all-start.1) | async-done | bytes 1835040 | tf_op jit(solution)/shard_map/all_to_all | solution.py:148
  108.9 1.2 copy-done.3
  110.2 6.8 %all-to-all-start = ((f32[64,3,2,14,128]{4,2,3,1,0:T(2,128)}), f32[64,3,2,14,128]{4,2,3,1,0:T(2,128)S(1)}, u32[]{:S(2)}, u32[]{:S(2)}) async-start(f32[64,3,2,14,128]{4,2,3,1,0:T(2,128)} %copy.56), calls=%async_computation | async-start | bytes 5505024 | tf_op jit(solution)/shard_map/all_to_all | solution.py:111
  117.0 1.9 gather_fusion.1
  118.9 1.9 gather_fusion.3
  120.9 1.9 gather_fusion.2
  123.0 1.8 copy.61
  124.8 2.0 copy.77
  126.8 2.7 %copy.62 = f32[1792,256]{1,0:T(8,128)} copy(f32[1792,256]{0,1:T(8,128)} %bitcast.78) | data formatting | bytes 3670016 | tf_op jit(solution)/shard_map/dot_general | solution.py:168
  129.5 51.2 %all-to-all-done = f32[64,3,2,14,128]{4,2,3,1,0:T(2,128)S(1)} async-done(((f32[64,3,2,14,128]{4,2,3,1,0:T(2,128)}), f32[64,3,2,14,128]{4,2,3,1,0:T(2,128)S(1)}, u32[]{:S(2)}, u32[]{:S(2)}) %all-to-all-start) | async-done | bytes 2752544 | tf_op jit(solution)/shard_map/all_to_all | solution.py:111
  180.7 1.5 copy.57
  182.3 3.2 %copy.58 = f32[3,128,14,128]{3,2,1,0:T(8,128)} copy(f32[3,128,14,128]{3,1,2,0:T(8,128)S(1)} %bitcast.76) | data formatting | bytes 5505024 | tf_op jit(solution)/shard_map/reshape | solution.py:114
  185.5 2.6 gather_fusion
  188.2 1.0 fusion
  189.2 0.5 copy-done.4
  189.6 2.5 multiply_subtract_fusion
  192.2 1.5 copy.63
  193.7 1.5 copy.64
  195.2 1.5 copy.65
  196.8 66.2 %shard_map.112 = (f32[64,2,14,128]{3,2,1,0:T(8,128)}, f32[64,2,14,128]{3,2,1,0:T(8,128)}, f32[64,2,14,128]{3,2,1,0:T(8,128)}) custom-call(f32[64,2,14,128]{3,2,1,0:T(8,128)} %bitcast.79, f32[64,2,14,128]{3,2,1,0:T(8,128)} %bitcast.80, f32[64,2,14,128]{3,2,1,0:T(8,128)} %bitcast.81), custom_call_target="tpu_custom_call" | custom-call | bytes 5505024 | tf_op jit(solution)/shard_map/pallas_call | solution.py:79
  263.0 1.8 copy.66
  264.8 1.0 copy.69
  265.8 0.5 copy.67
  266.2 1.0 copy.70
  267.2 0.5 copy.68
  267.7 1.0 copy.71
  (33 shorter events, 0.4 us)
Async XLA Ops:
  0.6 118.3 %copy-start = (s32[64]{0:T(128)S(1)}, s32[64]{0:T(128)}, u32[]{:S(2)}) copy-start(s32[64]{0:T(128)} %param.17) | copy-start | bytes 772
  0.6 7.4 %copy-start.5 = (bf16[1,2,3584,128]{3,2,1,0:T(8,128)(2,1)S(1)}, bf16[1,2,3584,128]{3,2,1,0:T(8,128)(2,1)}, u32[]{:S(2)}) copy-start(bf16[1,2,3584,128]{3,2,1,0:T(8,128)(2,1)} %param.13) | copy-start | bytes 5505028
  3.0 11.3 %collective-permute-start = (bf16[2,896,128]{2,1,0:T(8,128)(2,1)S(1)}, bf16[2,896,128]{2,1,0:T(8,128)(2,1)S(1)}, u32[]{:S(2)}, u32[]{:S(2)}) collective-permute-start(bf16[2,896,128]{2,1,0:T(8,128)(2,1)S(1)} %get-tuple-element.21), channel_id=1, source_target_pairs={{0,1},{1,2},{2,3},{3,0},{4,5},{5,6},{6,7},{7,4},{8,9},{9,10},{10,1... | collective-permute-start | bytes 1376264 | tf_op jit(solution)/shard_map/ppermute | solution.py:128
  5.0 13.3 %collective-permute-start.2 = (bf16[2,896,128]{2,1,0:T(8,128)(2,1)}, bf16[2,896,128]{2,1,0:T(8,128)(2,1)}, u32[]{:S(2)}, u32[]{:S(2)}) collective-permute-start(bf16[2,896,128]{2,1,0:T(8,128)(2,1)} %get-tuple-element.22), channel_id=1, source_target_pairs={{0,3},{1,0},{2,1},{3,2},{4,7},{5,4},{6,5},{7,6},{8,11},{9,8},{10,9... | collective-permute-start | bytes 1376264 | tf_op jit(solution)/shard_map/ppermute | solution.py:128
  6.3 21.1 %collective-permute-start.1 = (bf16[2,896,128]{2,1,0:T(8,128)(2,1)S(1)}, bf16[2,896,128]{2,1,0:T(8,128)(2,1)}, u32[]{:S(2)}, u32[]{:S(2)}) collective-permute-start(bf16[2,896,128]{2,1,0:T(8,128)(2,1)S(1)} %get-tuple-element.23), channel_id=1, source_target_pairs={{0,2},{1,3},{2,0},{3,1},{4,6},{5,7},{6,4},{7,5},{8,10},{9,11},{10,... | collective-permute-start | bytes 1376264 | tf_op jit(solution)/shard_map/ppermute | solution.py:128
  9.0 25.0 %collective-permute-start.3 = (bf16[2,896,128]{2,1,0:T(8,128)(2,1)}, bf16[2,896,128]{2,1,0:T(8,128)(2,1)}, u32[]{:S(2)}, u32[]{:S(2)}) collective-permute-start(bf16[2,896,128]{2,1,0:T(8,128)(2,1)} %get-tuple-element.24), channel_id=1, source_target_pairs={{0,1},{1,2},{2,3},{3,0},{4,5},{5,6},{6,7},{7,4},{8,9},{9,10},{10,1... | collective-permute-start | bytes 1376264 | tf_op jit(solution)/shard_map/ppermute | solution.py:128
  9.4 26.6 %collective-permute-start.5 = (bf16[2,896,128]{2,1,0:T(8,128)(2,1)}, bf16[2,896,128]{2,1,0:T(8,128)(2,1)}, u32[]{:S(2)}, u32[]{:S(2)}) collective-permute-start(bf16[2,896,128]{2,1,0:T(8,128)(2,1)} %get-tuple-element.25), channel_id=1, source_target_pairs={{0,3},{1,0},{2,1},{3,2},{4,7},{5,4},{6,5},{7,6},{8,11},{9,8},{10,9... | collective-permute-start | bytes 1376264 | tf_op jit(solution)/shard_map/ppermute | solution.py:128
  14.3 32.7 %collective-permute-start.4 = (bf16[2,896,128]{2,1,0:T(8,128)(2,1)S(1)}, bf16[2,896,128]{2,1,0:T(8,128)(2,1)}, u32[]{:S(2)}, u32[]{:S(2)}) collective-permute-start(bf16[2,896,128]{2,1,0:T(8,128)(2,1)S(1)} %get-tuple-element.26), channel_id=1, source_target_pairs={{0,2},{1,3},{2,0},{3,1},{4,6},{5,7},{6,4},{7,5},{8,10},{9,11},{10,... | collective-permute-start | bytes 1376264 | tf_op jit(solution)/shard_map/ppermute | solution.py:128
  51.2 13.3 %copy-start.8 = (f32[2,896,128]{2,1,0:T(8,128)S(1)}, f32[2,896,128]{2,1,0:T(8,128)}, u32[]{:S(2)}) copy-start(f32[2,896,128]{2,1,0:T(8,128)} %param.9) | copy-start | bytes 2752516
  51.2 57.7 %all-to-all-start.1 = ((f32[64,4,14,128]{3,1,2,0:T(4,128)}), f32[64,4,14,128]{3,1,2,0:T(4,128)S(1)}, u32[]{:S(2)}, u32[]{:S(2)}) async-start(f32[64,4,14,128]{3,1,2,0:T(4,128)} %bitcast.24), calls=%async_computation.1 | async-start | bytes 3670016 | tf_op jit(solution)/shard_map/all_to_all | solution.py:148
  64.5 2.6 copy-start.9
  71.6 45.4 %copy-start.2 = (s32[128]{0:T(128)S(1)}, s32[128]{0:T(128)}, u32[]{:S(2)}) copy-start(s32[128]{0:T(128)} %param.14) | copy-start | bytes 1540
  71.6 49.2 %copy-start.1 = (s32[128]{0:T(128)S(1)}, s32[128]{0:T(128)}, u32[]{:S(2)}) copy-start(s32[128]{0:T(128)} %param.16) | copy-start | bytes 1540
  108.9 1.2 copy-start.3
  110.2 70.6 %all-to-all-start = ((f32[64,3,2,14,128]{4,2,3,1,0:T(2,128)}), f32[64,3,2,14,128]{4,2,3,1,0:T(2,128)S(1)}, u32[]{:S(2)}, u32[]{:S(2)}) async-start(f32[64,3,2,14,128]{4,2,3,1,0:T(2,128)} %copy.56), calls=%async_computation | async-start | bytes 5505024 | tf_op jit(solution)/shard_map/all_to_all | solution.py:111
  117.0 5.8 %copy-start.10 = (s32[128]{0:T(128)S(1)}, s32[128]{0:T(128)}, u32[]{:S(2)}) copy-start(s32[128]{0:T(128)} %param.15) | copy-start | bytes 1540
  188.1 1.5 copy-start.4
  263.0 2.8 %copy-start.7 = (f32[64,2,14,128]{3,2,1,0:T(8,128)S(1)}, f32[64,2,14,128]{3,2,1,0:T(8,128)}, u32[]{:S(2)}) copy-start(f32[64,2,14,128]{3,2,1,0:T(8,128)} %get-tuple-element.7) | copy-start | bytes 2752516
  264.8 2.5 copy-start.6

commit v9 on v8

--- a/solution.py
+++ b/solution.py
@@ -26,9 +26,23 @@
     arrays = (len(refs) - 1) // 2
     srcs, dsts, sems = refs[:arrays], refs[arrays : 2 * arrays], refs[2 * arrays]
     count = srcs[0].shape[0]
+    piece = dsts[0].shape[1] // count
     me = lax.axis_index("ep")
     row = lax.axis_index("dp")
     mesh_id = pl.DeviceIdType.MESH
+
+    def window(ref, source):
+        return ref.at[:, pl.ds(source * piece, piece), :]
+
+    def copy(a, k, peer):
+        return pltpu.make_async_remote_copy(
+            src_ref=srcs[a].at[peer],
+            dst_ref=window(dsts[a], me),
+            send_sem=sems.at[a, 0, k],
+            recv_sem=sems.at[a, 1, k],
+            device_id=(peer, row),
+            device_id_type=mesh_id,
+        )
 
     barrier = pltpu.get_barrier_semaphore()
 
@@ -42,46 +56,48 @@
 
     locals_ = []
     for a in range(arrays):
-        local = pltpu.make_async_copy(srcs[a].at[me], dsts[a].at[me], sems.at[a, 2])
+        local = pltpu.make_async_copy(srcs[a].at[me], window(dsts[a], me), sems.at[a, 0, 0])
         local.start()
         locals_.append(local)
 
     def send(k, carry):
         peer = lax.rem(me + k, count)
         for a in range(arrays):
+            copy(a, k, peer).start()
+        return carry
+
+    lax.fori_loop(1, count, send, 0)
+
+    def finish(k, carry):
+        peer = lax.rem(me + k, count)
+        for a in range(arrays):
+            copy(a, k, peer).wait_send()
             pltpu.make_async_remote_copy(
                 src_ref=srcs[a].at[peer],
-                dst_ref=dsts[a].at[me],
-                send_sem=sems.at[a, 0],
-                recv_sem=sems.at[a, 1],
+                dst_ref=window(dsts[a], lax.rem(me + count - k, count)),
+                send_sem=sems.at[a, 0, k],
+                recv_sem=sems.at[a, 1, k],
                 device_id=(peer, row),
                 device_id_type=mesh_id,
-            ).start()
+            ).wait_recv()
         return carry
 
-    lax.fori_loop(1, count, send, 0)
-    for a in range(arrays):
-        every = pltpu.make_async_remote_copy(
-            src_ref=srcs[a].at[pl.ds(0, count - 1)],
-            dst_ref=dsts[a].at[pl.ds(0, count - 1)],
-            send_sem=sems.at[a, 0],
-            recv_sem=sems.at[a, 1],
-            device_id=(lax.rem(me + 1, count), row),
-            device_id_type=mesh_id,
-        )
-        every.wait_send()
-        every.wait_recv()
-        locals_[a].wait()
-
-
-def exchange(*arrays):
+    lax.fori_loop(1, count, finish, 0)
+    for local in locals_:
+        local.wait()
+
+
+def exchange(rows, *arrays):
+    count, slots, _, lanes = arrays[0].shape
     size = sum(array.size * array.dtype.itemsize for array in arrays)
     return pl.pallas_call(
         exchange_kernel,
-        out_shape=tuple(jax.ShapeDtypeStruct(array.shape, array.dtype) for array in arrays),
+        out_shape=tuple(
+            jax.ShapeDtypeStruct((slots, rows, lanes), array.dtype) for array in arrays
+        ),
         in_specs=[pl.BlockSpec(memory_space=pl.ANY)] * len(arrays),
         out_specs=tuple(pl.BlockSpec(memory_space=pl.ANY) for _ in arrays),
-        scratch_shapes=[pltpu.SemaphoreType.DMA((len(arrays), 3))],
+        scratch_shapes=[pltpu.SemaphoreType.DMA((len(arrays), 2, count))],
         compiler_params=pltpu.CompilerParams(collective_id=0, has_side_effects=True),
         cost_estimate=pl.CostEstimate(flops=0, transcendentals=0, bytes_accessed=2 * size),
     )(*arrays)
@@ -172,9 +188,8 @@
         preferred_element_type=jnp.float32,
     ).reshape(experts, piece_rows, columns)
     moved = adam_update(state_new[0], state_new[1], state_new[2], gradient)
-    back = exchange(*(array.reshape(ep_count, exp_dev, piece_rows, columns) for array in moved))
-    return tuple(
-        array.transpose(1, 0, 2, 3).reshape(exp_dev, shard_rows, columns) for array in back
+    return exchange(
+        shard_rows, *(array.reshape(ep_count, exp_dev, piece_rows, columns) for array in moved)
     )
 
 

time: 273 us -> 277 us (1.015)
  Pallas kernels: 66.2 us -> 69.6 us
    pallas_call x1, Pallas kernels: 66.2 us -> 69.6 us  [exchange(): pl.pallas_call(exchange_kernel, out_shape=tuple((jax.ShapeDtypeStruct((sl...]
    unnamed x29 -> x27, local copies, waits for them, and re-layouts: 10.1 us -> 12.4 us
where the time goes in v9:
time: 277 us; the launch traced here: 272 us
  waiting for transfers between devices  118 us (43%)
  Pallas kernels  69.6 us (25%)
  local copies, waits for them, and re-layouts  42.7 us (15%)
  starting transfers between devices  31.8 us (11%)
  other arithmetic  5.79 us (2%)
    pallas_call x1, Pallas kernels, exchange(): pl.pallas_call(exchange_kernel, out_shape=tuple((jax.ShapeDtypeStruct((sl...  69.6 us
    all_to_all x1, waiting for transfers between devices, per_device_body(): lax.all_to_all(state.transpose(2, 0, 1, 3, 4), 'ep', split_axis=0, concat...  51.2 us
    all_to_all x1, waiting for transfers between devices, per_device_body(): lax.all_to_all(grads.reshape(exp_dev + rep_dev, ep_count, piece_rows, col...  37.3 us
    ppermute x6, waiting for transfers between devices, per_device_body(): lax.ppermute(block_of(array, target), 'dp', [(i, (i + shift) % dp_count)...  29.8 us
    all_to_all x1, starting transfers between devices, per_device_body(): lax.all_to_all(grads.reshape(exp_dev + rep_dev, ep_count, piece_rows, col...  13.3 us
    unnamed x27, local copies, waits for them, and re-layouts  12.4 us
    ppermute x6, starting transfers between devices, per_device_body(): lax.ppermute(block_of(array, target), 'dp', [(i, (i + shift) % dp_count)...  11.7 us
    all_to_all x1, starting transfers between devices, per_device_body(): lax.all_to_all(state.transpose(2, 0, 1, 3, 4), 'ep', split_axis=0, concat...  6.82 us
  transfers between devices with their start and end apart: 8, of which 7 were waited for; matrix products, arithmetic and copies ran while one was open for 8% of the time, Pallas kernels for 0%

profile of v9, /device:TPU:1, one launch (start us, length us, event | category | flops | bytes accessed | tf_op | source)
XLA Modules:
  0.0 271.7 jit_solution(3861883268642129258)
XLA Ops:
  0.6 0.0 copy-start
  0.7 2.3 dynamic-slice_bitcast_fusion.5
  3.0 2.0 collective-permute-start
  5.0 1.3 collective-permute-start.2
  6.3 1.7 collective-permute-start.1
  8.0 1.0 dynamic-slice_bitcast_fusion.2
  9.0 0.3 collective-permute-start.3
  9.4 2.4 collective-permute-start.5
  11.7 2.6 collective-permute-done
  14.3 4.0 %collective-permute-start.4 = (bf16[2,896,128]{2,1,0:T(8,128)(2,1)S(1)}, bf16[2,896,128]{2,1,0:T(8,128)(2,1)}, u32[]{:S(2)}, u32[]{:S(2)}) collective-permute-start(bf16[2,896,128]{2,1,0:T(8,128)(2,1)S(1)} %get-tuple-element.11), channel_id=1, source_target_pairs={{0,2},{1,3},{2,0},{3,1},{4,6},{5,7},{6,4},{7,5},{8,10},{9,11},{10,... | collective-permute-start | bytes 1376264 | tf_op jit(solution)/shard_map/ppermute | solution.py:144
  18.3 9.1 %collective-permute-done.1 = bf16[2,896,128]{2,1,0:T(8,128)(2,1)} collective-permute-done((bf16[2,896,128]{2,1,0:T(8,128)(2,1)S(1)}, bf16[2,896,128]{2,1,0:T(8,128)(2,1)}, u32[]{:S(2)}, u32[]{:S(2)}) %collective-permute-start.1) | collective-permute-done | bytes 458784 | tf_op jit(solution)/shard_map/ppermute | solution.py:144
  27.4 1.6 fusion.8
  29.0 5.1 %collective-permute-done.3 = bf16[2,896,128]{2,1,0:T(8,128)(2,1)} collective-permute-done((bf16[2,896,128]{2,1,0:T(8,128)(2,1)}, bf16[2,896,128]{2,1,0:T(8,128)(2,1)}, u32[]{:S(2)}, u32[]{:S(2)}) %collective-permute-start.3) | collective-permute-done | bytes 458784 | tf_op jit(solution)/shard_map/ppermute | solution.py:144
  34.1 1.9 collective-permute-done.5
  35.9 11.1 %collective-permute-done.4 = bf16[2,896,128]{2,1,0:T(8,128)(2,1)} collective-permute-done((bf16[2,896,128]{2,1,0:T(8,128)(2,1)S(1)}, bf16[2,896,128]{2,1,0:T(8,128)(2,1)}, u32[]{:S(2)}, u32[]{:S(2)}) %collective-permute-start.4) | collective-permute-done | bytes 458784 | tf_op jit(solution)/shard_map/ppermute | solution.py:144
  47.1 1.6 fusion.6
  48.6 0.1 pad_maximum_fusion
  48.7 2.4 copy.48
  51.2 13.3 %all-to-all-start.1 = ((f32[64,4,14,128]{3,1,2,0:T(4,128)}), f32[64,4,14,128]{3,1,2,0:T(4,128)S(1)}, u32[]{:S(2)}, u32[]{:S(2)}) async-start(f32[64,4,14,128]{3,1,2,0:T(4,128)} %bitcast.24), calls=%async_computation.1 | async-start | bytes 3670016 | tf_op jit(solution)/shard_map/all_to_all | solution.py:164
  64.5 0.7 copy.41
  65.2 1.9 copy.42
  67.1 0.7 copy.43
  67.9 1.3 maximum_bitcast_fusion
  69.1 2.5 copy.44
  71.6 37.3 %all-to-all-done.1 = f32[64,4,14,128]{3,1,2,0:T(4,128)S(1)} async-done(((f32[64,4,14,128]{3,1,2,0:T(4,128)}), f32[64,4,14,128]{3,1,2,0:T(4,128)S(1)}, u32[]{:S(2)}, u32[]{:S(2)}) %all-to-all-start.1) | async-done | bytes 1835040 | tf_op jit(solution)/shard_map/all_to_all | solution.py:164
  108.9 1.2 copy-done.3
  110.2 6.8 %all-to-all-start = ((f32[64,3,2,14,128]{4,2,3,1,0:T(2,128)}), f32[64,3,2,14,128]{4,2,3,1,0:T(2,128)S(1)}, u32[]{:S(2)}, u32[]{:S(2)}) async-start(f32[64,3,2,14,128]{4,2,3,1,0:T(2,128)} %copy.44), calls=%async_computation | async-start | bytes 5505024 | tf_op jit(solution)/shard_map/all_to_all | solution.py:127
  117.0 1.9 gather_fusion.1
  118.9 1.9 gather_fusion.3
  120.9 1.9 gather_fusion.2
  122.7 0.2 select_reduce_fusion
  123.0 1.8 copy.49
  124.8 2.0 copy.59
  126.8 2.7 %copy.50 = f32[1792,256]{1,0:T(8,128)} copy(f32[1792,256]{0,1:T(8,128)} %bitcast.72) | data formatting | bytes 3670016 | tf_op jit(solution)/shard_map/dot_general | solution.py:184
  129.5 51.2 %all-to-all-done = f32[64,3,2,14,128]{4,2,3,1,0:T(2,128)S(1)} async-done(((f32[64,3,2,14,128]{4,2,3,1,0:T(2,128)}), f32[64,3,2,14,128]{4,2,3,1,0:T(2,128)S(1)}, u32[]{:S(2)}, u32[]{:S(2)}) %all-to-all-start) | async-done | bytes 2752544 | tf_op jit(solution)/shard_map/all_to_all | solution.py:127
  180.7 1.5 copy.45
  182.3 3.2 %copy.46 = f32[3,128,14,128]{3,2,1,0:T(8,128)} copy(f32[3,128,14,128]{3,1,2,0:T(8,128)S(1)} %bitcast.70) | data formatting | bytes 5505024 | tf_op jit(solution)/shard_map/reshape | solution.py:130
  185.5 2.6 gather_fusion
  188.2 1.0 fusion
  189.2 0.5 copy-done.4
  189.6 2.5 multiply_subtract_fusion
  192.2 1.5 copy.51
  193.7 1.5 copy.52
  195.2 1.5 copy.53
  196.8 69.6 %shard_map.112 = (f32[2,896,128]{2,1,0:T(8,128)}, f32[2,896,128]{2,1,0:T(8,128)}, f32[2,896,128]{2,1,0:T(8,128)}) custom-call(f32[64,2,14,128]{3,2,1,0:T(8,128)} %bitcast.73, f32[64,2,14,128]{3,2,1,0:T(8,128)} %bitcast.74, f32[64,2,14,128]{3,2,1,0:T(8,128)} %bitcast.75), custom_call_target="tpu_custom_call" | custom-call | bytes 5505024 | tf_op jit(solution)/shard_map/pallas_call | solution.py:93
  266.4 2.2 copy.63
  268.6 2.2 copy.64
  270.8 0.9 copy.65
  (28 shorter events, 0.1 us)
Async XLA Ops:
  0.6 118.3 %copy-start = (s32[64]{0:T(128)S(1)}, s32[64]{0:T(128)}, u32[]{:S(2)}) copy-start(s32[64]{0:T(128)} %param.17) | copy-start | bytes 772
  0.6 7.4 %copy-start.5 = (bf16[1,2,3584,128]{3,2,1,0:T(8,128)(2,1)S(1)}, bf16[1,2,3584,128]{3,2,1,0:T(8,128)(2,1)}, u32[]{:S(2)}) copy-start(bf16[1,2,3584,128]{3,2,1,0:T(8,128)(2,1)} %param.13) | copy-start | bytes 5505028
  3.0 11.3 %collective-permute-start = (bf16[2,896,128]{2,1,0:T(8,128)(2,1)S(1)}, bf16[2,896,128]{2,1,0:T(8,128)(2,1)S(1)}, u32[]{:S(2)}, u32[]{:S(2)}) collective-permute-start(bf16[2,896,128]{2,1,0:T(8,128)(2,1)S(1)} %get-tuple-element.6), channel_id=1, source_target_pairs={{0,1},{1,2},{2,3},{3,0},{4,5},{5,6},{6,7},{7,4},{8,9},{9,10},{10,1... | collective-permute-start | bytes 1376264 | tf_op jit(solution)/shard_map/ppermute | solution.py:144
  5.0 13.3 %collective-permute-start.2 = (bf16[2,896,128]{2,1,0:T(8,128)(2,1)}, bf16[2,896,128]{2,1,0:T(8,128)(2,1)}, u32[]{:S(2)}, u32[]{:S(2)}) collective-permute-start(bf16[2,896,128]{2,1,0:T(8,128)(2,1)} %get-tuple-element.7), channel_id=1, source_target_pairs={{0,3},{1,0},{2,1},{3,2},{4,7},{5,4},{6,5},{7,6},{8,11},{9,8},{10,9... | collective-permute-start | bytes 1376264 | tf_op jit(solution)/shard_map/ppermute | solution.py:144
  6.3 21.1 %collective-permute-start.1 = (bf16[2,896,128]{2,1,0:T(8,128)(2,1)S(1)}, bf16[2,896,128]{2,1,0:T(8,128)(2,1)}, u32[]{:S(2)}, u32[]{:S(2)}) collective-permute-start(bf16[2,896,128]{2,1,0:T(8,128)(2,1)S(1)} %get-tuple-element.8), channel_id=1, source_target_pairs={{0,2},{1,3},{2,0},{3,1},{4,6},{5,7},{6,4},{7,5},{8,10},{9,11},{10,... | collective-permute-start | bytes 1376264 | tf_op jit(solution)/shard_map/ppermute | solution.py:144
  9.0 25.0 %collective-permute-start.3 = (bf16[2,896,128]{2,1,0:T(8,128)(2,1)}, bf16[2,896,128]{2,1,0:T(8,128)(2,1)}, u32[]{:S(2)}, u32[]{:S(2)}) collective-permute-start(bf16[2,896,128]{2,1,0:T(8,128)(2,1)} %get-tuple-element.9), channel_id=1, source_target_pairs={{0,1},{1,2},{2,3},{3,0},{4,5},{5,6},{6,7},{7,4},{8,9},{9,10},{10,1... | collective-permute-start | bytes 1376264 | tf_op jit(solution)/shard_map/ppermute | solution.py:144
  9.4 26.6 %collective-permute-start.5 = (bf16[2,896,128]{2,1,0:T(8,128)(2,1)}, bf16[2,896,128]{2,1,0:T(8,128)(2,1)}, u32[]{:S(2)}, u32[]{:S(2)}) collective-permute-start(bf16[2,896,128]{2,1,0:T(8,128)(2,1)} %get-tuple-element.10), channel_id=1, source_target_pairs={{0,3},{1,0},{2,1},{3,2},{4,7},{5,4},{6,5},{7,6},{8,11},{9,8},{10,9... | collective-permute-start | bytes 1376264 | tf_op jit(solution)/shard_map/ppermute | solution.py:144
  14.3 32.7 %collective-permute-start.4 = (bf16[2,896,128]{2,1,0:T(8,128)(2,1)S(1)}, bf16[2,896,128]{2,1,0:T(8,128)(2,1)}, u32[]{:S(2)}, u32[]{:S(2)}) collective-permute-start(bf16[2,896,128]{2,1,0:T(8,128)(2,1)S(1)} %get-tuple-element.11), channel_id=1, source_target_pairs={{0,2},{1,3},{2,0},{3,1},{4,6},{5,7},{6,4},{7,5},{8,10},{9,11},{10,... | collective-permute-start | bytes 1376264 | tf_op jit(solution)/shard_map/ppermute | solution.py:144
  51.2 13.3 %copy-start.6 = (f32[2,896,128]{2,1,0:T(8,128)S(1)}, f32[2,896,128]{2,1,0:T(8,128)}, u32[]{:S(2)}) copy-start(f32[2,896,128]{2,1,0:T(8,128)} %param.9) | copy-start | bytes 2752516
  51.2 57.7 %all-to-all-start.1 = ((f32[64,4,14,128]{3,1,2,0:T(4,128)}), f32[64,4,14,128]{3,1,2,0:T(4,128)S(1)}, u32[]{:S(2)}, u32[]{:S(2)}) async-start(f32[64,4,14,128]{3,1,2,0:T(4,128)} %bitcast.24), calls=%async_computation.1 | async-start | bytes 3670016 | tf_op jit(solution)/shard_map/all_to_all | solution.py:164
  64.5 2.6 copy-start.7
  71.6 45.4 %copy-start.2 = (s32[128]{0:T(128)S(1)}, s32[128]{0:T(128)}, u32[]{:S(2)}) copy-start(s32[128]{0:T(128)} %param.14) | copy-start | bytes 1540
  71.6 49.2 %copy-start.1 = (s32[128]{0:T(128)S(1)}, s32[128]{0:T(128)}, u32[]{:S(2)}) copy-start(s32[128]{0:T(128)} %param.16) | copy-start | bytes 1540
  108.9 1.2 copy-start.3
  110.2 70.6 %all-to-all-start = ((f32[64,3,2,14,128]{4,2,3,1,0:T(2,128)}), f32[64,3,2,14,128]{4,2,3,1,0:T(2,128)S(1)}, u32[]{:S(2)}, u32[]{:S(2)}) async-start(f32[64,3,2,14,128]{4,2,3,1,0:T(2,128)} %copy.44), calls=%async_computation | async-start | bytes 5505024 | tf_op jit(solution)/shard_map/all_to_all | solution.py:127
  117.0 5.8 %copy-start.9 = (s32[128]{0:T(128)S(1)}, s32[128]{0:T(128)}, u32[]{:S(2)}) copy-start(s32[128]{0:T(128)} %param.15) | copy-start | bytes 1540
  188.1 1.5 copy-start.4
  266.3 4.4 %copy-start.8 = (f32[2,896,128]{2,1,0:T(8,128)S(1)}, f32[2,896,128]{2,1,0:T(8,128)}, u32[]{:S(2)}) copy-start(f32[2,896,128]{2,1,0:T(8,128)} %get-tuple-element.19) | copy-start | bytes 2752516

commit v10 on v6

--- a/solution.py
+++ b/solution.py
@@ -10,14 +10,6 @@
 adam_eps = 1e-08
 corr_first = 1.0 - 0.9**10
 corr_second = 1.0 - 0.95**10
-
-
-def adam_update(weight_now, first_now, second_now, gradient):
-    moved_first = beta_first * first_now + (1.0 - beta_first) * gradient
-    moved_second = beta_second * second_now + (1.0 - beta_second) * gradient * gradient
-    step_size = moved_first / corr_first / (jnp.sqrt(moved_second / corr_second) + adam_eps)
-    moved_weight = weight_now - learn_rate * (step_size + decay_rate * weight_now)
-    return (moved_weight, moved_first, moved_second)
 
 
 def per_device_body(
@@ -48,6 +40,7 @@
 
     dp_count = lax.axis_size("dp")
     dp_index = lax.axis_index("dp")
+
     def block_of(array, index):
         return lax.dynamic_slice_in_dim(array, index * shard_rows, shard_rows, axis=1)
 
@@ -103,16 +96,26 @@
         precision=lax.Precision.HIGHEST,
         preferred_element_type=jnp.float32,
     ).reshape(experts, piece_rows, columns)
-    moved = jnp.stack(adam_update(state_new[0], state_new[1], state_new[2], gradient))
-    back = lax.all_to_all(
-        moved.reshape(3, ep_count, exp_dev, piece_rows, columns).transpose(1, 0, 2, 3, 4),
-        "ep",
-        split_axis=0,
-        concat_axis=0,
-        tiled=True,
-    )
-    back = back.transpose(1, 2, 0, 3, 4).reshape(3, exp_dev, shard_rows, columns)
-    return (back[0], back[1], back[2])
+    weight_now, first_now, second_now = state_new
+    moved_first = beta_first * first_now + (1.0 - beta_first) * gradient
+    moved_second = beta_second * second_now + (1.0 - beta_second) * gradient * gradient
+
+    def send_home(parts):
+        count = parts.shape[0]
+        back = lax.all_to_all(
+            parts.reshape(count, ep_count, exp_dev, piece_rows, columns).transpose(1, 0, 2, 3, 4),
+            "ep",
+            split_axis=0,
+            concat_axis=0,
+            tiled=True,
+        )
+        return back.transpose(1, 2, 0, 3, 4).reshape(count, exp_dev, shard_rows, columns)
+
+    moments = send_home(jnp.stack([moved_first, moved_second]))
+    step_size = moved_first / corr_first / (jnp.sqrt(moved_second / corr_second) + adam_eps)
+    moved_weight = weight_now - learn_rate * (step_size + decay_rate * weight_now)
+    weight = send_home(moved_weight[None])
+    return (weight[0], moments[0], moments[1])
 
 
 def solution(mesh):

time: 270 us -> 279 us (1.033)
  blocking collectives: 72 us -> 0 us
  waiting for transfers between devices: 118 us -> 186 us
  starting transfers between devices: 31.8 us -> 44.9 us
    all_to_all x1 -> x0, blocking collectives: 72 us -> none  [per_device_body(): lax.all_to_all(moved.reshape(3, ep_count, exp_dev, piece_rows, columns).t...]
    all_to_all x0 -> x2, waiting for transfers between devices: none -> 66.8 us  [send_home(): lax.all_to_all(parts.reshape(count, ep_count, exp_dev, piece_rows, column...]
    all_to_all x0 -> x2, starting transfers between devices: none -> 13.1 us  [send_home(): lax.all_to_all(parts.reshape(count, ep_count, exp_dev, piece_rows, column...]
    unnamed x25 -> x27, local copies, waits for them, and re-layouts: 10 us -> 9.31 us
  transfers between devices with their start and end apart: 8 -> 10, of which waited for: 7 -> 9; matrix products, arithmetic and copies ran while one was open for 8% -> 9% of each run, Pallas kernels for 0% -> 0%
where the time goes in v10:
time: 279 us
  waiting for transfers between devices  186 us (67%)
  starting transfers between devices  44.9 us (16%)
  local copies, waits for them, and re-layouts  36.4 us (13%)
  other arithmetic  7.96 us (3%)
    all_to_all x2, waiting for transfers between devices, send_home(): lax.all_to_all(parts.reshape(count, ep_count, exp_dev, piece_rows, column...  66.8 us
    all_to_all x1, waiting for transfers between devices, per_device_body(): lax.all_to_all(state.transpose(2, 0, 1, 3, 4), 'ep', split_axis=0, concat...  51.2 us
    all_to_all x1, waiting for transfers between devices, per_device_body(): lax.all_to_all(grads.reshape(exp_dev + rep_dev, ep_count, piece_rows, col...  38 us
    ppermute x6, waiting for transfers between devices, per_device_body(): lax.ppermute(block_of(array, target), 'dp', [(i, (i + shift) % dp_count)...  29.8 us
    all_to_all x1, starting transfers between devices, per_device_body(): lax.all_to_all(grads.reshape(exp_dev + rep_dev, ep_count, piece_rows, col...  13.3 us
    all_to_all x2, starting transfers between devices, send_home(): lax.all_to_all(parts.reshape(count, ep_count, exp_dev, piece_rows, column...  13.1 us
    ppermute x6, starting transfers between devices, per_device_body(): lax.ppermute(block_of(array, target), 'dp', [(i, (i + shift) % dp_count)...  11.7 us
    unnamed x27, local copies, waits for them, and re-layouts  9.31 us
  transfers between devices with their start and end apart: 10, of which 9 were waited for; matrix products, arithmetic and copies ran while one was open for 9% of the time, Pallas kernels for 0%

profile of v10, /device:TPU:1, one launch (start us, length us, event | category | flops | bytes accessed | tf_op | source)
XLA Modules:
  0.0 278.6 jit_solution(5823220334673343269)
XLA Ops:
  0.7 2.3 dynamic-slice_bitcast_fusion.5
  3.0 2.0 collective-permute-start
  5.0 1.3 collective-permute-start.2
  6.3 1.7 collective-permute-start.1
  8.0 1.0 dynamic-slice_bitcast_fusion.2
  9.0 0.3 collective-permute-start.3
  9.4 2.4 collective-permute-start.5
  11.7 2.6 collective-permute-done
  14.3 4.0 %collective-permute-start.4 = (bf16[2,896,128]{2,1,0:T(8,128)(2,1)S(1)}, bf16[2,896,128]{2,1,0:T(8,128)(2,1)}, u32[]{:S(2)}, u32[]{:S(2)}) collective-permute-start(bf16[2,896,128]{2,1,0:T(8,128)(2,1)S(1)} %get-tuple-element.22), channel_id=1, source_target_pairs={{0,2},{1,3},{2,0},{3,1},{4,6},{5,7},{6,4},{7,5},{8,10},{9,11},{10,... | collective-permute-start | bytes 1376264 | tf_op jit(solution)/shard_map/ppermute | solution.py:53
  18.3 9.1 %collective-permute-done.1 = bf16[2,896,128]{2,1,0:T(8,128)(2,1)} collective-permute-done((bf16[2,896,128]{2,1,0:T(8,128)(2,1)S(1)}, bf16[2,896,128]{2,1,0:T(8,128)(2,1)}, u32[]{:S(2)}, u32[]{:S(2)}) %collective-permute-start.1) | collective-permute-done | bytes 458784 | tf_op jit(solution)/shard_map/ppermute | solution.py:53
  27.4 1.6 fusion.8
  29.0 5.1 %collective-permute-done.3 = bf16[2,896,128]{2,1,0:T(8,128)(2,1)} collective-permute-done((bf16[2,896,128]{2,1,0:T(8,128)(2,1)}, bf16[2,896,128]{2,1,0:T(8,128)(2,1)}, u32[]{:S(2)}, u32[]{:S(2)}) %collective-permute-start.3) | collective-permute-done | bytes 458784 | tf_op jit(solution)/shard_map/ppermute | solution.py:53
  34.1 1.9 collective-permute-done.5
  35.9 11.1 %collective-permute-done.4 = bf16[2,896,128]{2,1,0:T(8,128)(2,1)} collective-permute-done((bf16[2,896,128]{2,1,0:T(8,128)(2,1)S(1)}, bf16[2,896,128]{2,1,0:T(8,128)(2,1)}, u32[]{:S(2)}, u32[]{:S(2)}) %collective-permute-start.4) | collective-permute-done | bytes 458784 | tf_op jit(solution)/shard_map/ppermute | solution.py:53
  47.1 1.6 fusion.6
  48.7 2.4 copy.54
  51.2 13.3 %all-to-all-start.1 = ((f32[64,4,14,128]{3,1,2,0:T(4,128)}), f32[64,4,14,128]{3,1,2,0:T(4,128)S(1)}, u32[]{:S(2)}, u32[]{:S(2)}) async-start(f32[64,4,14,128]{3,1,2,0:T(4,128)} %bitcast.24), calls=%async_computation.1 | async-start | bytes 3670016 | tf_op jit(solution)/shard_map/all_to_all | solution.py:73
  64.5 0.7 copy.47
  65.2 0.4 copy-done.7
  65.7 0.7 copy.48
  66.4 0.7 copy.49
  67.1 1.3 maximum_bitcast_fusion
  68.4 2.5 copy.50
  70.9 38.0 %all-to-all-done.1 = f32[64,4,14,128]{3,1,2,0:T(4,128)S(1)} async-done(((f32[64,4,14,128]{3,1,2,0:T(4,128)}), f32[64,4,14,128]{3,1,2,0:T(4,128)S(1)}, u32[]{:S(2)}, u32[]{:S(2)}) %all-to-all-start.1) | async-done | bytes 1835040 | tf_op jit(solution)/shard_map/all_to_all | solution.py:73
  108.9 1.2 copy-done.3
  110.2 6.8 %all-to-all-start = ((f32[64,3,2,14,128]{4,2,3,1,0:T(2,128)}), f32[64,3,2,14,128]{4,2,3,1,0:T(2,128)S(1)}, u32[]{:S(2)}, u32[]{:S(2)}) async-start(f32[64,3,2,14,128]{4,2,3,1,0:T(2,128)} %copy.50), calls=%async_computation | async-start | bytes 5505024 | tf_op jit(solution)/shard_map/all_to_all | solution.py:36
  117.1 1.9 gather_fusion.1
  119.0 1.9 gather_fusion.3
  120.9 1.9 gather_fusion.2
  123.0 1.8 copy.55
  124.8 2.0 copy.70
  126.8 2.7 copy.56
  129.5 51.2 %all-to-all-done = f32[64,3,2,14,128]{4,2,3,1,0:T(2,128)S(1)} async-done(((f32[64,3,2,14,128]{4,2,3,1,0:T(2,128)}), f32[64,3,2,14,128]{4,2,3,1,0:T(2,128)S(1)}, u32[]{:S(2)}, u32[]{:S(2)}) %all-to-all-start) | async-done | bytes 2752544 | tf_op jit(solution)/shard_map/all_to_all | solution.py:36
  180.7 1.5 copy.51
  182.3 3.2 %copy.52 = f32[3,128,14,128]{3,2,1,0:T(8,128)} copy(f32[3,128,14,128]{3,1,2,0:T(8,128)S(1)} %bitcast.78) | data formatting | bytes 5505024 | tf_op jit(solution)/shard_map/reshape | solution.py:39
  185.5 2.6 gather_fusion
  188.1 1.0 fusion
  189.2 0.5 copy-done.4
  189.6 2.5 multiply_subtract_fusion
  192.2 1.2 copy.57
  193.4 7.0 %all-to-all-start.2 = ((f32[64,1,2,14,128]{4,2,3,1,0:T(2,128)}), f32[64,1,2,14,128]{4,2,3,1,0:T(2,128)S(1)}, u32[]{:S(2)}, u32[]{:S(2)}) async-start(f32[64,1,2,14,128]{4,2,3,1,0:T(2,128)} %copy.57), calls=%async_computation.2 | async-start | bytes 1835008 | tf_op jit(solution)/shard_map/all_to_all | solution.py:105
  200.4 2.2 copy_bitcast_fusion
  202.6 23.4 %all-to-all-done.2 = f32[64,1,2,14,128]{4,2,3,1,0:T(2,128)S(1)} async-done(((f32[64,1,2,14,128]{4,2,3,1,0:T(2,128)}), f32[64,1,2,14,128]{4,2,3,1,0:T(2,128)S(1)}, u32[]{:S(2)}, u32[]{:S(2)}) %all-to-all-start.2) | async-done | bytes 917536 | tf_op jit(solution)/shard_map/all_to_all | solution.py:105
  226.0 6.1 %all-to-all-start.3 = ((f32[64,2,2,14,128]{4,2,3,1,0:T(2,128)}), f32[64,2,2,14,128]{4,2,3,1,0:T(2,128)S(1)}, u32[]{:S(2)}, u32[]{:S(2)}) async-start(f32[64,2,2,14,128]{4,2,3,1,0:T(2,128)} %copy_bitcast_fusion), calls=%async_computation.3 | async-start | bytes 3670016 | tf_op jit(solution)/shard_map/all_to_all | solution.py:105
  232.1 1.0 copy.60
  233.1 43.4 %all-to-all-done.3 = f32[64,2,2,14,128]{4,2,3,1,0:T(2,128)S(1)} async-done(((f32[64,2,2,14,128]{4,2,3,1,0:T(2,128)}), f32[64,2,2,14,128]{4,2,3,1,0:T(2,128)S(1)}, u32[]{:S(2)}, u32[]{:S(2)}) %all-to-all-start.3) | async-done | bytes 1835040 | tf_op jit(solution)/shard_map/all_to_all | solution.py:105
  276.6 1.0 copy.62
  277.6 1.0 copy.61
  (31 shorter events, 0.6 us)
Async XLA Ops:
  0.6 118.3 %copy-start = (s32[64]{0:T(128)S(1)}, s32[64]{0:T(128)}, u32[]{:S(2)}) copy-start(s32[64]{0:T(128)} %param.17) | copy-start | bytes 772
  0.6 7.4 %copy-start.5 = (bf16[1,2,3584,128]{3,2,1,0:T(8,128)(2,1)S(1)}, bf16[1,2,3584,128]{3,2,1,0:T(8,128)(2,1)}, u32[]{:S(2)}) copy-start(bf16[1,2,3584,128]{3,2,1,0:T(8,128)(2,1)} %param.13) | copy-start | bytes 5505028
  3.0 11.3 %collective-permute-start = (bf16[2,896,128]{2,1,0:T(8,128)(2,1)S(1)}, bf16[2,896,128]{2,1,0:T(8,128)(2,1)S(1)}, u32[]{:S(2)}, u32[]{:S(2)}) collective-permute-start(bf16[2,896,128]{2,1,0:T(8,128)(2,1)S(1)} %get-tuple-element.17), channel_id=1, source_target_pairs={{0,1},{1,2},{2,3},{3,0},{4,5},{5,6},{6,7},{7,4},{8,9},{9,10},{10,1... | collective-permute-start | bytes 1376264 | tf_op jit(solution)/shard_map/ppermute | solution.py:53
  5.0 13.3 %collective-permute-start.2 = (bf16[2,896,128]{2,1,0:T(8,128)(2,1)}, bf16[2,896,128]{2,1,0:T(8,128)(2,1)}, u32[]{:S(2)}, u32[]{:S(2)}) collective-permute-start(bf16[2,896,128]{2,1,0:T(8,128)(2,1)} %get-tuple-element.18), channel_id=1, source_target_pairs={{0,3},{1,0},{2,1},{3,2},{4,7},{5,4},{6,5},{7,6},{8,11},{9,8},{10,9... | collective-permute-start | bytes 1376264 | tf_op jit(solution)/shard_map/ppermute | solution.py:53
  6.3 21.1 %collective-permute-start.1 = (bf16[2,896,128]{2,1,0:T(8,128)(2,1)S(1)}, bf16[2,896,128]{2,1,0:T(8,128)(2,1)}, u32[]{:S(2)}, u32[]{:S(2)}) collective-permute-start(bf16[2,896,128]{2,1,0:T(8,128)(2,1)S(1)} %get-tuple-element.19), channel_id=1, source_target_pairs={{0,2},{1,3},{2,0},{3,1},{4,6},{5,7},{6,4},{7,5},{8,10},{9,11},{10,... | collective-permute-start | bytes 1376264 | tf_op jit(solution)/shard_map/ppermute | solution.py:53
  9.0 25.0 %collective-permute-start.3 = (bf16[2,896,128]{2,1,0:T(8,128)(2,1)}, bf16[2,896,128]{2,1,0:T(8,128)(2,1)}, u32[]{:S(2)}, u32[]{:S(2)}) collective-permute-start(bf16[2,896,128]{2,1,0:T(8,128)(2,1)} %get-tuple-element.20), channel_id=1, source_target_pairs={{0,1},{1,2},{2,3},{3,0},{4,5},{5,6},{6,7},{7,4},{8,9},{9,10},{10,1... | collective-permute-start | bytes 1376264 | tf_op jit(solution)/shard_map/ppermute | solution.py:53
  9.4 26.6 %collective-permute-start.5 = (bf16[2,896,128]{2,1,0:T(8,128)(2,1)}, bf16[2,896,128]{2,1,0:T(8,128)(2,1)}, u32[]{:S(2)}, u32[]{:S(2)}) collective-permute-start(bf16[2,896,128]{2,1,0:T(8,128)(2,1)} %get-tuple-element.21), channel_id=1, source_target_pairs={{0,3},{1,0},{2,1},{3,2},{4,7},{5,4},{6,5},{7,6},{8,11},{9,8},{10,9... | collective-permute-start | bytes 1376264 | tf_op jit(solution)/shard_map/ppermute | solution.py:53
  14.3 32.7 %collective-permute-start.4 = (bf16[2,896,128]{2,1,0:T(8,128)(2,1)S(1)}, bf16[2,896,128]{2,1,0:T(8,128)(2,1)}, u32[]{:S(2)}, u32[]{:S(2)}) collective-permute-start(bf16[2,896,128]{2,1,0:T(8,128)(2,1)S(1)} %get-tuple-element.22), channel_id=1, source_target_pairs={{0,2},{1,3},{2,0},{3,1},{4,6},{5,7},{6,4},{7,5},{8,10},{9,11},{10,... | collective-permute-start | bytes 1376264 | tf_op jit(solution)/shard_map/ppermute | solution.py:53
  51.2 13.3 %copy-start.6 = (f32[2,896,128]{2,1,0:T(8,128)S(1)}, f32[2,896,128]{2,1,0:T(8,128)}, u32[]{:S(2)}) copy-start(f32[2,896,128]{2,1,0:T(8,128)} %param.9) | copy-start | bytes 2752516
  51.2 57.7 %all-to-all-start.1 = ((f32[64,4,14,128]{3,1,2,0:T(4,128)}), f32[64,4,14,128]{3,1,2,0:T(4,128)S(1)}, u32[]{:S(2)}, u32[]{:S(2)}) async-start(f32[64,4,14,128]{3,1,2,0:T(4,128)} %bitcast.24), calls=%async_computation.1 | async-start | bytes 3670016 | tf_op jit(solution)/shard_map/all_to_all | solution.py:73
  64.5 1.2 copy-start.7
  64.5 1.9 copy-start.8
  70.9 46.2 %copy-start.2 = (s32[128]{0:T(128)S(1)}, s32[128]{0:T(128)}, u32[]{:S(2)}) copy-start(s32[128]{0:T(128)} %param.14) | copy-start | bytes 1540
  108.9 1.2 copy-start.3
  110.2 70.6 %all-to-all-start = ((f32[64,3,2,14,128]{4,2,3,1,0:T(2,128)}), f32[64,3,2,14,128]{4,2,3,1,0:T(2,128)S(1)}, u32[]{:S(2)}, u32[]{:S(2)}) async-start(f32[64,3,2,14,128]{4,2,3,1,0:T(2,128)} %copy.50), calls=%async_computation | async-start | bytes 5505024 | tf_op jit(solution)/shard_map/all_to_all | solution.py:36
  117.0 3.9 %copy-start.1 = (s32[128]{0:T(128)S(1)}, s32[128]{0:T(128)}, u32[]{:S(2)}) copy-start(s32[128]{0:T(128)} %param.16) | copy-start | bytes 1540
  117.0 5.8 %copy-start.9 = (s32[128]{0:T(128)S(1)}, s32[128]{0:T(128)}, u32[]{:S(2)}) copy-start(s32[128]{0:T(128)} %param.15) | copy-start | bytes 1540
  188.1 1.5 copy-start.4
  193.4 32.6 %all-to-all-start.2 = ((f32[64,1,2,14,128]{4,2,3,1,0:T(2,128)}), f32[64,1,2,14,128]{4,2,3,1,0:T(2,128)S(1)}, u32[]{:S(2)}, u32[]{:S(2)}) async-start(f32[64,1,2,14,128]{4,2,3,1,0:T(2,128)} %copy.57), calls=%async_computation.2 | async-start | bytes 1835008 | tf_op jit(solution)/shard_map/all_to_all | solution.py:105
  226.0 50.5 %all-to-all-start.3 = ((f32[64,2,2,14,128]{4,2,3,1,0:T(2,128)}), f32[64,2,2,14,128]{4,2,3,1,0:T(2,128)S(1)}, u32[]{:S(2)}, u32[]{:S(2)}) async-start(f32[64,2,2,14,128]{4,2,3,1,0:T(2,128)} %copy_bitcast_fusion), calls=%async_computation.3 | async-start | bytes 3670016 | tf_op jit(solution)/shard_map/all_to_all | solution.py:105
